TPU v7x, 256 devices: a whole 4x4x8 slice. The times are simulated.
256 devices in a mesh: band: 32 (over y, z), chan: 8 (over x, core).
Axes of the slice: x: 4, y: 4, z: 8, core: 2. Of those that a mesh axis runs over, the one named last changes fastest.
Arguments:
- new_frames: bfloat16 [4, 128, 512, 320], P(None, 'band', 'chan'), may hold values from -6 to 6
- cached_frames: bfloat16 [2, 128, 512, 320], P(None, 'band', 'chan'), may hold values from -6 to 6
- conv_weight: bfloat16 [3, 3, 3, 512, 512], P(None, None, None, 'chan'), may hold values from -0.0546875 to 0.0546875
- out_bias: float32 [512], P('chan'), may hold values from -3 to 3
Outputs:
- conv_out: bfloat16 [4, 128, 512, 320], P(None, 'band', 'chan')
All inputs are finite; a program needn't handle non-finite values.
Results may differ from a plain program's by a relative error of at most 0.001.
Values may be sent and summed in bfloat16 or wider, within the bound.
No kernel may reach another device: no remote copies, remote signals or barrier semaphores. Data moves between devices by JAX's collectives and lax.ppermute only.
A program may use at most 128 MiB of HBM per device.

v0:
```python
import functools

import jax
import jax.numpy as jnp
from jax import lax
from jax.experimental import pallas as pl
from jax.experimental.pallas import tpu as pltpu
from jax.sharding import PartitionSpec as P


BF = jnp.bfloat16
F32 = jnp.float32
LANES = 128
HALF = 64


def turn(pairs):
    width = pairs.shape[-1]
    return pltpu.roll(pairs.astype(F32), width // 2, axis=1)


def pack_kernel(flip_ref, cached_ref, new_ref, kept_ref, sent_ref):
    cols = cached_ref.shape[-1]
    upper = flip_ref[0]
    place = [
        (lax.broadcasted_iota(jnp.int32, (cols, 2 * cols), 0) + h * cols
         == lax.broadcasted_iota(jnp.int32, (cols, 2 * cols), 1)).astype(F32).astype(BF)
        for h in range(2)
    ]
    for out, flip in ((kept_ref, upper), (sent_ref, 1 - upper)):
        for row in range(2):
            at = jnp.where(flip == 0, row, 3 - row)
            for pair in range(3):
                first = cached_ref[0, at] if pair == 0 else new_ref[2 * pair - 2, at]
                second = cached_ref[1, at] if pair == 0 else new_ref[2 * pair - 1, at]
                both = jnp.dot(first, place[0], preferred_element_type=F32)
                both = both + jnp.dot(second, place[1], preferred_element_type=F32)
                out[row, pair] = both.astype(BF)


def pack(flip, cached, new):
    channels, cols = cached.shape[2:]
    shape = jax.ShapeDtypeStruct((2, 3, channels, 2 * cols), BF)
    return pl.pallas_call(
        pack_kernel,
        in_specs=[pl.BlockSpec(memory_space=pltpu.SMEM)] + [pl.BlockSpec(memory_space=pltpu.VMEM)] * 2,
        out_specs=[pl.BlockSpec(memory_space=pltpu.VMEM)] * 2,
        out_shape=[shape, shape],
        compiler_params=pltpu.CompilerParams(vmem_limit_bytes=16 * 2**20),
        cost_estimate=pl.CostEstimate(flops=10**8, bytes_accessed=4 * 2**20, transcendentals=0),
        name="pack",
    )(flip, cached, new)


def block_kernel(mixed, first, last, *refs):
    scalars, refs = refs[0], list(refs[1:])
    bodies = [refs.pop(0), refs.pop(0)]
    zsides = [refs.pop(0), refs.pop(0)]
    csides = [refs.pop(0), refs.pop(0)]
    weights = [(refs.pop(0), refs.pop(0)) for _ in range(2 if mixed else 1)]
    before = None if first else refs.pop(0)
    bias = refs.pop(0) if last else None
    outs = [refs.pop(0), refs.pop(0)] if last else [refs.pop(0)]
    (xs,) = refs
    p = pl.program_id(0)
    flip, edge = scalars[0], scalars[3] == 1
    width = xs.shape[-1]
    cols = width // 2
    near = lax.broadcasted_iota(jnp.int32, (HALF, width), 1) < cols
    for piece in range(2):
        at = pl.ds(piece * HALF, HALF)
        rows = [
            lambda q: jnp.where(edge, jnp.zeros((HALF, width), BF), zsides[piece][q]),
            lambda q: bodies[piece][0, q],
            lambda q: bodies[piece][1, q],
            lambda q: csides[piece][q],
        ]
        for row in range(4):
            low, high = rows[row](p), rows[row](p + 1)
            xs[0, row, at] = low
            xs[2, row, at] = high
            xs[1, row, at] = jnp.where(near, turn(low), turn(high)).astype(BF)

    channel = lax.broadcasted_iota(jnp.int32, (1, LANES), 1)
    from_first = channel < HALF
    taps = []
    for t in range(3):
        for delta in range(3):
            row_tap = jnp.where(flip == 0, delta, 2 - delta)
            halves = []
            for half in range(2):
                w = weights[0][half][t, row_tap]
                w = w.reshape(w.shape[0] * w.shape[1], LANES)
                if mixed:
                    v = weights[1][half][t, row_tap].reshape(w.shape)
                    w = jnp.where(jnp.broadcast_to(from_first, w.shape), w, v)
                halves.append(w)
            taps.append(jnp.concatenate(halves, axis=0))
    lhs = jnp.concatenate(taps, axis=1)
    rows = lhs.shape[0] // 6
    lane = lax.broadcasted_iota(jnp.int32, (rows, width), 1)
    zero = jnp.zeros((rows, width), F32)
    left_edge = (lane == 0) | (lane == cols)
    right_edge = (lane == cols - 1) | (lane == width - 1)
    for row in range(2):
        window = jnp.concatenate(
            [xs[t, row : row + 3].reshape(3 * LANES, width) for t in range(3)], axis=0
        )
        acc = jnp.dot(lhs, window, preferred_element_type=F32)
        if not first:
            acc = acc + before[0, row]
        if not last:
            outs[0][0, row] = acc
            continue
        for half in range(2):
            part = acc[half * 3 * rows : (half + 1) * 3 * rows]
            from_left = jnp.where(left_edge, zero, pltpu.roll(part[:rows], 1, axis=1))
            from_right = jnp.where(right_edge, zero, pltpu.roll(part[2 * rows :], width - 1, axis=1))
            total = part[rows : 2 * rows] + from_left + from_right + bias[half][:, None]
            outs[half][0, row] = total.astype(BF)


def block_call(scalars, bodies, zsides, csides, weights, mixed, before, bias):
    first, last = before is None, bias is not None
    own, other = weights
    taps, outs64 = own.shape[:3], own.shape[3]
    rows = 2 * 3 * outs64
    width = bodies[0].shape[-1]
    operands = [*bodies, *zsides, *csides]
    specs = [pl.BlockSpec(a.shape, lambda p, s, n=a.ndim: (0,) * n) for a in operands]
    for slot in range(2 if mixed else 1):
        for array in (own, other):
            operands.append(array)
            specs.append(pl.BlockSpec((*taps, outs64, LANES), lambda p, s, slot=slot: (0, 0, 0, 0, s[1 + slot])))
    if not first:
        operands.append(before)
        specs.append(pl.BlockSpec((1, 2, rows, width), lambda p, s: (p, 0, 0, 0)))
    if last:
        operands.append(bias)
        specs.append(pl.BlockSpec(bias.shape, lambda p, s: (0, 0)))
        out_shape = [jax.ShapeDtypeStruct((2, 2, outs64, width), BF)] * 2
        out_specs = [pl.BlockSpec((1, 2, outs64, width), lambda p, s: (p, 0, 0, 0))] * 2
    else:
        out_shape = jax.ShapeDtypeStruct((2, 2, rows, width), F32)
        out_specs = pl.BlockSpec((1, 2, rows, width), lambda p, s: (p, 0, 0, 0))
    return pl.pallas_call(
        functools.partial(block_kernel, mixed, first, last),
        grid_spec=pltpu.PrefetchScalarGridSpec(
            num_scalar_prefetch=1,
            grid=(2,),
            in_specs=specs,
            out_specs=out_specs,
            scratch_shapes=[pltpu.VMEM((3, 4, LANES, width), BF)],
        ),
        out_shape=out_shape,
        compiler_params=pltpu.CompilerParams(vmem_limit_bytes=32 * 2**20),
        cost_estimate=pl.CostEstimate(
            flops=2 * 4 * rows * 9 * LANES * width, bytes_accessed=8 * 2**20, transcendentals=0
        ),
    )(scalars, *operands)


def solution(mesh):
    bands, chans = mesh.shape["band"], mesh.shape["chan"]
    chips = chans // 2
    swap = [(2 * x + c, 2 * x + 1 - c) for x in range(chips) for c in range(2)]
    right = [(2 * x + c, 2 * ((x + 1) % chips) + c) for x in range(chips) for c in range(2)]
    left = [(target, source) for source, target in right]
    across = []
    for b in range(1, bands):
        for x in range(chips):
            here, there = b * chans + 2 * x + b % 2, (b - 1) * chans + 2 * x + b % 2
            across += [(here, there), (there, here)]
    for x in range(chips):
        here, there = 2 * x, (bands - 1) * chans + 2 * x + bands % 2
        across += [(here, there), (there, here)]

    def on_device(new_frames, cached_frames, conv_weight, out_bias):
        cols = new_frames.shape[-1]
        index = lax.axis_index("chan")
        core, chip = index % 2, index // 2
        even = core == 0
        flip = (core + lax.axis_index("band")) % 2
        upper = flip == 0
        band = lax.axis_index("band")
        edge = jnp.where(upper, band == 0, band == bands - 1)

        def send(a, pairs, axes="chan"):
            return lax.ppermute(a, axes, pairs)

        def halos(a, b):
            c = send(jnp.stack([a[1], b[1]]), swap)
            z = send(jnp.stack([a[0], b[0]]), across, ("band", "chan"))
            return (z[0], z[1]), (c[0], c[1])

        kept, sent = pack(flip.astype(jnp.int32).reshape(1), cached_frames, new_frames)
        got = send(sent, swap)
        got, conv_weight, out_bias = lax.optimization_barrier((got, conv_weight, out_bias))
        other_weight = send(conv_weight, swap)
        biases = jnp.stack([out_bias, send(out_bias, swap)])
        lo, hi = jnp.where(even, kept, got), jnp.where(even, got, kept)
        l_lo = send(lo, right)
        r_hi = send(hi, left)
        l_hi = send(hi, right)
        r_lo = send(lo, left)
        weights = (conv_weight, other_weight)

        def scalars(*offsets):
            first, second = (offsets * 2)[:2]
            return jnp.stack([flip, (chip + first) % chips, (chip + second) % chips, edge]).astype(jnp.int32)

        acc = block_call(scalars(0), (lo, hi), *halos(lo, hi), weights, False, None, None)
        l_lo, r_hi, acc = lax.optimization_barrier((l_lo, r_hi, acc))
        f_lo = send(l_lo, right)
        f_hi = send(r_hi, left)
        r_lo, l_hi, acc = lax.optimization_barrier((r_lo, l_hi, acc))
        acc = block_call(scalars(chips - 1, 1), (l_lo, r_hi), *halos(l_lo, r_hi), weights, True, acc, None)
        f_lo, f_hi, acc = lax.optimization_barrier((f_lo, f_hi, acc))
        acc = block_call(scalars(1, chips - 1), (r_lo, l_hi), *halos(r_lo, l_hi), weights, True, acc, None)
        mine, theirs = block_call(scalars(2), (f_lo, f_hi), *halos(f_lo, f_hi), weights, False, acc, biases)
        given = send(theirs, swap)

        def row(a, r):
            a = a[:, r]
            return jnp.stack([a[..., :cols], a[..., cols:]], axis=1).reshape(4, a.shape[1], cols)

        m, g = [row(mine, 0), row(mine, 1)], [row(given, 0), row(given, 1)]
        return jnp.stack([jnp.where(upper, a, b) for a, b in zip(m + g[::-1], g + m[::-1])], axis=1)

    in_specs = (
        P(None, "band", "chan", None),
        P(None, "band", "chan", None),
        P(None, None, None, "chan", None),
        P("chan"),
    )

    return jax.shard_map(
        on_device, mesh=mesh, in_specs=in_specs, out_specs=P(None, "band", "chan", None), check_vma=False
    )
```

profile of v0, /device:TPU:1, one launch (start us, length us, event | category | flops | bytes accessed | tf_op | source)
XLA Modules:
  0.0 88.4 jit_solution(13606126125023039641)
XLA Ops:
  0.0 1.1 %copy-done.5 = bf16[4,4,64,320]{3,2,1,0:T(8,128)(2,1)S(1)} copy-done((bf16[4,4,64,320]{3,2,1,0:T(8,128)(2,1)S(1)}, bf16[4,4,64,320]{3,2,1,0:T(8,128)(2,1)}, u32[]{:S(2)}) %copy-start.5) | copy-done | bytes 655384
  1.2 1.0 %copy-done.7 = bf16[2,4,64,320]{3,2,1,0:T(8,128)(2,1)S(1)} copy-done((bf16[2,4,64,320]{3,2,1,0:T(8,128)(2,1)S(1)}, bf16[2,4,64,320]{3,2,1,0:T(8,128)(2,1)}, u32[]{:S(2)}) %copy-start.7) | copy-done | bytes 327704
  2.1 1.4 %pack.1 = (bf16[2,3,64,640]{3,2,1,0:T(8,128)(2,1)S(1)}, bf16[2,3,64,640]{3,2,1,0:T(8,128)(2,1)S(1)}) custom-call(s32[1]{0:T(128)} %bitcast.flip_ref, bf16[2,4,64,320]{3,2,1,0:T(8,128)(2,1)S(1)} %copy-done.7, bf16[4,4,64,320]{3,2,1,0:T(8,128)(2,1)S(1)} %copy-done.5), custom_call_target="tpu_custom_call" | custom-call | flops 100000000 | bytes 4194304 | tf_op jit(solution)/shard_map/pack/pallas_call | solution.py:44
  3.5 0.0 copy-start.6
  3.6 0.8 copy-done.6
  4.3 3.2 %collective-permute-start = (bf16[2,3,64,640]{3,2,1,0:T(8,128)(2,1)S(1)}, bf16[2,3,64,640]{3,2,1,0:T(8,128)(2,1)}, u32[]{:S(2)}, u32[]{:S(2)}) collective-permute-start(bf16[2,3,64,640]{3,2,1,0:T(8,128)(2,1)S(1)} %get-tuple-element.22), channel_id=1, source_target_pairs={{0,1},{1,0},{2,3},{3,2},{4,5},{5,4},{6,7},{7,6},{8,9},{9,8},{10,11... | collective-permute-start | bytes 1474568 | tf_op jit(solution)/shard_map/ppermute | solution.py:189
  7.5 1.6 %collective-permute-done = bf16[2,3,64,640]{3,2,1,0:T(8,128)(2,1)} collective-permute-done((bf16[2,3,64,640]{3,2,1,0:T(8,128)(2,1)S(1)}, bf16[2,3,64,640]{3,2,1,0:T(8,128)(2,1)}, u32[]{:S(2)}, u32[]{:S(2)}) %collective-permute-start) | collective-permute-done | bytes 491552 | tf_op jit(solution)/shard_map/ppermute | solution.py:189
  9.2 0.4 collective-permute-start.5
  9.5 0.1 add_add_fusion.2.refs_0_
  9.6 1.4 %broadcast_select_fusion = (bf16[2,3,64,640]{3,2,1,0:T(8,128)(2,1)S(1)}, bf16[2,3,64,640]{3,2,1,0:T(8,128)(2,1)S(1)}) fusion(bf16[2,3,64,640]{3,2,1,0:T(8,128)(2,1)} %collective-permute-done, bf16[2,3,64,640]{3,2,1,0:T(8,128)(2,1)} %copy-done.6, pred[]{:T(512)S(6)} %eq.26), kind=kLoop, calls=%fused_computation.9 | loop fusion | flops 491520 | bytes 1966081 | tf_op jit(solution)/shard_map/jit(_where)/select_n | solution.py:201
  11.0 0.0 copy-start.1
  11.0 0.8 copy-done.1
  11.8 0.9 fusion.6
  12.7 0.9 pad_maximum_fusion.1
  13.6 0.1 add_add_fusion.3.refs_0_
  13.6 1.9 %pad_maximum_fusion.2 = bf16[2,3,64,640]{3,2,1,0:T(8,128)(2,1)} fusion(bf16[1,3,64,640]{3,2,1,0:T(8,128)(2,1)} %get-tuple-element.88, bf16[1,3,64,640]{3,2,1,0:T(8,128)(2,1)} %get-tuple-element.65), kind=kLoop, calls=%fused_computation.2 | loop fusion | flops 245760 | bytes 983040 | tf_op jit(solution)/shard_map/stack | solution.py:192
  15.5 6.7 %collective-permute-start.4 = (bf16[2,3,64,640]{3,2,1,0:T(8,128)(2,1)}, bf16[2,3,64,640]{3,2,1,0:T(8,128)(2,1)}, u32[]{:S(2)}, u32[]{:S(2)}) collective-permute-start(bf16[2,3,64,640]{3,2,1,0:T(8,128)(2,1)} %pad_maximum_fusion.2), channel_id=1, source_target_pairs={{0,1},{1,0},{2,3},{3,2},{4,5},{5,4},{6,7},{7,6},{8,9},{9,8},{10,11... | collective-permute-start | bytes 1474568 | tf_op jit(solution)/shard_map/ppermute | solution.py:189
  22.3 0.1 add_add_fusion.1.refs_0_
  22.4 0.1 collective-permute-start.16
  22.4 0.1 add_add_fusion.refs_0_
  22.5 1.2 %collective-permute-start.11 = (bf16[2,3,64,640]{3,2,1,0:T(8,128)(2,1)}, bf16[2,3,64,640]{3,2,1,0:T(8,128)(2,1)S(1)}, u32[]{:S(2)}, u32[]{:S(2)}) collective-permute-start(bf16[2,3,64,640]{3,2,1,0:T(8,128)(2,1)} %copy-done.3), channel_id=1, source_target_pairs={{0,2},{1,3},{2,4},{3,5},{4,6},{5,7},{6,0},{7,1},{8,10},{9,11},{10,... | collective-permute-start | bytes 1474568 | tf_op jit(solution)/shard_map/ppermute | solution.py:189
  23.7 0.4 collective-permute-done.16
  24.1 2.5 %collective-permute-start.2 = (bf16[2,3,64,640]{3,2,1,0:T(8,128)(2,1)}, bf16[2,3,64,640]{3,2,1,0:T(8,128)(2,1)S(1)}, u32[]{:S(2)}, u32[]{:S(2)}) collective-permute-start(bf16[2,3,64,640]{3,2,1,0:T(8,128)(2,1)} %copy-done.3), channel_id=1, source_target_pairs={{2,0},{3,1},{4,2},{5,3},{6,4},{7,5},{0,6},{1,7},{10,8},{11,9},{12,... | collective-permute-start | bytes 1474568 | tf_op jit(solution)/shard_map/ppermute | solution.py:189
  26.6 0.1 collective-permute-start.1
  26.7 1.1 %slice_bitcast_fusion.14 = (bf16[3,64,640]{2,1,0:T(8,128)(2,1)S(1)}, bf16[3,64,640]{2,1,0:T(8,128)(2,1)S(1)}) fusion(bf16[2,3,64,640]{3,2,1,0:T(8,128)(2,1)} %collective-permute-done.3), kind=kLoop, calls=%fused_computation.25 | loop fusion | bytes 983040 | tf_op jit(solution)/shard_map/squeeze | solution.py:194
  27.8 2.7 %collective-permute-start.10 = (bf16[2,3,64,640]{3,2,1,0:T(8,128)(2,1)}, bf16[2,3,64,640]{3,2,1,0:T(8,128)(2,1)S(1)}, u32[]{:S(2)}, u32[]{:S(2)}) collective-permute-start(bf16[2,3,64,640]{3,2,1,0:T(8,128)(2,1)} %copy-done.1), channel_id=1, source_target_pairs={{2,0},{3,1},{4,2},{5,3},{6,4},{7,5},{0,6},{1,7},{10,8},{11,9},{12,... | collective-permute-start | bytes 1474568 | tf_op jit(solution)/shard_map/ppermute | solution.py:189
  30.6 1.1 %slice_bitcast_fusion.12 = (bf16[3,64,640]{2,1,0:T(8,128)(2,1)S(1)}, bf16[3,64,640]{2,1,0:T(8,128)(2,1)S(1)}) fusion(bf16[2,3,64,640]{3,2,1,0:T(8,128)(2,1)} %collective-permute-done.4), kind=kLoop, calls=%fused_computation.23 | loop fusion | bytes 983040 | tf_op jit(solution)/shard_map/squeeze | solution.py:194
  31.7 0.0 collective-permute-done.5.refs_8_.refs_10_
  31.7 0.0 copy-start.2
  31.7 1.0 %copy-done.2 = bf16[2,3,64,640]{3,2,1,0:T(8,128)(2,1)S(1)} copy-done((bf16[2,3,64,640]{3,2,1,0:T(8,128)(2,1)S(1)}, bf16[2,3,64,640]{3,2,1,0:T(8,128)(2,1)}, u32[]{:S(2)}) %copy-start.2) | copy-done | bytes 491544
  32.7 1.0 %copy-done.4 = bf16[2,3,64,640]{3,2,1,0:T(8,128)(2,1)S(1)} copy-done((bf16[2,3,64,640]{3,2,1,0:T(8,128)(2,1)S(1)}, bf16[2,3,64,640]{3,2,1,0:T(8,128)(2,1)}, u32[]{:S(2)}) %copy-start.4) | copy-done | bytes 491544
  33.7 4.2 %shard_map.46.refs_11_ = f32[2,2,384,640]{3,2,1,0:T(8,128)S(1)} custom-call(s32[4]{0:T(128)S(1)} %add_add_fusion.1.refs_0_, bf16[2,3,64,640]{3,2,1,0:T(8,128)(2,1)S(1)} %copy-done.2, bf16[2,3,64,640]{3,2,1,0:T(8,128)(2,1)S(1)} %copy-done.4, bf16[3,64,640]{2,1,0:T(8,128)(2,1)S(1)} %get-tuple-element.70.refs_3_, ...), custom_call_target="tpu_custom_call" | custom-call | flops 2264924160 | bytes 8388608 | tf_op jit(solution)/shard_map/pallas_call | solution.py:146
  38.0 8.8 %collective-permute-done.1.refs_1_ = bf16[2,3,64,640]{3,2,1,0:T(8,128)(2,1)S(1)} collective-permute-done((bf16[2,3,64,640]{3,2,1,0:T(8,128)(2,1)}, bf16[2,3,64,640]{3,2,1,0:T(8,128)(2,1)S(1)}, u32[]{:S(2)}, u32[]{:S(2)}) %collective-permute-start.1) | collective-permute-done | bytes 491552 | tf_op jit(solution)/shard_map/ppermute | solution.py:189
  46.8 0.0 collective-permute-start.6
  46.8 2.7 %collective-permute-start.7 = (bf16[2,3,64,640]{3,2,1,0:T(8,128)(2,1)S(1)}, bf16[2,3,64,640]{3,2,1,0:T(8,128)(2,1)S(1)}, u32[]{:S(2)}, u32[]{:S(2)}) collective-permute-start(bf16[2,3,64,640]{3,2,1,0:T(8,128)(2,1)S(1)} %collective-permute-done.2.refs_2_), channel_id=1, source_target_pairs={{2,0},{3,1},{4,2},{5,3},{6,4},{7,5},{0,6},{1,7},{10,8},{11,9},{12,... | collective-permute-start | bytes 1474568 | tf_op jit(solution)/shard_map/ppermute | solution.py:189
  49.5 0.0 collective-permute-done.10.refs_1_
  49.6 0.1 pad_maximum_fusion.3
  49.7 0.1 collective-permute-start.8
  49.8 0.1 pad_maximum_fusion.4
  49.8 3.2 %collective-permute-start.9 = (bf16[2,3,64,640]{3,2,1,0:T(8,128)(2,1)S(1)}, bf16[2,3,64,640]{3,2,1,0:T(8,128)(2,1)S(1)}, u32[]{:S(2)}, u32[]{:S(2)}) collective-permute-start(bf16[2,3,64,640]{3,2,1,0:T(8,128)(2,1)S(1)} %pad_maximum_fusion.4), channel_id=1, source_target_pairs={{0,1},{1,0},{2,3},{3,2},{4,5},{5,4},{6,7},{7,6},{8,9},{9,8},{10,11... | collective-permute-start | bytes 1474568 | tf_op jit(solution)/shard_map/ppermute | solution.py:189
  53.1 0.1 pad_maximum_fusion.7
  53.2 0.1 collective-permute-start.14
  53.3 0.1 pad_maximum_fusion.8
  53.4 4.4 %collective-permute-done.8 = bf16[2,3,64,640]{3,2,1,0:T(8,128)(2,1)S(1)} collective-permute-done((bf16[2,3,64,640]{3,2,1,0:T(8,128)(2,1)S(1)}, bf16[2,3,64,640]{3,2,1,0:T(8,128)(2,1)S(1)}, u32[]{:S(2)}, u32[]{:S(2)}) %collective-permute-start.8) | collective-permute-done | bytes 491552 | tf_op jit(solution)/shard_map/ppermute | solution.py:189
  57.7 6.1 %collective-permute-start.15 = (bf16[2,3,64,640]{3,2,1,0:T(8,128)(2,1)S(1)}, bf16[2,3,64,640]{3,2,1,0:T(8,128)(2,1)S(1)}, u32[]{:S(2)}, u32[]{:S(2)}) collective-permute-start(bf16[2,3,64,640]{3,2,1,0:T(8,128)(2,1)S(1)} %pad_maximum_fusion.8), channel_id=1, source_target_pairs={{0,1},{1,0},{2,3},{3,2},{4,5},{5,4},{6,7},{7,6},{8,9},{9,8},{10,11... | collective-permute-start | bytes 1474568 | tf_op jit(solution)/shard_map/ppermute | solution.py:189
  63.9 0.0 collective-permute-done.9
  63.9 4.5 %shard_map.47.refs_11_ = f32[2,2,384,640]{3,2,1,0:T(8,128)S(1)} custom-call(s32[4]{0:T(128)S(1)} %add_add_fusion.2.refs_0_, bf16[2,3,64,640]{3,2,1,0:T(8,128)(2,1)S(1)} %collective-permute-done.1.refs_1_, bf16[2,3,64,640]{3,2,1,0:T(8,128)(2,1)S(1)} %collective-permute-done.2.refs_2_, bf16[3,64,640]{2,1,0:T(8,128)(2,1)S(1)} %get-tuple-element.62.refs_3_, ...), custom_call_target="tpu_custom_call" | custom-call | flops 2264924160 | bytes 8388608 | tf_op jit(solution)/shard_map/pallas_call | solution.py:146
  68.5 0.1 pad_maximum_fusion.5
  68.6 0.1 collective-permute-start.12
  68.7 0.1 pad_maximum_fusion.6
  68.8 1.1 %collective-permute-start.13 = (bf16[2,3,64,640]{3,2,1,0:T(8,128)(2,1)S(1)}, bf16[2,3,64,640]{3,2,1,0:T(8,128)(2,1)S(1)}, u32[]{:S(2)}, u32[]{:S(2)}) collective-permute-start(bf16[2,3,64,640]{3,2,1,0:T(8,128)(2,1)S(1)} %pad_maximum_fusion.6), channel_id=1, source_target_pairs={{0,1},{1,0},{2,3},{3,2},{4,5},{5,4},{6,7},{7,6},{8,9},{9,8},{10,11... | collective-permute-start | bytes 1474568 | tf_op jit(solution)/shard_map/ppermute | solution.py:189
  70.0 4.5 %shard_map.48.refs_9_ = f32[2,2,384,640]{3,2,1,0:T(8,128)S(1)} custom-call(s32[4]{0:T(128)S(1)} %add_add_fusion.3.refs_0_, bf16[2,3,64,640]{3,2,1,0:T(8,128)(2,1)S(1)} %collective-permute-done.10.refs_1_, bf16[2,3,64,640]{3,2,1,0:T(8,128)(2,1)S(1)} %collective-permute-done.11.refs_2_, bf16[3,64,640]{2,1,0:T(8,128)(2,1)S(1)} %get-tuple-element.46.refs_3_, ...), custom_call_target="tpu_custom_call" | custom-call | flops 2264924160 | bytes 8388608 | tf_op jit(solution)/shard_map/pallas_call | solution.py:146
  74.5 2.2 %collective-permute-done.12 = bf16[2,3,64,640]{3,2,1,0:T(8,128)(2,1)S(1)} collective-permute-done((bf16[2,3,64,640]{3,2,1,0:T(8,128)(2,1)S(1)}, bf16[2,3,64,640]{3,2,1,0:T(8,128)(2,1)S(1)}, u32[]{:S(2)}, u32[]{:S(2)}) %collective-permute-start.12) | collective-permute-done | bytes 491552 | tf_op jit(solution)/shard_map/ppermute | solution.py:189
  76.8 4.4 %shard_map.49 = (bf16[2,2,64,640]{3,2,1,0:T(8,128)(2,1)S(1)}, bf16[2,2,64,640]{3,2,1,0:T(8,128)(2,1)S(1)}) custom-call(s32[4]{0:T(128)S(1)} %add_add_fusion.refs_0_, bf16[2,3,64,640]{3,2,1,0:T(8,128)(2,1)S(1)} %collective-permute-done.6.refs_1_, bf16[2,3,64,640]{3,2,1,0:T(8,128)(2,1)S(1)} %collective-permute-done.7.refs_2_, ...), custom_call_target="tpu_custom_call" | custom-call | flops 2264924160 | bytes 8388608 | tf_op jit(solution)/shard_map/pallas_call | solution.py:146
  81.2 4.2 %collective-permute-start.17 = (bf16[2,2,64,640]{3,2,1,0:T(8,128)(2,1)S(1)}, bf16[2,2,64,640]{3,2,1,0:T(8,128)(2,1)S(1)}, u32[]{:S(2)}, u32[]{:S(2)}) collective-permute-start(bf16[2,2,64,640]{3,2,1,0:T(8,128)(2,1)S(1)} %get-tuple-element.36), channel_id=1, source_target_pairs={{0,1},{1,0},{2,3},{3,2},{4,5},{5,4},{6,7},{7,6},{8,9},{9,8},{10,11... | collective-permute-start | bytes 983048 | tf_op jit(solution)/shard_map/ppermute | solution.py:189
  85.4 0.1 slice_bitcast_fusion.23
  85.5 0.1 slice_bitcast_fusion.27
  85.7 1.1 %collective-permute-done.17 = bf16[2,2,64,640]{3,2,1,0:T(8,128)(2,1)S(1)} collective-permute-done((bf16[2,2,64,640]{3,2,1,0:T(8,128)(2,1)S(1)}, bf16[2,2,64,640]{3,2,1,0:T(8,128)(2,1)S(1)}, u32[]{:S(2)}, u32[]{:S(2)}) %collective-permute-start.17) | collective-permute-done | bytes 327712 | tf_op jit(solution)/shard_map/ppermute | solution.py:189
  86.7 0.1 slice_bitcast_fusion.21
  86.8 0.1 broadcast_select_fusion.4
  87.0 0.1 slice_bitcast_fusion.25
  87.1 0.1 broadcast_select_fusion.5
  87.3 0.2 pad_maximum_fusion
  87.4 1.0 %copy.15 = bf16[4,4,64,320]{3,2,1,0:T(8,128)(2,1)} copy(bf16[4,4,64,320]{3,2,0,1:T(8,128)(2,1)S(1)} %pad_maximum_fusion) | data formatting | bytes 1310720 | tf_op jit(solution)/shard_map/stack | solution.py:228
  (38 shorter events, 0.7 us)
Async XLA Ops:
  0.0 22.4 %copy-start.8 = (f32[64]{0:T(128)S(1)}, f32[64]{0:T(128)}, u32[]{:S(2)}) copy-start(f32[64]{0:T(128)} %param.7) | copy-start | bytes 772
  0.0 1.1 %copy-start.5 = (bf16[4,4,64,320]{3,2,1,0:T(8,128)(2,1)S(1)}, bf16[4,4,64,320]{3,2,1,0:T(8,128)(2,1)}, u32[]{:S(2)}) copy-start(bf16[4,4,64,320]{3,2,1,0:T(8,128)(2,1)} %new_ref.1) | copy-start | bytes 1966084
  1.1 1.0 %copy-start.7 = (bf16[2,4,64,320]{3,2,1,0:T(8,128)(2,1)S(1)}, bf16[2,4,64,320]{3,2,1,0:T(8,128)(2,1)}, u32[]{:S(2)}) copy-start(bf16[2,4,64,320]{3,2,1,0:T(8,128)(2,1)} %cached_ref.1) | copy-start | bytes 983044
  3.5 0.8 copy-start.6
  4.3 4.8 %collective-permute-start = (bf16[2,3,64,640]{3,2,1,0:T(8,128)(2,1)S(1)}, bf16[2,3,64,640]{3,2,1,0:T(8,128)(2,1)}, u32[]{:S(2)}, u32[]{:S(2)}) collective-permute-start(bf16[2,3,64,640]{3,2,1,0:T(8,128)(2,1)S(1)} %get-tuple-element.22), channel_id=1, source_target_pairs={{0,1},{1,0},{2,3},{3,2},{4,5},{5,4},{6,7},{7,6},{8,9},{9,8},{10,11... | collective-permute-start | bytes 1474568 | tf_op jit(solution)/shard_map/ppermute | solution.py:189
  9.2 22.5 %collective-permute-start.5 = (bf16[3,3,3,64,512]{4,3,2,1,0:T(8,128)(2,1)}, bf16[3,3,3,64,512]{4,3,2,1,0:T(8,128)(2,1)S(1)}, u32[]{:S(2)}, u32[]{:S(2)}) collective-permute-start(bf16[3,3,3,64,512]{4,3,2,1,0:T(8,128)(2,1)} %refs_7_.3), channel_id=1, source_target_pairs={{0,1},{1,0},{2,3},{3,2},{4,5},{5,4},{6,7},{7,6},{8,9},{9,8},{10,11... | collective-permute-start | bytes 5308424 | tf_op jit(solution)/shard_map/ppermute | solution.py:189
  9.6 22.1 %copy-start = (bf16[3,3,3,64,512]{4,3,2,1,0:T(8,128)(2,1)S(1)}, bf16[3,3,3,64,512]{4,3,2,1,0:T(8,128)(2,1)}, u32[]{:S(2)}) copy-start(bf16[3,3,3,64,512]{4,3,2,1,0:T(8,128)(2,1)} %refs_7_.3) | copy-start | bytes 5308420
  11.0 0.8 copy-start.1
  11.0 1.7 %copy-start.3 = (bf16[2,3,64,640]{3,2,1,0:T(8,128)(2,1)}, bf16[2,3,64,640]{3,2,1,0:T(8,128)(2,1)S(1)}, u32[]{:S(2)}) copy-start(bf16[2,3,64,640]{3,2,1,0:T(8,128)(2,1)S(1)} %get-tuple-element.37.refs_2_) | copy-start | bytes 1474564
  13.5 13.1 %collective-permute-start.3 = (bf16[2,3,64,640]{3,2,1,0:T(8,128)(2,1)}, bf16[2,3,64,640]{3,2,1,0:T(8,128)(2,1)}, u32[]{:S(2)}, u32[]{:S(2)}) collective-permute-start(bf16[2,3,64,640]{3,2,1,0:T(8,128)(2,1)} %pad_maximum_fusion.1), channel_id=1, source_target_pairs={{9,1},{1,9},{11,3},{3,11},{13,5},{5,13},{15,7},{7,15},{16,8},{8,16... | collective-permute-start | bytes 1474568 | tf_op jit(solution)/shard_map/ppermute | solution.py:189
  15.5 12.3 %collective-permute-start.4 = (bf16[2,3,64,640]{3,2,1,0:T(8,128)(2,1)}, bf16[2,3,64,640]{3,2,1,0:T(8,128)(2,1)}, u32[]{:S(2)}, u32[]{:S(2)}) collective-permute-start(bf16[2,3,64,640]{3,2,1,0:T(8,128)(2,1)} %pad_maximum_fusion.2), channel_id=1, source_target_pairs={{0,1},{1,0},{2,3},{3,2},{4,5},{5,4},{6,7},{7,6},{8,9},{9,8},{10,11... | collective-permute-start | bytes 1474568 | tf_op jit(solution)/shard_map/ppermute | solution.py:189
  22.4 1.8 %collective-permute-start.16 = (f32[64]{0:T(128)S(1)}, f32[64]{0:T(128)S(1)}, u32[]{:S(2)}, u32[]{:S(2)}) collective-permute-start(f32[64]{0:T(128)S(1)} %copy-done.8), channel_id=1, source_target_pairs={{0,1},{1,0},{2,3},{3,2},{4,5},{5,4},{6,7},{7,6},{8,9},{9,8},{10,11... | collective-permute-start | bytes 776 | tf_op jit(solution)/shard_map/ppermute | solution.py:189
  22.5 27.0 %collective-permute-start.11 = (bf16[2,3,64,640]{3,2,1,0:T(8,128)(2,1)}, bf16[2,3,64,640]{3,2,1,0:T(8,128)(2,1)S(1)}, u32[]{:S(2)}, u32[]{:S(2)}) collective-permute-start(bf16[2,3,64,640]{3,2,1,0:T(8,128)(2,1)} %copy-done.3), channel_id=1, source_target_pairs={{0,2},{1,3},{2,4},{3,5},{4,6},{5,7},{6,0},{7,1},{8,10},{9,11},{10,... | collective-permute-start | bytes 1474568 | tf_op jit(solution)/shard_map/ppermute | solution.py:189
  24.1 13.8 %collective-permute-start.2 = (bf16[2,3,64,640]{3,2,1,0:T(8,128)(2,1)}, bf16[2,3,64,640]{3,2,1,0:T(8,128)(2,1)S(1)}, u32[]{:S(2)}, u32[]{:S(2)}) collective-permute-start(bf16[2,3,64,640]{3,2,1,0:T(8,128)(2,1)} %copy-done.3), channel_id=1, source_target_pairs={{2,0},{3,1},{4,2},{5,3},{6,4},{7,5},{0,6},{1,7},{10,8},{11,9},{12,... | collective-permute-start | bytes 1474568 | tf_op jit(solution)/shard_map/ppermute | solution.py:189
  26.6 20.2 %collective-permute-start.1 = (bf16[2,3,64,640]{3,2,1,0:T(8,128)(2,1)}, bf16[2,3,64,640]{3,2,1,0:T(8,128)(2,1)S(1)}, u32[]{:S(2)}, u32[]{:S(2)}) collective-permute-start(bf16[2,3,64,640]{3,2,1,0:T(8,128)(2,1)} %copy-done.1), channel_id=1, source_target_pairs={{0,2},{1,3},{2,4},{3,5},{4,6},{5,7},{6,0},{7,1},{8,10},{9,11},{10,... | collective-permute-start | bytes 1474568 | tf_op jit(solution)/shard_map/ppermute | solution.py:189
  27.8 21.7 %collective-permute-start.10 = (bf16[2,3,64,640]{3,2,1,0:T(8,128)(2,1)}, bf16[2,3,64,640]{3,2,1,0:T(8,128)(2,1)S(1)}, u32[]{:S(2)}, u32[]{:S(2)}) collective-permute-start(bf16[2,3,64,640]{3,2,1,0:T(8,128)(2,1)} %copy-done.1), channel_id=1, source_target_pairs={{2,0},{3,1},{4,2},{5,3},{6,4},{7,5},{0,6},{1,7},{10,8},{11,9},{12,... | collective-permute-start | bytes 1474568 | tf_op jit(solution)/shard_map/ppermute | solution.py:189
  31.7 1.0 %copy-start.2 = (bf16[2,3,64,640]{3,2,1,0:T(8,128)(2,1)S(1)}, bf16[2,3,64,640]{3,2,1,0:T(8,128)(2,1)}, u32[]{:S(2)}) copy-start(bf16[2,3,64,640]{3,2,1,0:T(8,128)(2,1)} %copy-done.1) | copy-start | bytes 1474564
  32.7 1.0 %copy-start.4 = (bf16[2,3,64,640]{3,2,1,0:T(8,128)(2,1)S(1)}, bf16[2,3,64,640]{3,2,1,0:T(8,128)(2,1)}, u32[]{:S(2)}) copy-start(bf16[2,3,64,640]{3,2,1,0:T(8,128)(2,1)} %copy-done.3) | copy-start | bytes 1474564
  46.8 21.6 %collective-permute-start.6 = (bf16[2,3,64,640]{3,2,1,0:T(8,128)(2,1)S(1)}, bf16[2,3,64,640]{3,2,1,0:T(8,128)(2,1)S(1)}, u32[]{:S(2)}, u32[]{:S(2)}) collective-permute-start(bf16[2,3,64,640]{3,2,1,0:T(8,128)(2,1)S(1)} %collective-permute-done.1.refs_1_), channel_id=1, source_target_pairs={{0,2},{1,3},{2,4},{3,5},{4,6},{5,7},{6,0},{7,1},{8,10},{9,11},{10,... | collective-permute-start | bytes 1474568 | tf_op jit(solution)/shard_map/ppermute | solution.py:189
  46.8 21.7 %collective-permute-start.7 = (bf16[2,3,64,640]{3,2,1,0:T(8,128)(2,1)S(1)}, bf16[2,3,64,640]{3,2,1,0:T(8,128)(2,1)S(1)}, u32[]{:S(2)}, u32[]{:S(2)}) collective-permute-start(bf16[2,3,64,640]{3,2,1,0:T(8,128)(2,1)S(1)} %collective-permute-done.2.refs_2_), channel_id=1, source_target_pairs={{2,0},{3,1},{4,2},{5,3},{6,4},{7,5},{0,6},{1,7},{10,8},{11,9},{12,... | collective-permute-start | bytes 1474568 | tf_op jit(solution)/shard_map/ppermute | solution.py:189
  49.7 8.1 %collective-permute-start.8 = (bf16[2,3,64,640]{3,2,1,0:T(8,128)(2,1)S(1)}, bf16[2,3,64,640]{3,2,1,0:T(8,128)(2,1)S(1)}, u32[]{:S(2)}, u32[]{:S(2)}) collective-permute-start(bf16[2,3,64,640]{3,2,1,0:T(8,128)(2,1)S(1)} %pad_maximum_fusion.3), channel_id=1, source_target_pairs={{9,1},{1,9},{11,3},{3,11},{13,5},{5,13},{15,7},{7,15},{16,8},{8,16... | collective-permute-start | bytes 1474568 | tf_op jit(solution)/shard_map/ppermute | solution.py:189
  49.8 14.0 %collective-permute-start.9 = (bf16[2,3,64,640]{3,2,1,0:T(8,128)(2,1)S(1)}, bf16[2,3,64,640]{3,2,1,0:T(8,128)(2,1)S(1)}, u32[]{:S(2)}, u32[]{:S(2)}) collective-permute-start(bf16[2,3,64,640]{3,2,1,0:T(8,128)(2,1)S(1)} %pad_maximum_fusion.4), channel_id=1, source_target_pairs={{0,1},{1,0},{2,3},{3,2},{4,5},{5,4},{6,7},{7,6},{8,9},{9,8},{10,11... | collective-permute-start | bytes 1474568 | tf_op jit(solution)/shard_map/ppermute | solution.py:189
  53.2 16.7 %collective-permute-start.14 = (bf16[2,3,64,640]{3,2,1,0:T(8,128)(2,1)S(1)}, bf16[2,3,64,640]{3,2,1,0:T(8,128)(2,1)S(1)}, u32[]{:S(2)}, u32[]{:S(2)}) collective-permute-start(bf16[2,3,64,640]{3,2,1,0:T(8,128)(2,1)S(1)} %pad_maximum_fusion.7), channel_id=1, source_target_pairs={{9,1},{1,9},{11,3},{3,11},{13,5},{5,13},{15,7},{7,15},{16,8},{8,16... | collective-permute-start | bytes 1474568 | tf_op jit(solution)/shard_map/ppermute | solution.py:189
  57.7 12.2 %collective-permute-start.15 = (bf16[2,3,64,640]{3,2,1,0:T(8,128)(2,1)S(1)}, bf16[2,3,64,640]{3,2,1,0:T(8,128)(2,1)S(1)}, u32[]{:S(2)}, u32[]{:S(2)}) collective-permute-start(bf16[2,3,64,640]{3,2,1,0:T(8,128)(2,1)S(1)} %pad_maximum_fusion.8), channel_id=1, source_target_pairs={{0,1},{1,0},{2,3},{3,2},{4,5},{5,4},{6,7},{7,6},{8,9},{9,8},{10,11... | collective-permute-start | bytes 1474568 | tf_op jit(solution)/shard_map/ppermute | solution.py:189
  68.6 8.1 %collective-permute-start.12 = (bf16[2,3,64,640]{3,2,1,0:T(8,128)(2,1)S(1)}, bf16[2,3,64,640]{3,2,1,0:T(8,128)(2,1)S(1)}, u32[]{:S(2)}, u32[]{:S(2)}) collective-permute-start(bf16[2,3,64,640]{3,2,1,0:T(8,128)(2,1)S(1)} %pad_maximum_fusion.5), channel_id=1, source_target_pairs={{9,1},{1,9},{11,3},{3,11},{13,5},{5,13},{15,7},{7,15},{16,8},{8,16... | collective-permute-start | bytes 1474568 | tf_op jit(solution)/shard_map/ppermute | solution.py:189
  68.8 8.0 %collective-permute-start.13 = (bf16[2,3,64,640]{3,2,1,0:T(8,128)(2,1)S(1)}, bf16[2,3,64,640]{3,2,1,0:T(8,128)(2,1)S(1)}, u32[]{:S(2)}, u32[]{:S(2)}) collective-permute-start(bf16[2,3,64,640]{3,2,1,0:T(8,128)(2,1)S(1)} %pad_maximum_fusion.6), channel_id=1, source_target_pairs={{0,1},{1,0},{2,3},{3,2},{4,5},{5,4},{6,7},{7,6},{8,9},{9,8},{10,11... | collective-permute-start | bytes 1474568 | tf_op jit(solution)/shard_map/ppermute | solution.py:189
  81.2 5.5 %collective-permute-start.17 = (bf16[2,2,64,640]{3,2,1,0:T(8,128)(2,1)S(1)}, bf16[2,2,64,640]{3,2,1,0:T(8,128)(2,1)S(1)}, u32[]{:S(2)}, u32[]{:S(2)}) collective-permute-start(bf16[2,2,64,640]{3,2,1,0:T(8,128)(2,1)S(1)} %get-tuple-element.36), channel_id=1, source_target_pairs={{0,1},{1,0},{2,3},{3,2},{4,5},{5,4},{6,7},{7,6},{8,9},{9,8},{10,11... | collective-permute-start | bytes 983048 | tf_op jit(solution)/shard_map/ppermute | solution.py:189
where the time goes:
time: 88.7 us; the launch traced here: 88.4 us
  starting transfers between devices  34.6 us (39%)
  Pallas kernels  18.9 us (21%)
  waiting for transfers between devices  18.4 us (21%)
  local copies, waits for them, and re-layouts  10.9 us (12%)
  other arithmetic  5.21 us (6%)
    ppermute x18, starting transfers between devices, send(): return lax.ppermute(a, axes, pairs)  34.6 us
    ppermute x18, waiting for transfers between devices, send(): return lax.ppermute(a, axes, pairs)  18.4 us
    pallas_call x4, Pallas kernels, block_call(): pl.pallas_call(functools.partial(block_kernel, mixed, first, last), grid_...  17.5 us
    unnamed x18, local copies, waits for them, and re-layouts  5.74 us
    squeeze x8, local copies, waits for them, and re-layouts, halos(): return ((z[0], z[1]), (c[0], c[1]))  2.48 us
    another operation x4, other arithmetic, halos(): c = send(jnp.stack([a[1], b[1]]), swap)  2.08 us
  transfers between devices with their start and end apart: 18, of which 6 were waited for; matrix products, arithmetic and copies ran while one was open for 10% of the time, Pallas kernels for 15%

commit v1 on v0

v1 whole, which is shorter than its diff:
```python
import functools

import jax
import jax.numpy as jnp
from jax import lax
from jax.experimental import pallas as pl
from jax.experimental.pallas import tpu as pltpu
from jax.sharding import PartitionSpec as P


BF = jnp.bfloat16
F32 = jnp.float32
LANES = 128
OWN, LEFT_RIGHT, RIGHT_LEFT, FAR = (2, 2), (3, 4), (4, 3), (5, 5)
HALF = 64


def turn(pairs):
    width = pairs.shape[-1]
    return pltpu.roll(pairs.astype(F32), width // 2, axis=1)


def pack_kernel(flip_ref, cached_ref, new_ref, kept_ref, sent_ref):
    cols = cached_ref.shape[-1]
    upper = flip_ref[0]
    place = [
        (lax.broadcasted_iota(jnp.int32, (cols, 2 * cols), 0) + h * cols
         == lax.broadcasted_iota(jnp.int32, (cols, 2 * cols), 1)).astype(F32).astype(BF)
        for h in range(2)
    ]
    for out, flip in ((kept_ref, upper), (sent_ref, 1 - upper)):
        for row in range(2):
            at = jnp.where(flip == 0, row, 3 - row)
            for pair in range(3):
                first = cached_ref[0, at] if pair == 0 else new_ref[2 * pair - 2, at]
                second = cached_ref[1, at] if pair == 0 else new_ref[2 * pair - 1, at]
                both = jnp.dot(first, place[0], preferred_element_type=F32)
                both = both + jnp.dot(second, place[1], preferred_element_type=F32)
                out[row, pair] = both.astype(BF)


def pack(flip, cached, new):
    channels, cols = cached.shape[2:]
    shape = jax.ShapeDtypeStruct((2, 3, channels, 2 * cols), BF)
    return pl.pallas_call(
        pack_kernel,
        in_specs=[pl.BlockSpec(memory_space=pltpu.SMEM)] + [pl.BlockSpec(memory_space=pltpu.VMEM)] * 2,
        out_specs=[pl.BlockSpec(memory_space=pltpu.VMEM)] * 2,
        out_shape=[shape, shape],
        compiler_params=pltpu.CompilerParams(vmem_limit_bytes=16 * 2**20),
        cost_estimate=pl.CostEstimate(flops=10**8, bytes_accessed=4 * 2**20, transcendentals=0),
        name="pack",
    )(flip, cached, new)


def block_kernel(blocks, first, last, *refs):
    scalars, refs = refs[0], list(refs[1:])
    bodies = [refs.pop(0), refs.pop(0)]
    zsides, csides = refs.pop(0), refs.pop(0)
    weights = [refs.pop(0), refs.pop(0)]
    before = None if first else refs.pop(0)
    bias = refs.pop(0) if last else None
    outs = [refs.pop(0), refs.pop(0)] if last else [refs.pop(0)]
    (xs,) = refs
    flip, edge = scalars[0], scalars[1] == 1
    width = xs.shape[-1]
    cols = width // 2
    near = lax.broadcasted_iota(jnp.int32, (HALF, width), 1) < cols
    lanes = [pl.ds(pl.multiple_of(scalars[at] * LANES, LANES), LANES) for at in blocks]
    mixed = blocks[0] != blocks[1]

    channel = lax.broadcasted_iota(jnp.int32, (1, LANES), 1)
    from_first = channel < HALF

    def one_pair(p, carry):
        for piece in range(2):
            at = pl.ds(piece * HALF, HALF)
            rows = [
                lambda q: jnp.where(edge, jnp.zeros((HALF, width), BF), zsides[piece, q]),
                lambda q: bodies[piece][0, q],
                lambda q: bodies[piece][1, q],
                lambda q: csides[piece, q],
            ]
            for row in range(4):
                low, high = rows[row](p), rows[row](p + 1)
                xs[0, row, at] = low
                xs[2, row, at] = high
                xs[1, row, at] = jnp.where(near, turn(low), turn(high)).astype(BF)

        taps = []
        for t in range(3):
            for delta in range(3):
                row_tap = jnp.where(flip == 0, delta, 2 - delta)
                halves = []
                for half in range(2):
                    w = weights[half][t, row_tap, :, :, lanes[0]]
                    w = w.reshape(w.shape[0] * w.shape[1], LANES)
                    if mixed:
                        v = weights[half][t, row_tap, :, :, lanes[1]].reshape(w.shape)
                        w = jnp.where(jnp.broadcast_to(from_first, w.shape), w, v)
                    halves.append(w)
                taps.append(jnp.concatenate(halves, axis=0))
        lhs = jnp.concatenate(taps, axis=1)
        rows = lhs.shape[0] // 6
        lane = lax.broadcasted_iota(jnp.int32, (rows, width), 1)
        zero = jnp.zeros((rows, width), F32)
        left_edge = (lane == 0) | (lane == cols)
        right_edge = (lane == cols - 1) | (lane == width - 1)
        for row in range(2):
            window = jnp.concatenate(
                [xs[t, row : row + 3].reshape(3 * LANES, width) for t in range(3)], axis=0
            )
            acc = jnp.dot(lhs, window, preferred_element_type=F32)
            if not first:
                acc = acc + before[p, row]
            if not last:
                outs[0][p, row] = acc
                continue
            for half in range(2):
                part = acc[half * 3 * rows : (half + 1) * 3 * rows]
                from_left = jnp.where(left_edge, zero, pltpu.roll(part[:rows], 1, axis=1))
                from_right = jnp.where(right_edge, zero, pltpu.roll(part[2 * rows :], width - 1, axis=1))
                total = part[rows : 2 * rows] + from_left + from_right + bias[half][:, None]
                outs[half][p, row] = total.astype(BF)
        return carry

    lax.fori_loop(0, 2, one_pair, 0)


def block_call(scalars, blocks, bodies, zsides, csides, weights, before, bias):
    first, last = before is None, bias is not None
    own, other = weights
    outs64 = own.shape[3]
    rows = 2 * 3 * outs64
    width = bodies[0].shape[-1]
    operands = [*bodies, zsides, csides, own, other]
    aliases = {}
    if not first:
        operands.append(before)
    if last:
        operands.append(bias)
        out_shape = [jax.ShapeDtypeStruct((2, 2, outs64, width), BF)] * 2
    else:
        out_shape = [jax.ShapeDtypeStruct((2, 2, rows, width), F32)]
        if not first:
            aliases = {len(operands): 0}
    vmem = pl.BlockSpec(memory_space=pltpu.VMEM)
    result = pl.pallas_call(
        functools.partial(block_kernel, blocks, first, last),
        in_specs=[pl.BlockSpec(memory_space=pltpu.SMEM)] + [vmem] * len(operands),
        out_specs=[vmem] * len(out_shape),
        scratch_shapes=[pltpu.VMEM((3, 4, LANES, width), BF)],
        out_shape=out_shape,
        input_output_aliases=aliases,
        compiler_params=pltpu.CompilerParams(vmem_limit_bytes=28 * 2**20),
        cost_estimate=pl.CostEstimate(
            flops=2 * 4 * rows * 9 * LANES * width, bytes_accessed=8 * 2**20, transcendentals=0
        ),
    )(scalars, *operands)
    return result if last else result[0]


def solution(mesh):
    bands, chans = mesh.shape["band"], mesh.shape["chan"]
    chips = chans // 2
    swap = [(2 * x + c, 2 * x + 1 - c) for x in range(chips) for c in range(2)]
    right = [(2 * x + c, 2 * ((x + 1) % chips) + c) for x in range(chips) for c in range(2)]
    left = [(target, source) for source, target in right]
    across = []
    for b in range(1, bands):
        for x in range(chips):
            here, there = b * chans + 2 * x + b % 2, (b - 1) * chans + 2 * x + b % 2
            across += [(here, there), (there, here)]
    for x in range(chips):
        for own in (2 * x, (bands - 1) * chans + 2 * x + bands % 2):
            across += [(own, own)]

    def on_device(new_frames, cached_frames, conv_weight, out_bias):
        cols = new_frames.shape[-1]
        index = lax.axis_index("chan")
        core, chip = index % 2, index // 2
        even = core == 0
        flip = (core + lax.axis_index("band")) % 2
        upper = flip == 0
        band = lax.axis_index("band")
        edge = jnp.where(upper, band == 0, band == bands - 1)

        def send(a, pairs, axes="chan"):
            return lax.ppermute(a, axes, pairs)

        def halos(a, b):
            c = send(jnp.stack([a[1], b[1]]), swap)
            z = send(jnp.stack([a[0], b[0]]), across, ("band", "chan"))
            return z, c

        scalars = jnp.stack([flip, edge.astype(flip.dtype)] + [(chip + o) % chips for o in (0, chips - 1, 1, 2)])
        scalars, upper, even = lax.optimization_barrier((scalars.astype(jnp.int32), upper, even))
        kept, sent = pack(scalars, cached_frames, new_frames)
        got = send(sent, swap)
        got, conv_weight, out_bias = lax.optimization_barrier((got, conv_weight, out_bias))
        other_weight = send(conv_weight, swap)
        biases = jnp.stack([out_bias, send(out_bias, swap)])
        lo, hi = jnp.where(even, kept, got), jnp.where(even, got, kept)
        l_lo = send(lo, right)
        r_hi = send(hi, left)
        l_hi = send(hi, right)
        r_lo = send(lo, left)
        weights = (conv_weight, other_weight)

        acc = block_call(scalars, OWN, (lo, hi), *halos(lo, hi), weights, None, None)
        l_lo, r_hi, acc = lax.optimization_barrier((l_lo, r_hi, acc))
        f_lo = send(l_lo, right)
        f_hi = send(r_hi, left)
        r_lo, l_hi, acc = lax.optimization_barrier((r_lo, l_hi, acc))
        acc = block_call(scalars, LEFT_RIGHT, (l_lo, r_hi), *halos(l_lo, r_hi), weights, acc, None)
        f_lo, f_hi, acc = lax.optimization_barrier((f_lo, f_hi, acc))
        acc = block_call(scalars, RIGHT_LEFT, (r_lo, l_hi), *halos(r_lo, l_hi), weights, acc, None)
        mine, theirs = block_call(scalars, FAR, (f_lo, f_hi), *halos(f_lo, f_hi), weights, acc, biases)
        given = send(theirs, swap)

        def row(a, r):
            a = a[:, r]
            return jnp.stack([a[..., :cols], a[..., cols:]], axis=1).reshape(4, a.shape[1], cols)

        m, g = [row(mine, 0), row(mine, 1)], [row(given, 0), row(given, 1)]
        return jnp.stack([jnp.where(upper, a, b) for a, b in zip(m + g[::-1], g + m[::-1])], axis=1)

    in_specs = (
        P(None, "band", "chan", None),
        P(None, "band", "chan", None),
        P(None, None, None, "chan", None),
        P("chan"),
    )

    return jax.shard_map(
        on_device, mesh=mesh, in_specs=in_specs, out_specs=P(None, "band", "chan", None), check_vma=False
    )
```

time: 88.7 us -> 80 us (0.902)
  the two profiles are of different devices: /device:TPU:1 before, /device:TPU:31 now
where the time goes in v1:
time: 80 us; the launch traced here: 79.7 us
  starting transfers between devices  34 us (42%)
  waiting for transfers between devices  21.8 us (27%)
  Pallas kernels  18.6 us (23%)
  local copies, waits for them, and re-layouts  4.19 us (5%)
  other arithmetic  0.91 us (1%)
    ppermute x18, starting transfers between devices, send(): return lax.ppermute(a, axes, pairs)  34 us
    ppermute x18, waiting for transfers between devices, send(): return lax.ppermute(a, axes, pairs)  21.8 us
    pallas_call x4, Pallas kernels, block_call(): pl.pallas_call(functools.partial(block_kernel, blocks, first, last), in_s...  16.6 us
    unnamed x8, local copies, waits for them, and re-layouts  2.25 us
    pallas_call x1, Pallas kernels, pack(): pl.pallas_call(pack_kernel, in_specs=[pl.BlockSpec(memory_space=pltpu.SME...  1.94 us
  transfers between devices with their start and end apart: 18, of which 7 were waited for; matrix products, arithmetic and copies ran while one was open for 1% of the time, Pallas kernels for 16%

profile of v1, /device:TPU:31, one launch (start us, length us, event | category | flops | bytes accessed | tf_op | source)
XLA Modules:
  0.0 79.7 jit_solution(16269399017578374962)
XLA Ops:
  0.0 0.0 copy-start
  0.0 0.1 stack.107.flip_ref.refs_0_
  0.1 1.2 %copy-done.1 = bf16[4,4,64,320]{3,2,1,0:T(8,128)(2,1)S(1)} copy-done((bf16[4,4,64,320]{3,2,1,0:T(8,128)(2,1)S(1)}, bf16[4,4,64,320]{3,2,1,0:T(8,128)(2,1)}, u32[]{:S(2)}) %copy-start.1) | copy-done | bytes 655384
  1.3 1.0 %copy-done.2 = bf16[2,4,64,320]{3,2,1,0:T(8,128)(2,1)S(1)} copy-done((bf16[2,4,64,320]{3,2,1,0:T(8,128)(2,1)S(1)}, bf16[2,4,64,320]{3,2,1,0:T(8,128)(2,1)}, u32[]{:S(2)}) %copy-start.2) | copy-done | bytes 327704
  2.3 1.9 %pack.1 = (bf16[2,3,64,640]{3,2,1,0:T(8,128)(2,1)S(1)}, bf16[2,3,64,640]{3,2,1,0:T(8,128)(2,1)S(1)}) custom-call(s32[6]{0:T(128)S(1)} %stack.107.flip_ref.refs_0_, bf16[2,4,64,320]{3,2,1,0:T(8,128)(2,1)S(1)} %copy-done.2, bf16[4,4,64,320]{3,2,1,0:T(8,128)(2,1)S(1)} %copy-done.1), custom_call_target="tpu_custom_call" | custom-call | flops 100000000 | bytes 4194304 | tf_op jit(solution)/shard_map/pack/pallas_call | solution.py:45
  4.3 0.8 collective-permute-start
  5.0 1.5 %collective-permute-done = bf16[2,3,64,640]{3,2,1,0:T(8,128)(2,1)S(1)} collective-permute-done((bf16[2,3,64,640]{3,2,1,0:T(8,128)(2,1)S(1)}, bf16[2,3,64,640]{3,2,1,0:T(8,128)(2,1)S(1)}, u32[]{:S(2)}, u32[]{:S(2)}) %collective-permute-start) | collective-permute-done | bytes 491552 | tf_op jit(solution)/shard_map/ppermute | solution.py:189
  6.5 0.4 collective-permute-start.5
  6.9 0.1 broadcast_select_fusion
  7.1 0.1 pad_maximum_fusion.2
  7.2 0.2 collective-permute-start.4
  7.4 0.1 pad_maximum_fusion.1
  7.5 3.6 %collective-permute-start.3 = (bf16[2,3,64,640]{3,2,1,0:T(8,128)(2,1)S(1)}, bf16[2,3,64,640]{3,2,1,0:T(8,128)(2,1)S(1)}, u32[]{:S(2)}, u32[]{:S(2)}) collective-permute-start(bf16[2,3,64,640]{3,2,1,0:T(8,128)(2,1)S(1)} %pad_maximum_fusion.1), channel_id=1, source_target_pairs={{9,1},{1,9},{11,3},{3,11},{13,5},{5,13},{15,7},{7,15},{16,8},{8,16... | collective-permute-start | bytes 1474568 | tf_op jit(solution)/shard_map/ppermute | solution.py:189
  11.0 0.3 collective-permute-start.1
  11.3 1.3 %collective-permute-start.2 = (bf16[2,3,64,640]{3,2,1,0:T(8,128)(2,1)S(1)}, bf16[2,3,64,640]{3,2,1,0:T(8,128)(2,1)S(1)}, u32[]{:S(2)}, u32[]{:S(2)}) collective-permute-start(bf16[2,3,64,640]{3,2,1,0:T(8,128)(2,1)S(1)} %get-tuple-element.43.refs_2_), channel_id=1, source_target_pairs={{2,0},{3,1},{4,2},{5,3},{6,4},{7,5},{0,6},{1,7},{10,8},{11,9},{12,... | collective-permute-start | bytes 1474568 | tf_op jit(solution)/shard_map/ppermute | solution.py:189
  12.6 0.0 collective-permute-done.4.refs_4_
  12.6 0.5 collective-permute-start.10
  13.1 4.4 %collective-permute-done.3.refs_3_ = bf16[2,3,64,640]{3,2,1,0:T(8,128)(2,1)S(1)} collective-permute-done((bf16[2,3,64,640]{3,2,1,0:T(8,128)(2,1)S(1)}, bf16[2,3,64,640]{3,2,1,0:T(8,128)(2,1)S(1)}, u32[]{:S(2)}, u32[]{:S(2)}) %collective-permute-start.3) | collective-permute-done | bytes 491552 | tf_op jit(solution)/shard_map/ppermute | solution.py:189
  17.5 0.2 collective-permute-start.11
  17.7 0.0 collective-permute-done.5.refs_6_
  17.7 0.0 copy-done
  17.7 4.0 %shard_map.46.refs_7_ = f32[2,2,384,640]{3,2,1,0:T(8,128)S(1)} custom-call(s32[6]{0:T(128)S(1)} %stack.107.flip_ref.refs_0_, bf16[2,3,64,640]{3,2,1,0:T(8,128)(2,1)S(1)} %get-tuple-element.44.refs_1_, bf16[2,3,64,640]{3,2,1,0:T(8,128)(2,1)S(1)} %get-tuple-element.43.refs_2_, bf16[2,3,64,640]{3,2,1,0:T(8,128)(2,1)S(1)} %collective-permute-done.3.refs_3_, ...), custom_call_target="tpu_custom_call" | custom-call | flops 2264924160 | bytes 8388608 | tf_op jit(solution)/shard_map/pallas_call | solution.py:148
  21.8 0.0 collective-permute-done.1.refs_1_
  21.8 0.0 collective-permute-done.2.refs_2_
  21.8 1.3 %collective-permute-start.6 = (bf16[2,3,64,640]{3,2,1,0:T(8,128)(2,1)S(1)}, bf16[2,3,64,640]{3,2,1,0:T(8,128)(2,1)S(1)}, u32[]{:S(2)}, u32[]{:S(2)}) collective-permute-start(bf16[2,3,64,640]{3,2,1,0:T(8,128)(2,1)S(1)} %collective-permute-done.1.refs_1_), channel_id=1, source_target_pairs={{0,2},{1,3},{2,4},{3,5},{4,6},{5,7},{6,0},{7,1},{8,10},{9,11},{10,... | collective-permute-start | bytes 1474568 | tf_op jit(solution)/shard_map/ppermute | solution.py:189
  23.1 0.3 collective-permute-start.7
  23.4 7.3 %collective-permute-done.10.refs_1_ = bf16[2,3,64,640]{3,2,1,0:T(8,128)(2,1)S(1)} collective-permute-done((bf16[2,3,64,640]{3,2,1,0:T(8,128)(2,1)S(1)}, bf16[2,3,64,640]{3,2,1,0:T(8,128)(2,1)S(1)}, u32[]{:S(2)}, u32[]{:S(2)}) %collective-permute-start.10) | collective-permute-done | bytes 491552 | tf_op jit(solution)/shard_map/ppermute | solution.py:189
  30.8 0.0 collective-permute-done.11.refs_2_
  30.8 0.1 pad_maximum_fusion.4
  30.9 11.3 %collective-permute-start.9 = (bf16[2,3,64,640]{3,2,1,0:T(8,128)(2,1)S(1)}, bf16[2,3,64,640]{3,2,1,0:T(8,128)(2,1)S(1)}, u32[]{:S(2)}, u32[]{:S(2)}) collective-permute-start(bf16[2,3,64,640]{3,2,1,0:T(8,128)(2,1)S(1)} %pad_maximum_fusion.4), channel_id=1, source_target_pairs={{0,1},{1,0},{2,3},{3,2},{4,5},{5,4},{6,7},{7,6},{8,9},{9,8},{10,11... | collective-permute-start | bytes 1474568 | tf_op jit(solution)/shard_map/ppermute | solution.py:189
  42.2 0.1 pad_maximum_fusion.3
  42.2 1.9 %collective-permute-start.8 = (bf16[2,3,64,640]{3,2,1,0:T(8,128)(2,1)S(1)}, bf16[2,3,64,640]{3,2,1,0:T(8,128)(2,1)S(1)}, u32[]{:S(2)}, u32[]{:S(2)}) collective-permute-start(bf16[2,3,64,640]{3,2,1,0:T(8,128)(2,1)S(1)} %pad_maximum_fusion.3), channel_id=1, source_target_pairs={{9,1},{1,9},{11,3},{3,11},{13,5},{5,13},{15,7},{7,15},{16,8},{8,16... | collective-permute-start | bytes 1474568 | tf_op jit(solution)/shard_map/ppermute | solution.py:189
  44.2 0.1 pad_maximum_fusion.8
  44.3 0.3 collective-permute-start.15
  44.6 0.1 pad_maximum_fusion.7
  44.7 0.0 collective-permute-done.9.refs_4_
  44.7 3.3 %collective-permute-start.14 = (bf16[2,3,64,640]{3,2,1,0:T(8,128)(2,1)S(1)}, bf16[2,3,64,640]{3,2,1,0:T(8,128)(2,1)S(1)}, u32[]{:S(2)}, u32[]{:S(2)}) collective-permute-start(bf16[2,3,64,640]{3,2,1,0:T(8,128)(2,1)S(1)} %pad_maximum_fusion.7), channel_id=1, source_target_pairs={{9,1},{1,9},{11,3},{3,11},{13,5},{5,13},{15,7},{7,15},{16,8},{8,16... | collective-permute-start | bytes 1474568 | tf_op jit(solution)/shard_map/ppermute | solution.py:189
  48.0 4.1 %collective-permute-done.8.refs_3_ = bf16[2,3,64,640]{3,2,1,0:T(8,128)(2,1)S(1)} collective-permute-done((bf16[2,3,64,640]{3,2,1,0:T(8,128)(2,1)S(1)}, bf16[2,3,64,640]{3,2,1,0:T(8,128)(2,1)S(1)}, u32[]{:S(2)}, u32[]{:S(2)}) %collective-permute-start.8) | collective-permute-done | bytes 491552 | tf_op jit(solution)/shard_map/ppermute | solution.py:189
  52.1 4.2 %shard_map.47.refs_7_ = f32[2,2,384,640]{3,2,1,0:T(8,128)S(1)} custom-call(s32[6]{0:T(128)S(1)} %stack.107.flip_ref.refs_0_, bf16[2,3,64,640]{3,2,1,0:T(8,128)(2,1)S(1)} %collective-permute-done.1.refs_1_, bf16[2,3,64,640]{3,2,1,0:T(8,128)(2,1)S(1)} %collective-permute-done.2.refs_2_, ...), custom_call_target="tpu_custom_call", output_to_operand_aliasing={{}: (7, {})} | custom-call | flops 2264924160 | bytes 8388608 | tf_op jit(solution)/shard_map/pallas_call | solution.py:148
  56.3 0.0 copy-start.3
  56.3 0.0 collective-permute-done.6.refs_1_
  56.3 0.0 collective-permute-done.7.refs_2_
  56.4 0.1 pad_maximum_fusion.6
  56.5 3.1 %collective-permute-start.13 = (bf16[2,3,64,640]{3,2,1,0:T(8,128)(2,1)S(1)}, bf16[2,3,64,640]{3,2,1,0:T(8,128)(2,1)S(1)}, u32[]{:S(2)}, u32[]{:S(2)}) collective-permute-start(bf16[2,3,64,640]{3,2,1,0:T(8,128)(2,1)S(1)} %pad_maximum_fusion.6), channel_id=1, source_target_pairs={{0,1},{1,0},{2,3},{3,2},{4,5},{5,4},{6,7},{7,6},{8,9},{9,8},{10,11... | collective-permute-start | bytes 1474568 | tf_op jit(solution)/shard_map/ppermute | solution.py:189
  59.6 0.1 pad_maximum_fusion.5
  59.6 1.9 %collective-permute-start.12 = (bf16[2,3,64,640]{3,2,1,0:T(8,128)(2,1)S(1)}, bf16[2,3,64,640]{3,2,1,0:T(8,128)(2,1)S(1)}, u32[]{:S(2)}, u32[]{:S(2)}) collective-permute-start(bf16[2,3,64,640]{3,2,1,0:T(8,128)(2,1)S(1)} %pad_maximum_fusion.5), channel_id=1, source_target_pairs={{9,1},{1,9},{11,3},{3,11},{13,5},{5,13},{15,7},{7,15},{16,8},{8,16... | collective-permute-start | bytes 1474568 | tf_op jit(solution)/shard_map/ppermute | solution.py:189
  61.5 0.0 copy-done.3
  61.6 0.3 collective-permute-start.16
  61.9 0.9 %collective-permute-done.16 = f32[64]{0:T(128)S(1)} collective-permute-done((f32[64]{0:T(128)S(1)}, f32[64]{0:T(128)S(1)}, u32[]{:S(2)}, u32[]{:S(2)}) %collective-permute-start.16) | collective-permute-done | bytes 288 | tf_op jit(solution)/shard_map/ppermute | solution.py:189
  62.8 0.0 collective-permute-done.15.refs_4_
  62.8 0.0 collective-permute-done.14.refs_3_
  62.8 4.2 %shard_map.48.refs_7_ = f32[2,2,384,640]{3,2,1,0:T(8,128)S(1)} custom-call(s32[6]{0:T(128)S(1)} %stack.107.flip_ref.refs_0_, bf16[2,3,64,640]{3,2,1,0:T(8,128)(2,1)S(1)} %collective-permute-done.10.refs_1_, bf16[2,3,64,640]{3,2,1,0:T(8,128)(2,1)S(1)} %collective-permute-done.11.refs_2_, ...), custom_call_target="tpu_custom_call", output_to_operand_aliasing={{}: (7, {})} | custom-call | flops 2264924160 | bytes 8388608 | tf_op jit(solution)/shard_map/pallas_call | solution.py:148
  67.0 0.0 collective-permute-done.13.refs_4_
  67.0 2.5 %collective-permute-done.12.refs_3_ = bf16[2,3,64,640]{3,2,1,0:T(8,128)(2,1)S(1)} collective-permute-done((bf16[2,3,64,640]{3,2,1,0:T(8,128)(2,1)S(1)}, bf16[2,3,64,640]{3,2,1,0:T(8,128)(2,1)S(1)}, u32[]{:S(2)}, u32[]{:S(2)}) %collective-permute-start.12) | collective-permute-done | bytes 491552 | tf_op jit(solution)/shard_map/ppermute | solution.py:189
  69.5 4.2 %shard_map.49 = (bf16[2,2,64,640]{3,2,1,0:T(8,128)(2,1)S(1)}, bf16[2,2,64,640]{3,2,1,0:T(8,128)(2,1)S(1)}) custom-call(s32[6]{0:T(128)S(1)} %stack.107.flip_ref.refs_0_, bf16[2,3,64,640]{3,2,1,0:T(8,128)(2,1)S(1)} %collective-permute-done.6.refs_1_, bf16[2,3,64,640]{3,2,1,0:T(8,128)(2,1)S(1)} %collective-permute-done.7.refs_2_, ...), custom_call_target="tpu_custom_call" | custom-call | flops 2264924160 | bytes 8388608 | tf_op jit(solution)/shard_map/pallas_call | solution.py:148
  73.7 3.1 %collective-permute-start.17 = (bf16[2,2,64,640]{3,2,1,0:T(8,128)(2,1)S(1)}, bf16[2,2,64,640]{3,2,1,0:T(8,128)(2,1)S(1)}, u32[]{:S(2)}, u32[]{:S(2)}) collective-permute-start(bf16[2,2,64,640]{3,2,1,0:T(8,128)(2,1)S(1)} %get-tuple-element.42), channel_id=1, source_target_pairs={{0,1},{1,0},{2,3},{3,2},{4,5},{5,4},{6,7},{7,6},{8,9},{9,8},{10,11... | collective-permute-start | bytes 983048 | tf_op jit(solution)/shard_map/ppermute | solution.py:189
  76.8 0.1 slice_bitcast_fusion.7
  76.9 0.1 slice_bitcast_fusion.11
  77.0 1.0 %collective-permute-done.17 = bf16[2,2,64,640]{3,2,1,0:T(8,128)(2,1)S(1)} collective-permute-done((bf16[2,2,64,640]{3,2,1,0:T(8,128)(2,1)S(1)}, bf16[2,2,64,640]{3,2,1,0:T(8,128)(2,1)S(1)}, u32[]{:S(2)}, u32[]{:S(2)}) %collective-permute-start.17) | collective-permute-done | bytes 327712 | tf_op jit(solution)/shard_map/ppermute | solution.py:189
  78.1 0.1 slice_bitcast_fusion.5
  78.2 0.1 slice_bitcast_fusion.9
  78.3 0.2 broadcast_select_fusion.4
  78.6 0.2 pad_maximum_fusion
  78.8 1.0 %copy.17 = bf16[4,4,64,320]{3,2,1,0:T(8,128)(2,1)} copy(bf16[4,4,64,320]{3,2,0,1:T(8,128)(2,1)S(1)} %pad_maximum_fusion) | data formatting | bytes 1310720 | tf_op jit(solution)/shard_map/stack | solution.py:226
  (17 shorter events, 0.5 us)
Async XLA Ops:
  0.0 17.7 %copy-start = (bf16[3,3,3,64,512]{4,3,2,1,0:T(8,128)(2,1)S(1)}, bf16[3,3,3,64,512]{4,3,2,1,0:T(8,128)(2,1)}, u32[]{:S(2)}) copy-start(bf16[3,3,3,64,512]{4,3,2,1,0:T(8,128)(2,1)} %refs_5_.3) | copy-start | bytes 5308420
  0.1 1.2 %copy-start.1 = (bf16[4,4,64,320]{3,2,1,0:T(8,128)(2,1)S(1)}, bf16[4,4,64,320]{3,2,1,0:T(8,128)(2,1)}, u32[]{:S(2)}) copy-start(bf16[4,4,64,320]{3,2,1,0:T(8,128)(2,1)} %new_ref.1) | copy-start | bytes 1966084
  1.3 1.0 %copy-start.2 = (bf16[2,4,64,320]{3,2,1,0:T(8,128)(2,1)S(1)}, bf16[2,4,64,320]{3,2,1,0:T(8,128)(2,1)}, u32[]{:S(2)}) copy-start(bf16[2,4,64,320]{3,2,1,0:T(8,128)(2,1)} %cached_ref.1) | copy-start | bytes 983044
  4.3 2.2 %collective-permute-start = (bf16[2,3,64,640]{3,2,1,0:T(8,128)(2,1)S(1)}, bf16[2,3,64,640]{3,2,1,0:T(8,128)(2,1)S(1)}, u32[]{:S(2)}, u32[]{:S(2)}) collective-permute-start(bf16[2,3,64,640]{3,2,1,0:T(8,128)(2,1)S(1)} %get-tuple-element.28), channel_id=1, source_target_pairs={{0,1},{1,0},{2,3},{3,2},{4,5},{5,4},{6,7},{7,6},{8,9},{9,8},{10,11... | collective-permute-start | bytes 1474568 | tf_op jit(solution)/shard_map/ppermute | solution.py:189
  6.5 11.2 %collective-permute-start.5 = (bf16[3,3,3,64,512]{4,3,2,1,0:T(8,128)(2,1)}, bf16[3,3,3,64,512]{4,3,2,1,0:T(8,128)(2,1)S(1)}, u32[]{:S(2)}, u32[]{:S(2)}) collective-permute-start(bf16[3,3,3,64,512]{4,3,2,1,0:T(8,128)(2,1)} %refs_5_.3), channel_id=1, source_target_pairs={{0,1},{1,0},{2,3},{3,2},{4,5},{5,4},{6,7},{7,6},{8,9},{9,8},{10,11... | collective-permute-start | bytes 5308424 | tf_op jit(solution)/shard_map/ppermute | solution.py:189
  7.2 5.4 %collective-permute-start.4 = (bf16[2,3,64,640]{3,2,1,0:T(8,128)(2,1)S(1)}, bf16[2,3,64,640]{3,2,1,0:T(8,128)(2,1)S(1)}, u32[]{:S(2)}, u32[]{:S(2)}) collective-permute-start(bf16[2,3,64,640]{3,2,1,0:T(8,128)(2,1)S(1)} %pad_maximum_fusion.2), channel_id=1, source_target_pairs={{0,1},{1,0},{2,3},{3,2},{4,5},{5,4},{6,7},{7,6},{8,9},{9,8},{10,11... | collective-permute-start | bytes 1474568 | tf_op jit(solution)/shard_map/ppermute | solution.py:189
  7.5 10.1 %collective-permute-start.3 = (bf16[2,3,64,640]{3,2,1,0:T(8,128)(2,1)S(1)}, bf16[2,3,64,640]{3,2,1,0:T(8,128)(2,1)S(1)}, u32[]{:S(2)}, u32[]{:S(2)}) collective-permute-start(bf16[2,3,64,640]{3,2,1,0:T(8,128)(2,1)S(1)} %pad_maximum_fusion.1), channel_id=1, source_target_pairs={{9,1},{1,9},{11,3},{3,11},{13,5},{5,13},{15,7},{7,15},{16,8},{8,16... | collective-permute-start | bytes 1474568 | tf_op jit(solution)/shard_map/ppermute | solution.py:189
  11.0 10.7 %collective-permute-start.1 = (bf16[2,3,64,640]{3,2,1,0:T(8,128)(2,1)S(1)}, bf16[2,3,64,640]{3,2,1,0:T(8,128)(2,1)S(1)}, u32[]{:S(2)}, u32[]{:S(2)}) collective-permute-start(bf16[2,3,64,640]{3,2,1,0:T(8,128)(2,1)S(1)} %get-tuple-element.44.refs_1_), channel_id=1, source_target_pairs={{0,2},{1,3},{2,4},{3,5},{4,6},{5,7},{6,0},{7,1},{8,10},{9,11},{10,... | collective-permute-start | bytes 1474568 | tf_op jit(solution)/shard_map/ppermute | solution.py:189
  11.3 10.5 %collective-permute-start.2 = (bf16[2,3,64,640]{3,2,1,0:T(8,128)(2,1)S(1)}, bf16[2,3,64,640]{3,2,1,0:T(8,128)(2,1)S(1)}, u32[]{:S(2)}, u32[]{:S(2)}) collective-permute-start(bf16[2,3,64,640]{3,2,1,0:T(8,128)(2,1)S(1)} %get-tuple-element.43.refs_2_), channel_id=1, source_target_pairs={{2,0},{3,1},{4,2},{5,3},{6,4},{7,5},{0,6},{1,7},{10,8},{11,9},{12,... | collective-permute-start | bytes 1474568 | tf_op jit(solution)/shard_map/ppermute | solution.py:189
  12.6 18.2 %collective-permute-start.10 = (bf16[2,3,64,640]{3,2,1,0:T(8,128)(2,1)S(1)}, bf16[2,3,64,640]{3,2,1,0:T(8,128)(2,1)S(1)}, u32[]{:S(2)}, u32[]{:S(2)}) collective-permute-start(bf16[2,3,64,640]{3,2,1,0:T(8,128)(2,1)S(1)} %get-tuple-element.44.refs_1_), channel_id=1, source_target_pairs={{2,0},{3,1},{4,2},{5,3},{6,4},{7,5},{0,6},{1,7},{10,8},{11,9},{12,... | collective-permute-start | bytes 1474568 | tf_op jit(solution)/shard_map/ppermute | solution.py:189
  17.5 13.3 %collective-permute-start.11 = (bf16[2,3,64,640]{3,2,1,0:T(8,128)(2,1)S(1)}, bf16[2,3,64,640]{3,2,1,0:T(8,128)(2,1)S(1)}, u32[]{:S(2)}, u32[]{:S(2)}) collective-permute-start(bf16[2,3,64,640]{3,2,1,0:T(8,128)(2,1)S(1)} %get-tuple-element.43.refs_2_), channel_id=1, source_target_pairs={{0,2},{1,3},{2,4},{3,5},{4,6},{5,7},{6,0},{7,1},{8,10},{9,11},{10,... | collective-permute-start | bytes 1474568 | tf_op jit(solution)/shard_map/ppermute | solution.py:189
  21.8 34.5 %collective-permute-start.6 = (bf16[2,3,64,640]{3,2,1,0:T(8,128)(2,1)S(1)}, bf16[2,3,64,640]{3,2,1,0:T(8,128)(2,1)S(1)}, u32[]{:S(2)}, u32[]{:S(2)}) collective-permute-start(bf16[2,3,64,640]{3,2,1,0:T(8,128)(2,1)S(1)} %collective-permute-done.1.refs_1_), channel_id=1, source_target_pairs={{0,2},{1,3},{2,4},{3,5},{4,6},{5,7},{6,0},{7,1},{8,10},{9,11},{10,... | collective-permute-start | bytes 1474568 | tf_op jit(solution)/shard_map/ppermute | solution.py:189
  23.1 33.3 %collective-permute-start.7 = (bf16[2,3,64,640]{3,2,1,0:T(8,128)(2,1)S(1)}, bf16[2,3,64,640]{3,2,1,0:T(8,128)(2,1)S(1)}, u32[]{:S(2)}, u32[]{:S(2)}) collective-permute-start(bf16[2,3,64,640]{3,2,1,0:T(8,128)(2,1)S(1)} %collective-permute-done.2.refs_2_), channel_id=1, source_target_pairs={{2,0},{3,1},{4,2},{5,3},{6,4},{7,5},{0,6},{1,7},{10,8},{11,9},{12,... | collective-permute-start | bytes 1474568 | tf_op jit(solution)/shard_map/ppermute | solution.py:189
  30.9 13.8 %collective-permute-start.9 = (bf16[2,3,64,640]{3,2,1,0:T(8,128)(2,1)S(1)}, bf16[2,3,64,640]{3,2,1,0:T(8,128)(2,1)S(1)}, u32[]{:S(2)}, u32[]{:S(2)}) collective-permute-start(bf16[2,3,64,640]{3,2,1,0:T(8,128)(2,1)S(1)} %pad_maximum_fusion.4), channel_id=1, source_target_pairs={{0,1},{1,0},{2,3},{3,2},{4,5},{5,4},{6,7},{7,6},{8,9},{9,8},{10,11... | collective-permute-start | bytes 1474568 | tf_op jit(solution)/shard_map/ppermute | solution.py:189
  42.2 9.9 %collective-permute-start.8 = (bf16[2,3,64,640]{3,2,1,0:T(8,128)(2,1)S(1)}, bf16[2,3,64,640]{3,2,1,0:T(8,128)(2,1)S(1)}, u32[]{:S(2)}, u32[]{:S(2)}) collective-permute-start(bf16[2,3,64,640]{3,2,1,0:T(8,128)(2,1)S(1)} %pad_maximum_fusion.3), channel_id=1, source_target_pairs={{9,1},{1,9},{11,3},{3,11},{13,5},{5,13},{15,7},{7,15},{16,8},{8,16... | collective-permute-start | bytes 1474568 | tf_op jit(solution)/shard_map/ppermute | solution.py:189
  44.3 18.6 %collective-permute-start.15 = (bf16[2,3,64,640]{3,2,1,0:T(8,128)(2,1)S(1)}, bf16[2,3,64,640]{3,2,1,0:T(8,128)(2,1)S(1)}, u32[]{:S(2)}, u32[]{:S(2)}) collective-permute-start(bf16[2,3,64,640]{3,2,1,0:T(8,128)(2,1)S(1)} %pad_maximum_fusion.8), channel_id=1, source_target_pairs={{0,1},{1,0},{2,3},{3,2},{4,5},{5,4},{6,7},{7,6},{8,9},{9,8},{10,11... | collective-permute-start | bytes 1474568 | tf_op jit(solution)/shard_map/ppermute | solution.py:189
  44.7 18.1 %collective-permute-start.14 = (bf16[2,3,64,640]{3,2,1,0:T(8,128)(2,1)S(1)}, bf16[2,3,64,640]{3,2,1,0:T(8,128)(2,1)S(1)}, u32[]{:S(2)}, u32[]{:S(2)}) collective-permute-start(bf16[2,3,64,640]{3,2,1,0:T(8,128)(2,1)S(1)} %pad_maximum_fusion.7), channel_id=1, source_target_pairs={{9,1},{1,9},{11,3},{3,11},{13,5},{5,13},{15,7},{7,15},{16,8},{8,16... | collective-permute-start | bytes 1474568 | tf_op jit(solution)/shard_map/ppermute | solution.py:189
  56.3 5.3 %copy-start.3 = (f32[64]{0:T(128)S(1)}, f32[64]{0:T(128)}, u32[]{:S(2)}) copy-start(f32[64]{0:T(128)} %param.7) | copy-start | bytes 772
  56.5 10.5 %collective-permute-start.13 = (bf16[2,3,64,640]{3,2,1,0:T(8,128)(2,1)S(1)}, bf16[2,3,64,640]{3,2,1,0:T(8,128)(2,1)S(1)}, u32[]{:S(2)}, u32[]{:S(2)}) collective-permute-start(bf16[2,3,64,640]{3,2,1,0:T(8,128)(2,1)S(1)} %pad_maximum_fusion.6), channel_id=1, source_target_pairs={{0,1},{1,0},{2,3},{3,2},{4,5},{5,4},{6,7},{7,6},{8,9},{9,8},{10,11... | collective-permute-start | bytes 1474568 | tf_op jit(solution)/shard_map/ppermute | solution.py:189
  59.6 9.9 %collective-permute-start.12 = (bf16[2,3,64,640]{3,2,1,0:T(8,128)(2,1)S(1)}, bf16[2,3,64,640]{3,2,1,0:T(8,128)(2,1)S(1)}, u32[]{:S(2)}, u32[]{:S(2)}) collective-permute-start(bf16[2,3,64,640]{3,2,1,0:T(8,128)(2,1)S(1)} %pad_maximum_fusion.5), channel_id=1, source_target_pairs={{9,1},{1,9},{11,3},{3,11},{13,5},{5,13},{15,7},{7,15},{16,8},{8,16... | collective-permute-start | bytes 1474568 | tf_op jit(solution)/shard_map/ppermute | solution.py:189
  61.6 1.2 %collective-permute-start.16 = (f32[64]{0:T(128)S(1)}, f32[64]{0:T(128)S(1)}, u32[]{:S(2)}, u32[]{:S(2)}) collective-permute-start(f32[64]{0:T(128)S(1)} %copy-done.3), channel_id=1, source_target_pairs={{0,1},{1,0},{2,3},{3,2},{4,5},{5,4},{6,7},{7,6},{8,9},{9,8},{10,11... | collective-permute-start | bytes 776 | tf_op jit(solution)/shard_map/ppermute | solution.py:189
  73.7 4.3 %collective-permute-start.17 = (bf16[2,2,64,640]{3,2,1,0:T(8,128)(2,1)S(1)}, bf16[2,2,64,640]{3,2,1,0:T(8,128)(2,1)S(1)}, u32[]{:S(2)}, u32[]{:S(2)}) collective-permute-start(bf16[2,2,64,640]{3,2,1,0:T(8,128)(2,1)S(1)} %get-tuple-element.42), channel_id=1, source_target_pairs={{0,1},{1,0},{2,3},{3,2},{4,5},{5,4},{6,7},{7,6},{8,9},{9,8},{10,11... | collective-permute-start | bytes 983048 | tf_op jit(solution)/shard_map/ppermute | solution.py:189

commit v2 on v1

--- a/solution.py
+++ b/solution.py
@@ -53,10 +53,12 @@
     )(flip, cached, new)
 
 
-def block_kernel(blocks, first, last, *refs):
+def block_kernel(blocks, part, first, last, *refs):
     scalars, refs = refs[0], list(refs[1:])
-    bodies = [refs.pop(0), refs.pop(0)]
-    zsides, csides = refs.pop(0), refs.pop(0)
+    bodies = None if part == "z" else [refs.pop(0), refs.pop(0)]
+    zsides = None if part == "main" else refs.pop(0)
+    csides = None if part == "z" else refs.pop(0)
+    held = {"all": range(4), "main": range(1, 4), "z": range(1)}[part]
     weights = [refs.pop(0), refs.pop(0)]
     before = None if first else refs.pop(0)
     bias = refs.pop(0) if last else None
@@ -81,7 +83,7 @@
                 lambda q: bodies[piece][1, q],
                 lambda q: csides[piece, q],
             ]
-            for row in range(4):
+            for row in held:
                 low, high = rows[row](p), rows[row](p + 1)
                 xs[0, row, at] = low
                 xs[2, row, at] = high
@@ -100,19 +102,19 @@
                         w = jnp.where(jnp.broadcast_to(from_first, w.shape), w, v)
                     halves.append(w)
                 taps.append(jnp.concatenate(halves, axis=0))
-        lhs = jnp.concatenate(taps, axis=1)
-        rows = lhs.shape[0] // 6
+        rows = taps[0].shape[0] // 6
         lane = lax.broadcasted_iota(jnp.int32, (rows, width), 1)
         zero = jnp.zeros((rows, width), F32)
         left_edge = (lane == 0) | (lane == cols)
         right_edge = (lane == cols - 1) | (lane == width - 1)
         for row in range(2):
-            window = jnp.concatenate(
-                [xs[t, row : row + 3].reshape(3 * LANES, width) for t in range(3)], axis=0
-            )
-            acc = jnp.dot(lhs, window, preferred_element_type=F32)
-            if not first:
-                acc = acc + before[p, row]
+            acc = None if first else before[p, row]
+            at = [(t, delta) for t in range(3) for delta in range(3) if row + delta in held]
+            if at:
+                lhs = jnp.concatenate([taps[3 * t + delta] for t, delta in at], axis=1)
+                window = jnp.concatenate([xs[t, row + delta] for t, delta in at], axis=0)
+                product = jnp.dot(lhs, window, preferred_element_type=F32)
+                acc = product if first else acc + product
             if not last:
                 outs[0][p, row] = acc
                 continue
@@ -127,13 +129,19 @@
     lax.fori_loop(0, 2, one_pair, 0)
 
 
-def block_call(scalars, blocks, bodies, zsides, csides, weights, before, bias):
+def block_call(scalars, blocks, part, bodies, zsides, csides, weights, before, bias):
     first, last = before is None, bias is not None
     own, other = weights
     outs64 = own.shape[3]
     rows = 2 * 3 * outs64
-    width = bodies[0].shape[-1]
-    operands = [*bodies, zsides, csides, own, other]
+    width = (bodies[0] if part != "z" else zsides).shape[-1]
+    operands = [own, other]
+    if part != "z":
+        operands.insert(0, csides)
+    if part != "main":
+        operands.insert(0, zsides)
+    if part != "z":
+        operands = [*bodies, *operands]
     aliases = {}
     if not first:
         operands.append(before)
@@ -146,7 +154,7 @@
             aliases = {len(operands): 0}
     vmem = pl.BlockSpec(memory_space=pltpu.VMEM)
     result = pl.pallas_call(
-        functools.partial(block_kernel, blocks, first, last),
+        functools.partial(block_kernel, blocks, part, first, last),
         in_specs=[pl.BlockSpec(memory_space=pltpu.SMEM)] + [vmem] * len(operands),
         out_specs=[vmem] * len(out_shape),
         scratch_shapes=[pltpu.VMEM((3, 4, LANES, width), BF)],
@@ -172,8 +180,8 @@
             here, there = b * chans + 2 * x + b % 2, (b - 1) * chans + 2 * x + b % 2
             across += [(here, there), (there, here)]
     for x in range(chips):
-        for own in (2 * x, (bands - 1) * chans + 2 * x + bands % 2):
-            across += [(own, own)]
+        here, there = 2 * x, (bands - 1) * chans + 2 * x + bands % 2
+        across += [(here, there), (there, here)]
 
     def on_device(new_frames, cached_frames, conv_weight, out_bias):
         cols = new_frames.shape[-1]
@@ -207,15 +215,14 @@
         r_lo = send(lo, left)
         weights = (conv_weight, other_weight)
 
-        acc = block_call(scalars, OWN, (lo, hi), *halos(lo, hi), weights, None, None)
-        l_lo, r_hi, acc = lax.optimization_barrier((l_lo, r_hi, acc))
+        acc = block_call(scalars, OWN, "all", (lo, hi), *halos(lo, hi), weights, None, None)
         f_lo = send(l_lo, right)
         f_hi = send(r_hi, left)
-        r_lo, l_hi, acc = lax.optimization_barrier((r_lo, l_hi, acc))
-        acc = block_call(scalars, LEFT_RIGHT, (l_lo, r_hi), *halos(l_lo, r_hi), weights, acc, None)
-        f_lo, f_hi, acc = lax.optimization_barrier((f_lo, f_hi, acc))
-        acc = block_call(scalars, RIGHT_LEFT, (r_lo, l_hi), *halos(r_lo, l_hi), weights, acc, None)
-        mine, theirs = block_call(scalars, FAR, (f_lo, f_hi), *halos(f_lo, f_hi), weights, acc, biases)
+        acc = block_call(scalars, LEFT_RIGHT, "all", (l_lo, r_hi), *halos(l_lo, r_hi), weights, acc, None)
+        acc = block_call(scalars, RIGHT_LEFT, "all", (r_lo, l_hi), *halos(r_lo, l_hi), weights, acc, None)
+        far_z, far_c = halos(f_lo, f_hi)
+        acc = block_call(scalars, FAR, "main", (f_lo, f_hi), None, far_c, weights, acc, None)
+        mine, theirs = block_call(scalars, FAR, "z", None, far_z, None, weights, acc, biases)
         given = send(theirs, swap)
 
         def row(a, r):

time: 80 us -> 85.7 us (1.071)
  the two profiles are of different devices: /device:TPU:31 before, /device:TPU:1 now
where the time goes in v2:
time: 85.7 us; the launch traced here: 85.5 us
  starting transfers between devices  31.2 us (36%)
  waiting for transfers between devices  29 us (34%)
  Pallas kernels  20 us (23%)
  local copies, waits for them, and re-layouts  4.06 us (5%)
  other arithmetic  0.92 us (1%)
    ppermute x18, starting transfers between devices, send(): return lax.ppermute(a, axes, pairs)  31.2 us
    ppermute x18, waiting for transfers between devices, send(): return lax.ppermute(a, axes, pairs)  29 us
    pallas_call x5, Pallas kernels, block_call(): pl.pallas_call(functools.partial(block_kernel, blocks, part, first, last)...  18 us
    unnamed x8, local copies, waits for them, and re-layouts  2.14 us
    pallas_call x1, Pallas kernels, pack(): pl.pallas_call(pack_kernel, in_specs=[pl.BlockSpec(memory_space=pltpu.SME...  1.94 us
  transfers between devices with their start and end apart: 18, of which 6 were waited for; matrix products, arithmetic and copies ran while one was open for 1% of the time, Pallas kernels for 19%

profile of v2, /device:TPU:1, one launch (start us, length us, event | category | flops | bytes accessed | tf_op | source)
XLA Modules:
  0.0 85.5 jit_solution(858996785874185403)
XLA Ops:
  0.0 0.0 copy-start.3
  0.0 0.1 stack.107.flip_ref.refs_0_
  0.1 1.1 %copy-done.1 = bf16[4,4,64,320]{3,2,1,0:T(8,128)(2,1)S(1)} copy-done((bf16[4,4,64,320]{3,2,1,0:T(8,128)(2,1)S(1)}, bf16[4,4,64,320]{3,2,1,0:T(8,128)(2,1)}, u32[]{:S(2)}) %copy-start.1) | copy-done | bytes 655384
  1.2 1.0 %copy-done.2 = bf16[2,4,64,320]{3,2,1,0:T(8,128)(2,1)S(1)} copy-done((bf16[2,4,64,320]{3,2,1,0:T(8,128)(2,1)S(1)}, bf16[2,4,64,320]{3,2,1,0:T(8,128)(2,1)}, u32[]{:S(2)}) %copy-start.2) | copy-done | bytes 327704
  2.2 1.9 %pack.1 = (bf16[2,3,64,640]{3,2,1,0:T(8,128)(2,1)S(1)}, bf16[2,3,64,640]{3,2,1,0:T(8,128)(2,1)S(1)}) custom-call(s32[6]{0:T(128)S(1)} %stack.107.flip_ref.refs_0_, bf16[2,4,64,320]{3,2,1,0:T(8,128)(2,1)S(1)} %copy-done.2, bf16[4,4,64,320]{3,2,1,0:T(8,128)(2,1)S(1)} %copy-done.1), custom_call_target="tpu_custom_call" | custom-call | flops 100000000 | bytes 4194304 | tf_op jit(solution)/shard_map/pack/pallas_call | solution.py:45
  4.2 3.3 %collective-permute-start = (bf16[2,3,64,640]{3,2,1,0:T(8,128)(2,1)S(1)}, bf16[2,3,64,640]{3,2,1,0:T(8,128)(2,1)S(1)}, u32[]{:S(2)}, u32[]{:S(2)}) collective-permute-start(bf16[2,3,64,640]{3,2,1,0:T(8,128)(2,1)S(1)} %get-tuple-element.19), channel_id=1, source_target_pairs={{0,1},{1,0},{2,3},{3,2},{4,5},{5,4},{6,7},{7,6},{8,9},{9,8},{10,11... | collective-permute-start | bytes 1474568 | tf_op jit(solution)/shard_map/ppermute | solution.py:197
  7.5 1.5 %collective-permute-done = bf16[2,3,64,640]{3,2,1,0:T(8,128)(2,1)S(1)} collective-permute-done((bf16[2,3,64,640]{3,2,1,0:T(8,128)(2,1)S(1)}, bf16[2,3,64,640]{3,2,1,0:T(8,128)(2,1)S(1)}, u32[]{:S(2)}, u32[]{:S(2)}) %collective-permute-start) | collective-permute-done | bytes 491552 | tf_op jit(solution)/shard_map/ppermute | solution.py:197
  8.9 0.1 broadcast_select_fusion.1
  9.1 0.1 collective-permute-start.1
  9.2 2.7 %collective-permute-start.8 = (bf16[2,3,64,640]{3,2,1,0:T(8,128)(2,1)S(1)}, bf16[2,3,64,640]{3,2,1,0:T(8,128)(2,1)S(1)}, u32[]{:S(2)}, u32[]{:S(2)}) collective-permute-start(bf16[2,3,64,640]{3,2,1,0:T(8,128)(2,1)S(1)} %get-tuple-element.25.refs_1_), channel_id=1, source_target_pairs={{2,0},{3,1},{4,2},{5,3},{6,4},{7,5},{0,6},{1,7},{10,8},{11,9},{12,... | collective-permute-start | bytes 1474568 | tf_op jit(solution)/shard_map/ppermute | solution.py:197
  11.9 0.0 collective-permute-start.3
  11.9 1.4 %collective-permute-start.9 = (bf16[2,3,64,640]{3,2,1,0:T(8,128)(2,1)S(1)}, bf16[2,3,64,640]{3,2,1,0:T(8,128)(2,1)S(1)}, u32[]{:S(2)}, u32[]{:S(2)}) collective-permute-start(bf16[2,3,64,640]{3,2,1,0:T(8,128)(2,1)S(1)} %get-tuple-element.26.refs_2_), channel_id=1, source_target_pairs={{0,2},{1,3},{2,4},{3,5},{4,6},{5,7},{6,0},{7,1},{8,10},{9,11},{10,... | collective-permute-start | bytes 1474568 | tf_op jit(solution)/shard_map/ppermute | solution.py:197
  13.3 0.0 copy-done.3
  13.3 1.5 %collective-permute-start.16 = (f32[64]{0:T(128)S(1)}, f32[64]{0:T(128)S(1)}, u32[]{:S(2)}, u32[]{:S(2)}) collective-permute-start(f32[64]{0:T(128)S(1)} %copy-done.3), channel_id=1, source_target_pairs={{0,1},{1,0},{2,3},{3,2},{4,5},{5,4},{6,7},{7,6},{8,9},{9,8},{10,11... | collective-permute-start | bytes 776 | tf_op jit(solution)/shard_map/ppermute | solution.py:197
  14.9 0.1 pad_maximum_fusion.7
  14.9 0.1 pad_maximum_fusion.8
  15.0 0.6 collective-permute-done.16
  15.6 0.0 collective-permute-start.14
  15.7 7.1 %collective-permute-done.1.refs_1_ = bf16[2,3,64,640]{3,2,1,0:T(8,128)(2,1)S(1)} collective-permute-done((bf16[2,3,64,640]{3,2,1,0:T(8,128)(2,1)S(1)}, bf16[2,3,64,640]{3,2,1,0:T(8,128)(2,1)S(1)}, u32[]{:S(2)}, u32[]{:S(2)}) %collective-permute-start.1) | collective-permute-done | bytes 491552 | tf_op jit(solution)/shard_map/ppermute | solution.py:197
  22.8 2.1 %collective-permute-start.15 = (bf16[2,3,64,640]{3,2,1,0:T(8,128)(2,1)S(1)}, bf16[2,3,64,640]{3,2,1,0:T(8,128)(2,1)S(1)}, u32[]{:S(2)}, u32[]{:S(2)}) collective-permute-start(bf16[2,3,64,640]{3,2,1,0:T(8,128)(2,1)S(1)} %pad_maximum_fusion.8), channel_id=1, source_target_pairs={{0,1},{1,0},{2,3},{3,2},{4,5},{5,4},{6,7},{7,6},{8,9},{9,8},{10,11... | collective-permute-start | bytes 1474568 | tf_op jit(solution)/shard_map/ppermute | solution.py:197
  24.9 7.4 %collective-permute-done.3.refs_2_ = bf16[2,3,64,640]{3,2,1,0:T(8,128)(2,1)S(1)} collective-permute-done((bf16[2,3,64,640]{3,2,1,0:T(8,128)(2,1)S(1)}, bf16[2,3,64,640]{3,2,1,0:T(8,128)(2,1)S(1)}, u32[]{:S(2)}, u32[]{:S(2)}) %collective-permute-start.3) | collective-permute-done | bytes 491552 | tf_op jit(solution)/shard_map/ppermute | solution.py:197
  32.3 0.0 copy-done
  32.3 1.5 %collective-permute-start.6 = (bf16[3,3,3,64,512]{4,3,2,1,0:T(8,128)(2,1)S(1)}, bf16[3,3,3,64,512]{4,3,2,1,0:T(8,128)(2,1)S(1)}, u32[]{:S(2)}, u32[]{:S(2)}) collective-permute-start(bf16[3,3,3,64,512]{4,3,2,1,0:T(8,128)(2,1)S(1)} %copy-done), channel_id=1, source_target_pairs={{0,1},{1,0},{2,3},{3,2},{4,5},{5,4},{6,7},{7,6},{8,9},{9,8},{10,11... | collective-permute-start | bytes 5308424 | tf_op jit(solution)/shard_map/ppermute | solution.py:197
  33.9 0.1 pad_maximum_fusion.5
  34.0 0.1 pad_maximum_fusion.6
  34.0 0.0 collective-permute-done.8.refs_1_
  34.0 0.3 collective-permute-start.2
  34.4 0.0 collective-permute-done.9.refs_2_
  34.4 3.3 %collective-permute-start.4 = (bf16[2,3,64,640]{3,2,1,0:T(8,128)(2,1)S(1)}, bf16[2,3,64,640]{3,2,1,0:T(8,128)(2,1)S(1)}, u32[]{:S(2)}, u32[]{:S(2)}) collective-permute-start(bf16[2,3,64,640]{3,2,1,0:T(8,128)(2,1)S(1)} %collective-permute-done.3.refs_2_), channel_id=1, source_target_pairs={{2,0},{3,1},{4,2},{5,3},{6,4},{7,5},{0,6},{1,7},{10,8},{11,9},{12,... | collective-permute-start | bytes 1474568 | tf_op jit(solution)/shard_map/ppermute | solution.py:197
  37.7 0.1 pad_maximum_fusion.3
  37.8 0.1 pad_maximum_fusion.4
  37.8 11.3 %collective-permute-done.2.refs_1_ = bf16[2,3,64,640]{3,2,1,0:T(8,128)(2,1)S(1)} collective-permute-done((bf16[2,3,64,640]{3,2,1,0:T(8,128)(2,1)S(1)}, bf16[2,3,64,640]{3,2,1,0:T(8,128)(2,1)S(1)}, u32[]{:S(2)}, u32[]{:S(2)}) %collective-permute-start.2) | collective-permute-done | bytes 491552 | tf_op jit(solution)/shard_map/ppermute | solution.py:197
  49.1 0.0 collective-permute-start.12
  49.2 0.0 collective-permute-done.4.refs_2_
  49.2 7.3 %collective-permute-start.13 = (bf16[2,3,64,640]{3,2,1,0:T(8,128)(2,1)S(1)}, bf16[2,3,64,640]{3,2,1,0:T(8,128)(2,1)S(1)}, u32[]{:S(2)}, u32[]{:S(2)}) collective-permute-start(bf16[2,3,64,640]{3,2,1,0:T(8,128)(2,1)S(1)} %pad_maximum_fusion.6), channel_id=1, source_target_pairs={{0,1},{1,0},{2,3},{3,2},{4,5},{5,4},{6,7},{7,6},{8,9},{9,8},{10,11... | collective-permute-start | bytes 1474568 | tf_op jit(solution)/shard_map/ppermute | solution.py:197
  56.5 0.1 pad_maximum_fusion.2
  56.6 0.0 collective-permute-done.14.refs_3_
  56.6 0.1 collective-permute-start.10
  56.7 0.0 collective-permute-done.15.refs_4_
  56.7 0.4 collective-permute-start.11
  57.1 0.1 pad_maximum_fusion.1
  57.1 0.0 collective-permute-done.6.refs_6_.refs_5_.refs_3_
  57.1 0.5 collective-permute-start.7
  57.6 4.1 %shard_map.46.refs_7_ = f32[2,2,384,640]{3,2,1,0:T(8,128)S(1)} custom-call(s32[6]{0:T(128)S(1)} %stack.107.flip_ref.refs_0_, bf16[2,3,64,640]{3,2,1,0:T(8,128)(2,1)S(1)} %get-tuple-element.25.refs_1_, bf16[2,3,64,640]{3,2,1,0:T(8,128)(2,1)S(1)} %get-tuple-element.26.refs_2_, bf16[2,3,64,640]{3,2,1,0:T(8,128)(2,1)S(1)} %collective-permute-done.14.refs_3_, ...), custom_call_target="tpu_custom_call" | custom-call | flops 2264924160 | bytes 8388608 | tf_op jit(solution)/shard_map/pallas_call | solution.py:156
  61.7 0.0 collective-permute-done.12.refs_3_
  61.7 1.4 %collective-permute-start.5 = (bf16[2,3,64,640]{3,2,1,0:T(8,128)(2,1)S(1)}, bf16[2,3,64,640]{3,2,1,0:T(8,128)(2,1)S(1)}, u32[]{:S(2)}, u32[]{:S(2)}) collective-permute-start(bf16[2,3,64,640]{3,2,1,0:T(8,128)(2,1)S(1)} %pad_maximum_fusion.1), channel_id=1, source_target_pairs={{9,1},{1,9},{11,3},{3,11},{13,5},{5,13},{15,7},{7,15},{16,8},{8,16... | collective-permute-start | bytes 1474568 | tf_op jit(solution)/shard_map/ppermute | solution.py:197
  63.1 0.0 collective-permute-done.13.refs_4_
  63.1 4.2 %shard_map.47.refs_7_ = f32[2,2,384,640]{3,2,1,0:T(8,128)S(1)} custom-call(s32[6]{0:T(128)S(1)} %stack.107.flip_ref.refs_0_, bf16[2,3,64,640]{3,2,1,0:T(8,128)(2,1)S(1)} %collective-permute-done.1.refs_1_, bf16[2,3,64,640]{3,2,1,0:T(8,128)(2,1)S(1)} %collective-permute-done.3.refs_2_, ...), custom_call_target="tpu_custom_call", output_to_operand_aliasing={{}: (7, {})} | custom-call | flops 2264924160 | bytes 8388608 | tf_op jit(solution)/shard_map/pallas_call | solution.py:156
  67.3 0.0 collective-permute-done.10.refs_3_
  67.3 0.0 collective-permute-done.11.refs_4_
  67.3 4.2 %shard_map.48.refs_6_ = f32[2,2,384,640]{3,2,1,0:T(8,128)S(1)} custom-call(s32[6]{0:T(128)S(1)} %stack.107.flip_ref.refs_0_, bf16[2,3,64,640]{3,2,1,0:T(8,128)(2,1)S(1)} %collective-permute-done.8.refs_1_, bf16[2,3,64,640]{3,2,1,0:T(8,128)(2,1)S(1)} %collective-permute-done.9.refs_2_, ...), custom_call_target="tpu_custom_call", output_to_operand_aliasing={{}: (7, {})} | custom-call | flops 2264924160 | bytes 8388608 | tf_op jit(solution)/shard_map/pallas_call | solution.py:156
  71.6 0.0 collective-permute-done.7.refs_3_
  71.6 3.7 %shard_map.49.refs_4_ = f32[2,2,384,640]{3,2,1,0:T(8,128)S(1)} custom-call(s32[6]{0:T(128)S(1)} %stack.107.flip_ref.refs_0_, bf16[2,3,64,640]{3,2,1,0:T(8,128)(2,1)S(1)} %collective-permute-done.2.refs_1_, bf16[2,3,64,640]{3,2,1,0:T(8,128)(2,1)S(1)} %collective-permute-done.4.refs_2_, ...), custom_call_target="tpu_custom_call", output_to_operand_aliasing={{}: (6, {})} | custom-call | flops 2264924160 | bytes 8388608 | tf_op jit(solution)/shard_map/pallas_call | solution.py:156
  75.3 0.0 collective-permute-done.5.refs_1_
  75.3 1.9 %shard_map.50 = (bf16[2,2,64,640]{3,2,1,0:T(8,128)(2,1)S(1)}, bf16[2,2,64,640]{3,2,1,0:T(8,128)(2,1)S(1)}) custom-call(s32[6]{0:T(128)S(1)} %stack.107.flip_ref.refs_0_, bf16[2,3,64,640]{3,2,1,0:T(8,128)(2,1)S(1)} %collective-permute-done.5.refs_1_, bf16[3,3,3,64,512]{4,3,2,1,0:T(8,128)(2,1)S(1)} %copy-done, ...), custom_call_target="tpu_custom_call" | custom-call | flops 2264924160 | bytes 8388608 | tf_op jit(solution)/shard_map/pallas_call | solution.py:156
  77.2 5.4 %collective-permute-start.17 = (bf16[2,2,64,640]{3,2,1,0:T(8,128)(2,1)S(1)}, bf16[2,2,64,640]{3,2,1,0:T(8,128)(2,1)S(1)}, u32[]{:S(2)}, u32[]{:S(2)}) collective-permute-start(bf16[2,2,64,640]{3,2,1,0:T(8,128)(2,1)S(1)} %get-tuple-element.24), channel_id=1, source_target_pairs={{0,1},{1,0},{2,3},{3,2},{4,5},{5,4},{6,7},{7,6},{8,9},{9,8},{10,11... | collective-permute-start | bytes 983048 | tf_op jit(solution)/shard_map/ppermute | solution.py:197
  82.6 0.1 slice_bitcast_fusion.7
  82.7 0.1 slice_bitcast_fusion.11
  82.8 1.0 %collective-permute-done.17 = bf16[2,2,64,640]{3,2,1,0:T(8,128)(2,1)S(1)} collective-permute-done((bf16[2,2,64,640]{3,2,1,0:T(8,128)(2,1)S(1)}, bf16[2,2,64,640]{3,2,1,0:T(8,128)(2,1)S(1)}, u32[]{:S(2)}, u32[]{:S(2)}) %collective-permute-start.17) | collective-permute-done | bytes 327712 | tf_op jit(solution)/shard_map/ppermute | solution.py:197
  83.9 0.1 slice_bitcast_fusion.5
  84.0 0.1 slice_bitcast_fusion.9
  84.1 0.2 broadcast_select_fusion.4
  84.4 0.2 pad_maximum_fusion
  84.6 1.0 %copy.18 = bf16[4,4,64,320]{3,2,1,0:T(8,128)(2,1)} copy(bf16[4,4,64,320]{3,2,0,1:T(8,128)(2,1)S(1)} %pad_maximum_fusion) | data formatting | bytes 1310720 | tf_op jit(solution)/shard_map/stack | solution.py:233
  (18 shorter events, 0.5 us)
Async XLA Ops:
  0.0 13.3 %copy-start.3 = (f32[64]{0:T(128)S(1)}, f32[64]{0:T(128)}, u32[]{:S(2)}) copy-start(f32[64]{0:T(128)} %param.7) | copy-start | bytes 772
  0.1 1.1 %copy-start.1 = (bf16[4,4,64,320]{3,2,1,0:T(8,128)(2,1)S(1)}, bf16[4,4,64,320]{3,2,1,0:T(8,128)(2,1)}, u32[]{:S(2)}) copy-start(bf16[4,4,64,320]{3,2,1,0:T(8,128)(2,1)} %new_ref.1) | copy-start | bytes 1966084
  1.2 1.0 %copy-start.2 = (bf16[2,4,64,320]{3,2,1,0:T(8,128)(2,1)S(1)}, bf16[2,4,64,320]{3,2,1,0:T(8,128)(2,1)}, u32[]{:S(2)}) copy-start(bf16[2,4,64,320]{3,2,1,0:T(8,128)(2,1)} %cached_ref.1) | copy-start | bytes 983044
  2.2 30.1 %copy-start = (bf16[3,3,3,64,512]{4,3,2,1,0:T(8,128)(2,1)S(1)}, bf16[3,3,3,64,512]{4,3,2,1,0:T(8,128)(2,1)}, u32[]{:S(2)}) copy-start(bf16[3,3,3,64,512]{4,3,2,1,0:T(8,128)(2,1)} %refs_2_) | copy-start | bytes 5308420
  4.2 4.8 %collective-permute-start = (bf16[2,3,64,640]{3,2,1,0:T(8,128)(2,1)S(1)}, bf16[2,3,64,640]{3,2,1,0:T(8,128)(2,1)S(1)}, u32[]{:S(2)}, u32[]{:S(2)}) collective-permute-start(bf16[2,3,64,640]{3,2,1,0:T(8,128)(2,1)S(1)} %get-tuple-element.19), channel_id=1, source_target_pairs={{0,1},{1,0},{2,3},{3,2},{4,5},{5,4},{6,7},{7,6},{8,9},{9,8},{10,11... | collective-permute-start | bytes 1474568 | tf_op jit(solution)/shard_map/ppermute | solution.py:197
  9.1 13.7 %collective-permute-start.1 = (bf16[2,3,64,640]{3,2,1,0:T(8,128)(2,1)S(1)}, bf16[2,3,64,640]{3,2,1,0:T(8,128)(2,1)S(1)}, u32[]{:S(2)}, u32[]{:S(2)}) collective-permute-start(bf16[2,3,64,640]{3,2,1,0:T(8,128)(2,1)S(1)} %get-tuple-element.25.refs_1_), channel_id=1, source_target_pairs={{0,2},{1,3},{2,4},{3,5},{4,6},{5,7},{6,0},{7,1},{8,10},{9,11},{10,... | collective-permute-start | bytes 1474568 | tf_op jit(solution)/shard_map/ppermute | solution.py:197
  9.2 24.8 %collective-permute-start.8 = (bf16[2,3,64,640]{3,2,1,0:T(8,128)(2,1)S(1)}, bf16[2,3,64,640]{3,2,1,0:T(8,128)(2,1)S(1)}, u32[]{:S(2)}, u32[]{:S(2)}) collective-permute-start(bf16[2,3,64,640]{3,2,1,0:T(8,128)(2,1)S(1)} %get-tuple-element.25.refs_1_), channel_id=1, source_target_pairs={{2,0},{3,1},{4,2},{5,3},{6,4},{7,5},{0,6},{1,7},{10,8},{11,9},{12,... | collective-permute-start | bytes 1474568 | tf_op jit(solution)/shard_map/ppermute | solution.py:197
  11.9 20.5 %collective-permute-start.3 = (bf16[2,3,64,640]{3,2,1,0:T(8,128)(2,1)S(1)}, bf16[2,3,64,640]{3,2,1,0:T(8,128)(2,1)S(1)}, u32[]{:S(2)}, u32[]{:S(2)}) collective-permute-start(bf16[2,3,64,640]{3,2,1,0:T(8,128)(2,1)S(1)} %get-tuple-element.26.refs_2_), channel_id=1, source_target_pairs={{2,0},{3,1},{4,2},{5,3},{6,4},{7,5},{0,6},{1,7},{10,8},{11,9},{12,... | collective-permute-start | bytes 1474568 | tf_op jit(solution)/shard_map/ppermute | solution.py:197
  11.9 22.5 %collective-permute-start.9 = (bf16[2,3,64,640]{3,2,1,0:T(8,128)(2,1)S(1)}, bf16[2,3,64,640]{3,2,1,0:T(8,128)(2,1)S(1)}, u32[]{:S(2)}, u32[]{:S(2)}) collective-permute-start(bf16[2,3,64,640]{3,2,1,0:T(8,128)(2,1)S(1)} %get-tuple-element.26.refs_2_), channel_id=1, source_target_pairs={{0,2},{1,3},{2,4},{3,5},{4,6},{5,7},{6,0},{7,1},{8,10},{9,11},{10,... | collective-permute-start | bytes 1474568 | tf_op jit(solution)/shard_map/ppermute | solution.py:197
  13.3 2.3 %collective-permute-start.16 = (f32[64]{0:T(128)S(1)}, f32[64]{0:T(128)S(1)}, u32[]{:S(2)}, u32[]{:S(2)}) collective-permute-start(f32[64]{0:T(128)S(1)} %copy-done.3), channel_id=1, source_target_pairs={{0,1},{1,0},{2,3},{3,2},{4,5},{5,4},{6,7},{7,6},{8,9},{9,8},{10,11... | collective-permute-start | bytes 776 | tf_op jit(solution)/shard_map/ppermute | solution.py:197
  15.6 40.9 %collective-permute-start.14 = (bf16[2,3,64,640]{3,2,1,0:T(8,128)(2,1)S(1)}, bf16[2,3,64,640]{3,2,1,0:T(8,128)(2,1)S(1)}, u32[]{:S(2)}, u32[]{:S(2)}) collective-permute-start(bf16[2,3,64,640]{3,2,1,0:T(8,128)(2,1)S(1)} %pad_maximum_fusion.7), channel_id=1, source_target_pairs={{9,1},{1,9},{11,3},{3,11},{13,5},{5,13},{15,7},{7,15},{16,8},{8,16... | collective-permute-start | bytes 1474568 | tf_op jit(solution)/shard_map/ppermute | solution.py:197
  22.8 33.9 %collective-permute-start.15 = (bf16[2,3,64,640]{3,2,1,0:T(8,128)(2,1)S(1)}, bf16[2,3,64,640]{3,2,1,0:T(8,128)(2,1)S(1)}, u32[]{:S(2)}, u32[]{:S(2)}) collective-permute-start(bf16[2,3,64,640]{3,2,1,0:T(8,128)(2,1)S(1)} %pad_maximum_fusion.8), channel_id=1, source_target_pairs={{0,1},{1,0},{2,3},{3,2},{4,5},{5,4},{6,7},{7,6},{8,9},{9,8},{10,11... | collective-permute-start | bytes 1474568 | tf_op jit(solution)/shard_map/ppermute | solution.py:197
  32.3 24.8 %collective-permute-start.6 = (bf16[3,3,3,64,512]{4,3,2,1,0:T(8,128)(2,1)S(1)}, bf16[3,3,3,64,512]{4,3,2,1,0:T(8,128)(2,1)S(1)}, u32[]{:S(2)}, u32[]{:S(2)}) collective-permute-start(bf16[3,3,3,64,512]{4,3,2,1,0:T(8,128)(2,1)S(1)} %copy-done), channel_id=1, source_target_pairs={{0,1},{1,0},{2,3},{3,2},{4,5},{5,4},{6,7},{7,6},{8,9},{9,8},{10,11... | collective-permute-start | bytes 5308424 | tf_op jit(solution)/shard_map/ppermute | solution.py:197
  34.0 15.1 %collective-permute-start.2 = (bf16[2,3,64,640]{3,2,1,0:T(8,128)(2,1)S(1)}, bf16[2,3,64,640]{3,2,1,0:T(8,128)(2,1)S(1)}, u32[]{:S(2)}, u32[]{:S(2)}) collective-permute-start(bf16[2,3,64,640]{3,2,1,0:T(8,128)(2,1)S(1)} %collective-permute-done.1.refs_1_), channel_id=1, source_target_pairs={{0,2},{1,3},{2,4},{3,5},{4,6},{5,7},{6,0},{7,1},{8,10},{9,11},{10,... | collective-permute-start | bytes 1474568 | tf_op jit(solution)/shard_map/ppermute | solution.py:197
  34.4 14.8 %collective-permute-start.4 = (bf16[2,3,64,640]{3,2,1,0:T(8,128)(2,1)S(1)}, bf16[2,3,64,640]{3,2,1,0:T(8,128)(2,1)S(1)}, u32[]{:S(2)}, u32[]{:S(2)}) collective-permute-start(bf16[2,3,64,640]{3,2,1,0:T(8,128)(2,1)S(1)} %collective-permute-done.3.refs_2_), channel_id=1, source_target_pairs={{2,0},{3,1},{4,2},{5,3},{6,4},{7,5},{0,6},{1,7},{10,8},{11,9},{12,... | collective-permute-start | bytes 1474568 | tf_op jit(solution)/shard_map/ppermute | solution.py:197
  49.1 12.6 %collective-permute-start.12 = (bf16[2,3,64,640]{3,2,1,0:T(8,128)(2,1)S(1)}, bf16[2,3,64,640]{3,2,1,0:T(8,128)(2,1)S(1)}, u32[]{:S(2)}, u32[]{:S(2)}) collective-permute-start(bf16[2,3,64,640]{3,2,1,0:T(8,128)(2,1)S(1)} %pad_maximum_fusion.5), channel_id=1, source_target_pairs={{9,1},{1,9},{11,3},{3,11},{13,5},{5,13},{15,7},{7,15},{16,8},{8,16... | collective-permute-start | bytes 1474568 | tf_op jit(solution)/shard_map/ppermute | solution.py:197
  49.2 14.0 %collective-permute-start.13 = (bf16[2,3,64,640]{3,2,1,0:T(8,128)(2,1)S(1)}, bf16[2,3,64,640]{3,2,1,0:T(8,128)(2,1)S(1)}, u32[]{:S(2)}, u32[]{:S(2)}) collective-permute-start(bf16[2,3,64,640]{3,2,1,0:T(8,128)(2,1)S(1)} %pad_maximum_fusion.6), channel_id=1, source_target_pairs={{0,1},{1,0},{2,3},{3,2},{4,5},{5,4},{6,7},{7,6},{8,9},{9,8},{10,11... | collective-permute-start | bytes 1474568 | tf_op jit(solution)/shard_map/ppermute | solution.py:197
  56.6 10.8 %collective-permute-start.10 = (bf16[2,3,64,640]{3,2,1,0:T(8,128)(2,1)S(1)}, bf16[2,3,64,640]{3,2,1,0:T(8,128)(2,1)S(1)}, u32[]{:S(2)}, u32[]{:S(2)}) collective-permute-start(bf16[2,3,64,640]{3,2,1,0:T(8,128)(2,1)S(1)} %pad_maximum_fusion.3), channel_id=1, source_target_pairs={{9,1},{1,9},{11,3},{3,11},{13,5},{5,13},{15,7},{7,15},{16,8},{8,16... | collective-permute-start | bytes 1474568 | tf_op jit(solution)/shard_map/ppermute | solution.py:197
  56.7 10.7 %collective-permute-start.11 = (bf16[2,3,64,640]{3,2,1,0:T(8,128)(2,1)S(1)}, bf16[2,3,64,640]{3,2,1,0:T(8,128)(2,1)S(1)}, u32[]{:S(2)}, u32[]{:S(2)}) collective-permute-start(bf16[2,3,64,640]{3,2,1,0:T(8,128)(2,1)S(1)} %pad_maximum_fusion.4), channel_id=1, source_target_pairs={{0,1},{1,0},{2,3},{3,2},{4,5},{5,4},{6,7},{7,6},{8,9},{9,8},{10,11... | collective-permute-start | bytes 1474568 | tf_op jit(solution)/shard_map/ppermute | solution.py:197
  57.1 14.4 %collective-permute-start.7 = (bf16[2,3,64,640]{3,2,1,0:T(8,128)(2,1)S(1)}, bf16[2,3,64,640]{3,2,1,0:T(8,128)(2,1)S(1)}, u32[]{:S(2)}, u32[]{:S(2)}) collective-permute-start(bf16[2,3,64,640]{3,2,1,0:T(8,128)(2,1)S(1)} %pad_maximum_fusion.2), channel_id=1, source_target_pairs={{0,1},{1,0},{2,3},{3,2},{4,5},{5,4},{6,7},{7,6},{8,9},{9,8},{10,11... | collective-permute-start | bytes 1474568 | tf_op jit(solution)/shard_map/ppermute | solution.py:197
  61.7 13.6 %collective-permute-start.5 = (bf16[2,3,64,640]{3,2,1,0:T(8,128)(2,1)S(1)}, bf16[2,3,64,640]{3,2,1,0:T(8,128)(2,1)S(1)}, u32[]{:S(2)}, u32[]{:S(2)}) collective-permute-start(bf16[2,3,64,640]{3,2,1,0:T(8,128)(2,1)S(1)} %pad_maximum_fusion.1), channel_id=1, source_target_pairs={{9,1},{1,9},{11,3},{3,11},{13,5},{5,13},{15,7},{7,15},{16,8},{8,16... | collective-permute-start | bytes 1474568 | tf_op jit(solution)/shard_map/ppermute | solution.py:197
  77.2 6.6 %collective-permute-start.17 = (bf16[2,2,64,640]{3,2,1,0:T(8,128)(2,1)S(1)}, bf16[2,2,64,640]{3,2,1,0:T(8,128)(2,1)S(1)}, u32[]{:S(2)}, u32[]{:S(2)}) collective-permute-start(bf16[2,2,64,640]{3,2,1,0:T(8,128)(2,1)S(1)} %get-tuple-element.24), channel_id=1, source_target_pairs={{0,1},{1,0},{2,3},{3,2},{4,5},{5,4},{6,7},{7,6},{8,9},{9,8},{10,11... | collective-permute-start | bytes 983048 | tf_op jit(solution)/shard_map/ppermute | solution.py:197

commit v3 on v1

v3 whole, which is shorter than its diff:
```python
import functools

import jax
import jax.numpy as jnp
from jax import lax
from jax.experimental import pallas as pl
from jax.experimental.pallas import tpu as pltpu
from jax.sharding import PartitionSpec as P


BF = jnp.bfloat16
F32 = jnp.float32
LANES = 128
OWN, LEFT_RIGHT, RIGHT_LEFT, FAR = (2, 2), (3, 4), (4, 3), (5, 5)
HALF = 64


def turn(pairs):
    width = pairs.shape[-1]
    return pltpu.roll(pairs.astype(F32), width // 2, axis=1)


def pack_kernel(flip_ref, cached_ref, new_ref, kept_ref, sent_ref):
    cols = cached_ref.shape[-1]
    upper = flip_ref[0]
    place = [
        (lax.broadcasted_iota(jnp.int32, (cols, 2 * cols), 0) + h * cols
         == lax.broadcasted_iota(jnp.int32, (cols, 2 * cols), 1)).astype(F32).astype(BF)
        for h in range(2)
    ]
    for out, flip in ((kept_ref, upper), (sent_ref, 1 - upper)):
        for row in range(2):
            at = jnp.where(flip == 0, row, 3 - row)
            channels = cached_ref.shape[2]
            firsts = jnp.concatenate([cached_ref[0, at], new_ref[0, at], new_ref[2, at]], axis=0)
            seconds = jnp.concatenate([cached_ref[1, at], new_ref[1, at], new_ref[3, at]], axis=0)
            both = jnp.dot(firsts, place[0], preferred_element_type=F32)
            both = both + jnp.dot(seconds, place[1], preferred_element_type=F32)
            out[row] = both.astype(BF).reshape(3, channels, 2 * cols)


def pack(flip, cached, new):
    channels, cols = cached.shape[2:]
    shape = jax.ShapeDtypeStruct((2, 3, channels, 2 * cols), BF)
    return pl.pallas_call(
        pack_kernel,
        in_specs=[pl.BlockSpec(memory_space=pltpu.SMEM)] + [pl.BlockSpec(memory_space=pltpu.VMEM)] * 2,
        out_specs=[pl.BlockSpec(memory_space=pltpu.VMEM)] * 2,
        out_shape=[shape, shape],
        compiler_params=pltpu.CompilerParams(vmem_limit_bytes=16 * 2**20),
        cost_estimate=pl.CostEstimate(flops=10**8, bytes_accessed=4 * 2**20, transcendentals=0),
        name="pack",
    )(flip, cached, new)


def unpack_kernel(scalars, *refs):
    rows, (out, turned, sems) = refs[:4], refs[4:]
    cols = turned.shape[-1]
    copies = []
    for at, source in enumerate(rows):
        inner = at % 2
        lower = scalars[0] if at < 2 else 1 - scalars[0]
        row = jnp.where(lower == 0, inner, 3 - inner)
        for p in range(2):
            pair = source[p]
            turned[at, 2 * p] = pair[:, :cols]
            turned[at, 2 * p + 1] = turn(pair).astype(BF)[:, :cols]
            both = pl.ds(2 * p, 2)
            copies.append(pltpu.make_async_copy(turned.at[at, both], out.at[both, row], sems.at[at, p]))
            copies[-1].start()
    for copy in copies:
        copy.wait()


def unpack(scalars, rows, shape):
    vmem = pl.BlockSpec(memory_space=pltpu.VMEM)
    return pl.pallas_call(
        unpack_kernel,
        in_specs=[pl.BlockSpec(memory_space=pltpu.SMEM)] + [vmem] * 4,
        out_specs=pl.BlockSpec(memory_space=pltpu.HBM),
        out_shape=jax.ShapeDtypeStruct(shape, BF),
        scratch_shapes=[pltpu.VMEM((4, 4, *shape[2:]), BF), pltpu.SemaphoreType.DMA((4, 2))],
        compiler_params=pltpu.CompilerParams(vmem_limit_bytes=16 * 2**20),
        cost_estimate=pl.CostEstimate(flops=10**7, bytes_accessed=4 * 2**20, transcendentals=0),
        name="unpack",
    )(scalars, *rows)


def column_sum(acc, bias, cols):
    rows, width = acc.shape[0] // 6, acc.shape[1]
    lane = lax.broadcasted_iota(jnp.int32, (rows, width), 1)
    zero = jnp.zeros((rows, width), F32)
    left_edge = (lane == 0) | (lane == cols)
    right_edge = (lane == cols - 1) | (lane == width - 1)
    totals = []
    for half in range(2):
        part = acc[half * 3 * rows : (half + 1) * 3 * rows]
        from_left = jnp.where(left_edge, zero, pltpu.roll(part[:rows], 1, axis=1))
        from_right = jnp.where(right_edge, zero, pltpu.roll(part[2 * rows :], width - 1, axis=1))
        totals.append((part[rows : 2 * rows] + from_left + from_right + bias[half][:, None]).astype(BF))
    return totals


def tap_weights(scalars, blocks, weights, t, delta):
    lanes = [pl.ds(pl.multiple_of(scalars[at] * LANES, LANES), LANES) for at in blocks]
    row_tap = jnp.where(scalars[0] == 0, delta, 2 - delta)
    halves = []
    for half in range(2):
        w = weights[half][t, row_tap, :, :, lanes[0]]
        w = w.reshape(w.shape[0] * w.shape[1], LANES)
        if blocks[0] != blocks[1]:
            v = weights[half][t, row_tap, :, :, lanes[1]].reshape(w.shape)
            first = lax.broadcasted_iota(jnp.int32, (1, LANES), 1) < HALF
            w = jnp.where(jnp.broadcast_to(first, w.shape), w, v)
        halves.append(w)
    return jnp.concatenate(halves, axis=0)


def put_pairs(xs, at, low, high):
    near = lax.broadcasted_iota(jnp.int32, low.shape, 1) < low.shape[1] // 2
    xs[(0, *at)] = low
    xs[(2, *at)] = high
    xs[(1, *at)] = jnp.where(near, turn(low), turn(high)).astype(BF)


def main_kernel(blocks, first, last, *refs):
    scalars, lo, hi, csides, own, other, *refs = refs
    before = None if first else refs.pop(0)
    bias = refs.pop(0) if last else None
    xs = refs.pop()
    cols = xs.shape[-1] // 2

    def one_pair(p, carry):
        for piece, body in enumerate((lo, hi)):
            at = pl.ds(piece * HALF, HALF)
            for row in range(3):
                low, high = ((body[row, p], body[row, p + 1]) if row < 2 else (csides[piece, p], csides[piece, p + 1]))
                put_pairs(xs, (row, at), low, high)
        taps = {
            (t, delta): tap_weights(scalars, blocks, (own, other), t, delta) for t in range(3) for delta in range(3)
        }
        for row in range(2):
            used = [at for at in taps if row + at[1] >= 1]
            lhs = jnp.concatenate([taps[at] for at in used], axis=1)
            window = jnp.concatenate([xs[t, row + delta - 1] for t, delta in used], axis=0)
            acc = jnp.dot(lhs, window, preferred_element_type=F32)
            if not first:
                acc = acc + before[p, row]
            if not last:
                refs[0][p, row] = acc
            elif row == 0:
                refs[0][p] = acc
            else:
                refs[1][p], refs[2][p] = column_sum(acc, bias, cols)
        return carry

    lax.fori_loop(0, 2, one_pair, 0)


def z_kernel(sources, last, *refs):
    scalars, *refs = refs
    zs = [refs.pop(0) for _ in range(1 + max(which for _, which, _ in sources))]
    own, other, before = refs[:3]
    refs = refs[3:]
    bias = refs.pop(0) if last else None
    xs = refs.pop()
    width = xs.shape[-1]
    edge = scalars[1] == 1

    def one_pair(p, carry):
        lhs, window = [], []
        for slot, (blocks, which, start) in enumerate(sources):
            for piece in range(2):
                low, high = (
                    jnp.where(edge, jnp.zeros((HALF, width), BF), zs[which][start + piece, q]) for q in (p, p + 1)
                )
                put_pairs(xs, (slot, pl.ds(piece * HALF, HALF)), low, high)
            for t in range(3):
                lhs.append(tap_weights(scalars, blocks, (own, other), t, 0))
                window.append(xs[t, slot])
        acc = before[p] + jnp.dot(
            jnp.concatenate(lhs, axis=1), jnp.concatenate(window, axis=0), preferred_element_type=F32
        )
        if last:
            refs[0][p], refs[1][p] = column_sum(acc, bias, width // 2)
        else:
            refs[0][p] = acc
        return carry

    lax.fori_loop(0, 2, one_pair, 0)


def kernel_call(body, scalars, operands, out_shape, aliases, scratch, flops):
    vmem = pl.BlockSpec(memory_space=pltpu.VMEM)
    return pl.pallas_call(
        body,
        in_specs=[pl.BlockSpec(memory_space=pltpu.SMEM)] + [vmem] * len(operands),
        out_specs=[vmem] * len(out_shape),
        scratch_shapes=[pltpu.VMEM(scratch, BF)],
        out_shape=out_shape,
        input_output_aliases=aliases,
        compiler_params=pltpu.CompilerParams(vmem_limit_bytes=28 * 2**20),
        cost_estimate=pl.CostEstimate(flops=flops, bytes_accessed=8 * 2**20, transcendentals=0),
    )(scalars, *operands)


def main_call(scalars, blocks, bodies, csides, weights, before, bias):
    first, last = before is None, bias is not None
    outs, width = weights[0].shape[3], csides.shape[-1]
    operands = [*bodies, csides, *weights]
    aliases = {}
    if last:
        operands += [before, bias]
        out_shape = [jax.ShapeDtypeStruct((2, 6 * outs, width), F32)] + [jax.ShapeDtypeStruct((2, outs, width), BF)] * 2
    else:
        out_shape = [jax.ShapeDtypeStruct((2, 2, 6 * outs, width), F32)]
        if not first:
            operands.append(before)
            aliases = {len(operands): 0}
    result = kernel_call(
        functools.partial(main_kernel, blocks, first, last), scalars, operands, out_shape, aliases,
        (3, 3, LANES, width), 2 * 6 * outs * 30 * LANES * width,
    )
    return result if last else result[0]


def z_call(scalars, sources, zs, weights, before, bias):
    last = bias is not None
    outs, width = weights[0].shape[3], before.shape[-1]
    operands = [*zs, *weights, before]
    aliases = {}
    if last:
        operands.append(bias)
        out_shape = [jax.ShapeDtypeStruct((2, outs, width), BF)] * 2
    else:
        out_shape = [jax.ShapeDtypeStruct((2, 6 * outs, width), F32)]
        aliases = {len(operands): 0}
    result = kernel_call(
        functools.partial(z_kernel, sources, last), scalars, operands, out_shape, aliases,
        (3, len(sources), LANES, width), 2 * 6 * outs * 6 * len(sources) * LANES * width,
    )
    return result if last else result[0]


def solution(mesh):
    bands, chans = mesh.shape["band"], mesh.shape["chan"]
    chips = chans // 2
    swap = [(2 * x + c, 2 * x + 1 - c) for x in range(chips) for c in range(2)]
    right = [(2 * x + c, 2 * ((x + 1) % chips) + c) for x in range(chips) for c in range(2)]
    left = [(target, source) for source, target in right]
    across = []
    for b in range(1, bands):
        for x in range(chips):
            here, there = b * chans + 2 * x + b % 2, (b - 1) * chans + 2 * x + b % 2
            across += [(here, there), (there, here)]
    for x in range(chips):
        here, there = 2 * x, (bands - 1) * chans + 2 * x + bands % 2
        across += [(here, there), (there, here)]

    def on_device(new_frames, cached_frames, conv_weight, out_bias):
        index = lax.axis_index("chan")
        core, chip = index % 2, index // 2
        even = core == 0
        flip = (core + lax.axis_index("band")) % 2
        upper = flip == 0
        band = lax.axis_index("band")
        edge = jnp.where(upper, band == 0, band == bands - 1)

        def send(a, pairs, axes="chan"):
            return lax.ppermute(a, axes, pairs)

        def other_core(*pieces):
            return send(jnp.stack([piece[1] for piece in pieces]), swap)

        def next_band(*pieces):
            return send(jnp.stack([piece[0] for piece in pieces]), across, ("band", "chan"))

        scalars = jnp.stack([flip, edge.astype(flip.dtype)] + [(chip + o) % chips for o in (0, chips - 1, 1, 2)])
        scalars, upper, even = lax.optimization_barrier((scalars.astype(jnp.int32), upper, even))
        kept, sent = pack(scalars, cached_frames, new_frames)
        got = send(sent, swap)
        got, conv_weight, out_bias = lax.optimization_barrier((got, conv_weight, out_bias))
        other_weight = send(conv_weight, swap)
        biases = jnp.stack([out_bias, send(out_bias, swap)])
        biases, scalars = lax.optimization_barrier((biases, scalars))
        lo, hi = jnp.where(even, kept, got), jnp.where(even, got, kept)
        l_lo = send(lo, right)
        r_hi = send(hi, left)
        l_hi = send(hi, right)
        r_lo = send(lo, left)
        weights = (conv_weight, other_weight)

        z_own = next_band(lo, hi)
        acc = main_call(scalars, OWN, (lo, hi), other_core(lo, hi), weights, None, None)
        f_lo = send(l_lo, right)
        f_hi = send(r_hi, left)
        acc = main_call(scalars, LEFT_RIGHT, (l_lo, r_hi), other_core(l_lo, r_hi), weights, acc, None)
        z_sides = next_band(l_lo, r_hi, r_lo, l_hi)
        acc = main_call(scalars, RIGHT_LEFT, (r_lo, l_hi), other_core(r_lo, l_hi), weights, acc, None)
        z_far = next_band(f_lo, f_hi)
        acc, inner, inner_theirs = main_call(scalars, FAR, (f_lo, f_hi), other_core(f_lo, f_hi), weights, acc, biases)
        inner_given = send(inner_theirs, swap)
        sources = ((OWN, 0, 0), (LEFT_RIGHT, 1, 0), (RIGHT_LEFT, 1, 2))
        acc = z_call(scalars, sources, (z_own, z_sides), weights, acc, None)
        outer, outer_theirs = z_call(scalars, ((FAR, 0, 0),), (z_far,), weights, acc, biases)
        outer_given = send(outer_theirs, swap)
        return unpack(scalars, (outer, inner, outer_given, inner_given), new_frames.shape)

    in_specs = (
        P(None, "band", "chan", None),
        P(None, "band", "chan", None),
        P(None, None, None, "chan", None),
        P("chan"),
    )

    return jax.shard_map(
        on_device, mesh=mesh, in_specs=in_specs, out_specs=P(None, "band", "chan", None), check_vma=False
    )
```

time: 80 us -> 83 us (1.038)
  the two profiles are of different devices: /device:TPU:31 before, /device:TPU:1 now
where the time goes in v3:
time: 83 us; the launch traced here: 82.9 us
  starting transfers between devices  28.9 us (35%)
  waiting for transfers between devices  27.7 us (33%)
  Pallas kernels  22.6 us (27%)
  local copies, waits for them, and re-layouts  2.58 us (3%)
    ppermute x18, starting transfers between devices, send(): return lax.ppermute(a, axes, pairs)  28.9 us
    ppermute x18, waiting for transfers between devices, send(): return lax.ppermute(a, axes, pairs)  27.7 us
    pallas_call x6, Pallas kernels, kernel_call(): pl.pallas_call(body, in_specs=[pl.BlockSpec(memory_space=pltpu.SMEM)] + [...  19.4 us
    unnamed x8, local copies, waits for them, and re-layouts  2.14 us
  transfers between devices with their start and end apart: 18, of which 8 were waited for; matrix products, arithmetic and copies ran while one was open for 1% of the time, Pallas kernels for 21%

profile of v3, /device:TPU:1, one launch (start us, length us, event | category | flops | bytes accessed | tf_op | source)
XLA Modules:
  0.0 82.9 jit_solution(7522346652743327390)
XLA Ops:
  0.0 0.1 stack.61.flip_ref.refs_0_.scalars
  0.1 0.0 copy-start.1
  0.1 1.1 %copy-done.1 = bf16[4,4,64,320]{3,2,1,0:T(8,128)(2,1)S(1)} copy-done((bf16[4,4,64,320]{3,2,1,0:T(8,128)(2,1)S(1)}, bf16[4,4,64,320]{3,2,1,0:T(8,128)(2,1)}, u32[]{:S(2)}) %copy-start.1) | copy-done | bytes 655384
  1.2 0.0 copy-start.2
  1.2 1.0 %copy-done.2 = bf16[2,4,64,320]{3,2,1,0:T(8,128)(2,1)S(1)} copy-done((bf16[2,4,64,320]{3,2,1,0:T(8,128)(2,1)S(1)}, bf16[2,4,64,320]{3,2,1,0:T(8,128)(2,1)}, u32[]{:S(2)}) %copy-start.2) | copy-done | bytes 327704
  2.2 1.6 %pack.1 = (bf16[2,3,64,640]{3,2,1,0:T(8,128)(2,1)S(1)}, bf16[2,3,64,640]{3,2,1,0:T(8,128)(2,1)S(1)}) custom-call(s32[6]{0:T(128)S(1)} %stack.61.flip_ref.refs_0_.scalars, bf16[2,4,64,320]{3,2,1,0:T(8,128)(2,1)S(1)} %copy-done.2, bf16[4,4,64,320]{3,2,1,0:T(8,128)(2,1)S(1)} %copy-done.1), custom_call_target="tpu_custom_call" | custom-call | flops 100000000 | bytes 4194304 | tf_op jit(solution)/shard_map/pack/pallas_call | solution.py:45
  3.8 3.3 %collective-permute-start = (bf16[2,3,64,640]{3,2,1,0:T(8,128)(2,1)S(1)}, bf16[2,3,64,640]{3,2,1,0:T(8,128)(2,1)S(1)}, u32[]{:S(2)}, u32[]{:S(2)}) collective-permute-start(bf16[2,3,64,640]{3,2,1,0:T(8,128)(2,1)S(1)} %get-tuple-element.20), channel_id=1, source_target_pairs={{0,1},{1,0},{2,3},{3,2},{4,5},{5,4},{6,7},{7,6},{8,9},{9,8},{10,11... | collective-permute-start | bytes 1474568 | tf_op jit(solution)/shard_map/ppermute | solution.py:270
  7.1 1.5 %collective-permute-done = bf16[2,3,64,640]{3,2,1,0:T(8,128)(2,1)S(1)} collective-permute-done((bf16[2,3,64,640]{3,2,1,0:T(8,128)(2,1)S(1)}, bf16[2,3,64,640]{3,2,1,0:T(8,128)(2,1)S(1)}, u32[]{:S(2)}, u32[]{:S(2)}) %collective-permute-start) | collective-permute-done | bytes 491552 | tf_op jit(solution)/shard_map/ppermute | solution.py:270
  8.6 0.0 copy-start.3
  8.6 0.1 broadcast_select_fusion.1
  8.7 0.1 collective-permute-start.2
  8.8 0.0 copy-start
  8.8 0.1 fusion
  8.9 2.7 %collective-permute-start.4 = (bf16[2,3,64,640]{3,2,1,0:T(8,128)(2,1)S(1)}, bf16[2,3,64,640]{3,2,1,0:T(8,128)(2,1)S(1)}, u32[]{:S(2)}, u32[]{:S(2)}) collective-permute-start(bf16[2,3,64,640]{3,2,1,0:T(8,128)(2,1)S(1)} %get-tuple-element.34.refs_2_), channel_id=1, source_target_pairs={{2,0},{3,1},{4,2},{5,3},{6,4},{7,5},{0,6},{1,7},{10,8},{11,9},{12,... | collective-permute-start | bytes 1474568 | tf_op jit(solution)/shard_map/ppermute | solution.py:270
  11.7 0.1 collective-permute-start.9
  11.7 1.4 %collective-permute-start.10 = (bf16[2,3,64,640]{3,2,1,0:T(8,128)(2,1)S(1)}, bf16[2,3,64,640]{3,2,1,0:T(8,128)(2,1)S(1)}, u32[]{:S(2)}, u32[]{:S(2)}) collective-permute-start(bf16[2,3,64,640]{3,2,1,0:T(8,128)(2,1)S(1)} %get-tuple-element.34.refs_2_), channel_id=1, source_target_pairs={{0,2},{1,3},{2,4},{3,5},{4,6},{5,7},{6,0},{7,1},{8,10},{9,11},{10,... | collective-permute-start | bytes 1474568 | tf_op jit(solution)/shard_map/ppermute | solution.py:270
  13.1 0.0 copy-done.3
  13.1 1.5 %collective-permute-start.1 = (f32[64]{0:T(128)S(1)}, f32[64]{0:T(128)S(1)}, u32[]{:S(2)}, u32[]{:S(2)}) collective-permute-start(f32[64]{0:T(128)S(1)} %copy-done.3), channel_id=1, source_target_pairs={{0,1},{1,0},{2,3},{3,2},{4,5},{5,4},{6,7},{7,6},{8,9},{9,8},{10,11... | collective-permute-start | bytes 776 | tf_op jit(solution)/shard_map/ppermute | solution.py:270
  14.6 0.1 pad_maximum_fusion.6
  14.7 0.1 pad_maximum_fusion.2
  14.7 0.7 collective-permute-done.1
  15.4 0.3 collective-permute-start.15
  15.8 6.6 %collective-permute-done.2.refs_1_ = bf16[2,3,64,640]{3,2,1,0:T(8,128)(2,1)S(1)} collective-permute-done((bf16[2,3,64,640]{3,2,1,0:T(8,128)(2,1)S(1)}, bf16[2,3,64,640]{3,2,1,0:T(8,128)(2,1)S(1)}, u32[]{:S(2)}, u32[]{:S(2)}) %collective-permute-start.2) | collective-permute-done | bytes 491552 | tf_op jit(solution)/shard_map/ppermute | solution.py:270
  22.4 0.0 copy-done
  22.4 2.1 %collective-permute-start.7 = (bf16[3,3,3,64,512]{4,3,2,1,0:T(8,128)(2,1)S(1)}, bf16[3,3,3,64,512]{4,3,2,1,0:T(8,128)(2,1)S(1)}, u32[]{:S(2)}, u32[]{:S(2)}) collective-permute-start(bf16[3,3,3,64,512]{4,3,2,1,0:T(8,128)(2,1)S(1)} %copy-done), channel_id=1, source_target_pairs={{0,1},{1,0},{2,3},{3,2},{4,5},{5,4},{6,7},{7,6},{8,9},{9,8},{10,11... | collective-permute-start | bytes 5308424 | tf_op jit(solution)/shard_map/ppermute | solution.py:270
  24.5 0.0 collective-permute-done.4.refs_2_
  24.6 0.1 pad_maximum_fusion.5
  24.7 0.1 collective-permute-start.14
  24.8 7.4 %collective-permute-done.9.refs_1_ = bf16[2,3,64,640]{3,2,1,0:T(8,128)(2,1)S(1)} collective-permute-done((bf16[2,3,64,640]{3,2,1,0:T(8,128)(2,1)S(1)}, bf16[2,3,64,640]{3,2,1,0:T(8,128)(2,1)S(1)}, u32[]{:S(2)}, u32[]{:S(2)}) %collective-permute-start.9) | collective-permute-done | bytes 491552 | tf_op jit(solution)/shard_map/ppermute | solution.py:270
  32.1 0.2 collective-permute-start.3
  32.4 0.5 collective-permute-done.10.refs_2_
  33.0 2.7 %collective-permute-start.5 = (bf16[2,3,64,640]{3,2,1,0:T(8,128)(2,1)S(1)}, bf16[2,3,64,640]{3,2,1,0:T(8,128)(2,1)S(1)}, u32[]{:S(2)}, u32[]{:S(2)}) collective-permute-start(bf16[2,3,64,640]{3,2,1,0:T(8,128)(2,1)S(1)} %collective-permute-done.4.refs_2_), channel_id=1, source_target_pairs={{2,0},{3,1},{4,2},{5,3},{6,4},{7,5},{0,6},{1,7},{10,8},{11,9},{12,... | collective-permute-start | bytes 1474568 | tf_op jit(solution)/shard_map/ppermute | solution.py:270
  35.7 0.1 pad_maximum_fusion.4
  35.8 0.1 pad_maximum_fusion
  35.9 9.7 %collective-permute-done.3.refs_1_ = bf16[2,3,64,640]{3,2,1,0:T(8,128)(2,1)S(1)} collective-permute-done((bf16[2,3,64,640]{3,2,1,0:T(8,128)(2,1)S(1)}, bf16[2,3,64,640]{3,2,1,0:T(8,128)(2,1)S(1)}, u32[]{:S(2)}, u32[]{:S(2)}) %collective-permute-start.3) | collective-permute-done | bytes 491552 | tf_op jit(solution)/shard_map/ppermute | solution.py:270
  45.6 2.1 %collective-permute-start.13 = (bf16[2,3,64,640]{3,2,1,0:T(8,128)(2,1)S(1)}, bf16[2,3,64,640]{3,2,1,0:T(8,128)(2,1)S(1)}, u32[]{:S(2)}, u32[]{:S(2)}) collective-permute-start(bf16[2,3,64,640]{3,2,1,0:T(8,128)(2,1)S(1)} %pad_maximum_fusion.4), channel_id=1, source_target_pairs={{0,1},{1,0},{2,3},{3,2},{4,5},{5,4},{6,7},{7,6},{8,9},{9,8},{10,11... | collective-permute-start | bytes 1474568 | tf_op jit(solution)/shard_map/ppermute | solution.py:270
  47.7 0.0 collective-permute-done.5.refs_2_
  47.8 0.1 collective-permute-start.11
  47.9 0.1 pad_maximum_fusion.3
  48.0 0.1 pad_maximum_fusion.1
  48.0 0.0 collective-permute-done.15.refs_3_
  48.1 1.5 %collective-permute-start.8 = (bf16[2,3,64,640]{3,2,1,0:T(8,128)(2,1)S(1)}, bf16[2,3,64,640]{3,2,1,0:T(8,128)(2,1)S(1)}, u32[]{:S(2)}, u32[]{:S(2)}) collective-permute-start(bf16[2,3,64,640]{3,2,1,0:T(8,128)(2,1)S(1)} %pad_maximum_fusion.2), channel_id=1, source_target_pairs={{9,1},{1,9},{11,3},{3,11},{13,5},{5,13},{15,7},{7,15},{16,8},{8,16... | collective-permute-start | bytes 1474568 | tf_op jit(solution)/shard_map/ppermute | solution.py:270
  49.6 0.0 collective-permute-done.7.refs_5_.refs_4_.refs_3_
  49.6 5.4 %collective-permute-start.12 = (bf16[2,3,64,640]{3,2,1,0:T(8,128)(2,1)S(1)}, bf16[2,3,64,640]{3,2,1,0:T(8,128)(2,1)S(1)}, u32[]{:S(2)}, u32[]{:S(2)}) collective-permute-start(bf16[2,3,64,640]{3,2,1,0:T(8,128)(2,1)S(1)} %pad_maximum_fusion.3), channel_id=1, source_target_pairs={{0,1},{1,0},{2,3},{3,2},{4,5},{5,4},{6,7},{7,6},{8,9},{9,8},{10,11... | collective-permute-start | bytes 1474568 | tf_op jit(solution)/shard_map/ppermute | solution.py:270
  55.0 3.5 %shard_map.46.refs_6_ = f32[2,2,384,640]{3,2,1,0:T(8,128)S(1)} custom-call(s32[6]{0:T(128)S(1)} %stack.61.flip_ref.refs_0_.scalars, bf16[2,3,64,640]{3,2,1,0:T(8,128)(2,1)S(1)} %get-tuple-element.33.refs_1_, bf16[2,3,64,640]{3,2,1,0:T(8,128)(2,1)S(1)} %get-tuple-element.34.refs_2_, bf16[2,3,64,640]{3,2,1,0:T(8,128)(2,1)S(1)} %collective-permute-done.15.refs_3_, ...), custom_call_target="tpu_custom_call" | custom-call | flops 1887436800 | bytes 8388608 | tf_op jit(solution)/shard_map/pallas_call | solution.py:195
  58.6 0.0 collective-permute-done.14.refs_3_
  58.6 0.1 collective-permute-start.6
  58.7 3.8 %shard_map.47.refs_6_ = f32[2,2,384,640]{3,2,1,0:T(8,128)S(1)} custom-call(s32[6]{0:T(128)S(1)} %stack.61.flip_ref.refs_0_.scalars, bf16[2,3,64,640]{3,2,1,0:T(8,128)(2,1)S(1)} %collective-permute-done.2.refs_1_, bf16[2,3,64,640]{3,2,1,0:T(8,128)(2,1)S(1)} %collective-permute-done.4.refs_2_, ...), custom_call_target="tpu_custom_call", output_to_operand_aliasing={{}: (6, {})} | custom-call | flops 1887436800 | bytes 8388608 | tf_op jit(solution)/shard_map/pallas_call | solution.py:195
  62.5 0.0 collective-permute-done.13.refs_3_
  62.5 3.8 %shard_map.48.refs_6_ = f32[2,2,384,640]{3,2,1,0:T(8,128)S(1)} custom-call(s32[6]{0:T(128)S(1)} %stack.61.flip_ref.refs_0_.scalars, bf16[2,3,64,640]{3,2,1,0:T(8,128)(2,1)S(1)} %collective-permute-done.9.refs_1_, bf16[2,3,64,640]{3,2,1,0:T(8,128)(2,1)S(1)} %collective-permute-done.10.refs_2_, ...), custom_call_target="tpu_custom_call", output_to_operand_aliasing={{}: (6, {})} | custom-call | flops 1887436800 | bytes 8388608 | tf_op jit(solution)/shard_map/pallas_call | solution.py:195
  66.3 0.0 collective-permute-done.12.refs_3_
  66.3 3.8 %shard_map.49 = (f32[2,384,640]{2,1,0:T(8,128)S(1)}, bf16[2,64,640]{2,1,0:T(8,128)(2,1)S(1)}, bf16[2,64,640]{2,1,0:T(8,128)(2,1)S(1)}) custom-call(s32[6]{0:T(128)S(1)} %stack.61.flip_ref.refs_0_.scalars, bf16[2,3,64,640]{3,2,1,0:T(8,128)(2,1)S(1)} %collective-permute-done.3.refs_1_, bf16[2,3,64,640]{3,2,1,0:T(8,128)(2,1)S(1)} %collective-permute-done.5.refs_2_, ...), custom_call_target="tpu_custom_call" | custom-call | flops 1887436800 | bytes 8388608 | tf_op jit(solution)/shard_map/pallas_call | solution.py:195
  70.1 0.0 collective-permute-done.8.refs_1_
  70.1 0.0 collective-permute-done.11.refs_2_
  70.1 2.7 %shard_map.50.refs_4_ = f32[2,384,640]{2,1,0:T(8,128)S(1)} custom-call(s32[6]{0:T(128)S(1)} %stack.61.flip_ref.refs_0_.scalars, bf16[2,3,64,640]{3,2,1,0:T(8,128)(2,1)S(1)} %collective-permute-done.8.refs_1_, bf16[4,3,64,640]{3,2,1,0:T(8,128)(2,1)S(1)} %collective-permute-done.11.refs_2_, ...), custom_call_target="tpu_custom_call", output_to_operand_aliasing={{}: (5, {})} | custom-call | flops 1132462080 | bytes 8388608 | tf_op jit(solution)/shard_map/pallas_call | solution.py:195
  72.9 0.0 collective-permute-done.6.refs_1_
  72.9 1.8 %shard_map.51 = (bf16[2,64,640]{2,1,0:T(8,128)(2,1)S(1)}, bf16[2,64,640]{2,1,0:T(8,128)(2,1)S(1)}) custom-call(s32[6]{0:T(128)S(1)} %stack.61.flip_ref.refs_0_.scalars, bf16[2,3,64,640]{3,2,1,0:T(8,128)(2,1)S(1)} %collective-permute-done.6.refs_1_, bf16[3,3,3,64,512]{4,3,2,1,0:T(8,128)(2,1)S(1)} %copy-done, ...), custom_call_target="tpu_custom_call" | custom-call | flops 377487360 | bytes 8388608 | tf_op jit(solution)/shard_map/pallas_call | solution.py:195
  74.7 5.1 %collective-permute-start.16 = (bf16[2,64,640]{2,1,0:T(8,128)(2,1)S(1)}, bf16[2,64,640]{2,1,0:T(8,128)(2,1)S(1)}, u32[]{:S(2)}, u32[]{:S(2)}) collective-permute-start(bf16[2,64,640]{2,1,0:T(8,128)(2,1)S(1)} %get-tuple-element.31), channel_id=1, source_target_pairs={{0,1},{1,0},{2,3},{3,2},{4,5},{5,4},{6,7},{7,6},{8,9},{9,8},{10,11... | collective-permute-start | bytes 491528 | tf_op jit(solution)/shard_map/ppermute | solution.py:270
  79.7 0.1 collective-permute-start.17
  79.8 0.9 %collective-permute-done.16.refs_2_ = bf16[2,64,640]{2,1,0:T(8,128)(2,1)S(1)} collective-permute-done((bf16[2,64,640]{2,1,0:T(8,128)(2,1)S(1)}, bf16[2,64,640]{2,1,0:T(8,128)(2,1)S(1)}, u32[]{:S(2)}, u32[]{:S(2)}) %collective-permute-start.16) | collective-permute-done | bytes 163872 | tf_op jit(solution)/shard_map/ppermute | solution.py:270
  80.8 0.4 collective-permute-done.17.refs_3_
  81.1 1.6 %unpack.1 = bf16[4,4,64,320]{3,2,1,0:T(8,128)(2,1)} custom-call(s32[6]{0:T(128)S(1)} %stack.61.flip_ref.refs_0_.scalars, bf16[2,64,640]{2,1,0:T(8,128)(2,1)S(1)} %get-tuple-element.29.refs_0_, bf16[2,64,640]{2,1,0:T(8,128)(2,1)S(1)} %get-tuple-element.30.refs_1_, bf16[2,64,640]{2,1,0:T(8,128)(2,1)S(1)} %collective-permute-done.16.refs_2_, ...), custom_call_target="tpu_custom_call" | custom-call | flops 10000000 | bytes 4194304 | tf_op jit(solution)/shard_map/unpack/pallas_call | solution.py:77
  (7 shorter events, 0.3 us)
Async XLA Ops:
  0.1 1.1 %copy-start.1 = (bf16[4,4,64,320]{3,2,1,0:T(8,128)(2,1)S(1)}, bf16[4,4,64,320]{3,2,1,0:T(8,128)(2,1)}, u32[]{:S(2)}) copy-start(bf16[4,4,64,320]{3,2,1,0:T(8,128)(2,1)} %new_ref.1) | copy-start | bytes 1966084
  1.2 1.0 %copy-start.2 = (bf16[2,4,64,320]{3,2,1,0:T(8,128)(2,1)S(1)}, bf16[2,4,64,320]{3,2,1,0:T(8,128)(2,1)}, u32[]{:S(2)}) copy-start(bf16[2,4,64,320]{3,2,1,0:T(8,128)(2,1)} %cached_ref.1) | copy-start | bytes 983044
  3.8 4.8 %collective-permute-start = (bf16[2,3,64,640]{3,2,1,0:T(8,128)(2,1)S(1)}, bf16[2,3,64,640]{3,2,1,0:T(8,128)(2,1)S(1)}, u32[]{:S(2)}, u32[]{:S(2)}) collective-permute-start(bf16[2,3,64,640]{3,2,1,0:T(8,128)(2,1)S(1)} %get-tuple-element.20), channel_id=1, source_target_pairs={{0,1},{1,0},{2,3},{3,2},{4,5},{5,4},{6,7},{7,6},{8,9},{9,8},{10,11... | collective-permute-start | bytes 1474568 | tf_op jit(solution)/shard_map/ppermute | solution.py:270
  8.6 4.5 %copy-start.3 = (f32[64]{0:T(128)S(1)}, f32[64]{0:T(128)}, u32[]{:S(2)}) copy-start(f32[64]{0:T(128)} %param.7) | copy-start | bytes 772
  8.7 13.7 %collective-permute-start.2 = (bf16[2,3,64,640]{3,2,1,0:T(8,128)(2,1)S(1)}, bf16[2,3,64,640]{3,2,1,0:T(8,128)(2,1)S(1)}, u32[]{:S(2)}, u32[]{:S(2)}) collective-permute-start(bf16[2,3,64,640]{3,2,1,0:T(8,128)(2,1)S(1)} %get-tuple-element.33.refs_1_), channel_id=1, source_target_pairs={{0,2},{1,3},{2,4},{3,5},{4,6},{5,7},{6,0},{7,1},{8,10},{9,11},{10,... | collective-permute-start | bytes 1474568 | tf_op jit(solution)/shard_map/ppermute | solution.py:270
  8.8 13.6 %copy-start = (bf16[3,3,3,64,512]{4,3,2,1,0:T(8,128)(2,1)S(1)}, bf16[3,3,3,64,512]{4,3,2,1,0:T(8,128)(2,1)}, u32[]{:S(2)}) copy-start(bf16[3,3,3,64,512]{4,3,2,1,0:T(8,128)(2,1)} %refs_2_) | copy-start | bytes 5308420
  8.9 15.6 %collective-permute-start.4 = (bf16[2,3,64,640]{3,2,1,0:T(8,128)(2,1)S(1)}, bf16[2,3,64,640]{3,2,1,0:T(8,128)(2,1)S(1)}, u32[]{:S(2)}, u32[]{:S(2)}) collective-permute-start(bf16[2,3,64,640]{3,2,1,0:T(8,128)(2,1)S(1)} %get-tuple-element.34.refs_2_), channel_id=1, source_target_pairs={{2,0},{3,1},{4,2},{5,3},{6,4},{7,5},{0,6},{1,7},{10,8},{11,9},{12,... | collective-permute-start | bytes 1474568 | tf_op jit(solution)/shard_map/ppermute | solution.py:270
  11.7 20.5 %collective-permute-start.9 = (bf16[2,3,64,640]{3,2,1,0:T(8,128)(2,1)S(1)}, bf16[2,3,64,640]{3,2,1,0:T(8,128)(2,1)S(1)}, u32[]{:S(2)}, u32[]{:S(2)}) collective-permute-start(bf16[2,3,64,640]{3,2,1,0:T(8,128)(2,1)S(1)} %get-tuple-element.33.refs_1_), channel_id=1, source_target_pairs={{2,0},{3,1},{4,2},{5,3},{6,4},{7,5},{0,6},{1,7},{10,8},{11,9},{12,... | collective-permute-start | bytes 1474568 | tf_op jit(solution)/shard_map/ppermute | solution.py:270
  11.7 21.2 %collective-permute-start.10 = (bf16[2,3,64,640]{3,2,1,0:T(8,128)(2,1)S(1)}, bf16[2,3,64,640]{3,2,1,0:T(8,128)(2,1)S(1)}, u32[]{:S(2)}, u32[]{:S(2)}) collective-permute-start(bf16[2,3,64,640]{3,2,1,0:T(8,128)(2,1)S(1)} %get-tuple-element.34.refs_2_), channel_id=1, source_target_pairs={{0,2},{1,3},{2,4},{3,5},{4,6},{5,7},{6,0},{7,1},{8,10},{9,11},{10,... | collective-permute-start | bytes 1474568 | tf_op jit(solution)/shard_map/ppermute | solution.py:270
  13.1 2.3 %collective-permute-start.1 = (f32[64]{0:T(128)S(1)}, f32[64]{0:T(128)S(1)}, u32[]{:S(2)}, u32[]{:S(2)}) collective-permute-start(f32[64]{0:T(128)S(1)} %copy-done.3), channel_id=1, source_target_pairs={{0,1},{1,0},{2,3},{3,2},{4,5},{5,4},{6,7},{7,6},{8,9},{9,8},{10,11... | collective-permute-start | bytes 776 | tf_op jit(solution)/shard_map/ppermute | solution.py:270
  15.4 32.6 %collective-permute-start.15 = (bf16[2,3,64,640]{3,2,1,0:T(8,128)(2,1)S(1)}, bf16[2,3,64,640]{3,2,1,0:T(8,128)(2,1)S(1)}, u32[]{:S(2)}, u32[]{:S(2)}) collective-permute-start(bf16[2,3,64,640]{3,2,1,0:T(8,128)(2,1)S(1)} %pad_maximum_fusion.6), channel_id=1, source_target_pairs={{0,1},{1,0},{2,3},{3,2},{4,5},{5,4},{6,7},{7,6},{8,9},{9,8},{10,11... | collective-permute-start | bytes 1474568 | tf_op jit(solution)/shard_map/ppermute | solution.py:270
  22.4 27.2 %collective-permute-start.7 = (bf16[3,3,3,64,512]{4,3,2,1,0:T(8,128)(2,1)S(1)}, bf16[3,3,3,64,512]{4,3,2,1,0:T(8,128)(2,1)S(1)}, u32[]{:S(2)}, u32[]{:S(2)}) collective-permute-start(bf16[3,3,3,64,512]{4,3,2,1,0:T(8,128)(2,1)S(1)} %copy-done), channel_id=1, source_target_pairs={{0,1},{1,0},{2,3},{3,2},{4,5},{5,4},{6,7},{7,6},{8,9},{9,8},{10,11... | collective-permute-start | bytes 5308424 | tf_op jit(solution)/shard_map/ppermute | solution.py:270
  24.7 33.9 %collective-permute-start.14 = (bf16[2,3,64,640]{3,2,1,0:T(8,128)(2,1)S(1)}, bf16[2,3,64,640]{3,2,1,0:T(8,128)(2,1)S(1)}, u32[]{:S(2)}, u32[]{:S(2)}) collective-permute-start(bf16[2,3,64,640]{3,2,1,0:T(8,128)(2,1)S(1)} %pad_maximum_fusion.5), channel_id=1, source_target_pairs={{0,1},{1,0},{2,3},{3,2},{4,5},{5,4},{6,7},{7,6},{8,9},{9,8},{10,11... | collective-permute-start | bytes 1474568 | tf_op jit(solution)/shard_map/ppermute | solution.py:270
  32.1 13.5 %collective-permute-start.3 = (bf16[2,3,64,640]{3,2,1,0:T(8,128)(2,1)S(1)}, bf16[2,3,64,640]{3,2,1,0:T(8,128)(2,1)S(1)}, u32[]{:S(2)}, u32[]{:S(2)}) collective-permute-start(bf16[2,3,64,640]{3,2,1,0:T(8,128)(2,1)S(1)} %collective-permute-done.2.refs_1_), channel_id=1, source_target_pairs={{0,2},{1,3},{2,4},{3,5},{4,6},{5,7},{6,0},{7,1},{8,10},{9,11},{10,... | collective-permute-start | bytes 1474568 | tf_op jit(solution)/shard_map/ppermute | solution.py:270
  33.0 14.8 %collective-permute-start.5 = (bf16[2,3,64,640]{3,2,1,0:T(8,128)(2,1)S(1)}, bf16[2,3,64,640]{3,2,1,0:T(8,128)(2,1)S(1)}, u32[]{:S(2)}, u32[]{:S(2)}) collective-permute-start(bf16[2,3,64,640]{3,2,1,0:T(8,128)(2,1)S(1)} %collective-permute-done.4.refs_2_), channel_id=1, source_target_pairs={{2,0},{3,1},{4,2},{5,3},{6,4},{7,5},{0,6},{1,7},{10,8},{11,9},{12,... | collective-permute-start | bytes 1474568 | tf_op jit(solution)/shard_map/ppermute | solution.py:270
  45.6 16.9 %collective-permute-start.13 = (bf16[2,3,64,640]{3,2,1,0:T(8,128)(2,1)S(1)}, bf16[2,3,64,640]{3,2,1,0:T(8,128)(2,1)S(1)}, u32[]{:S(2)}, u32[]{:S(2)}) collective-permute-start(bf16[2,3,64,640]{3,2,1,0:T(8,128)(2,1)S(1)} %pad_maximum_fusion.4), channel_id=1, source_target_pairs={{0,1},{1,0},{2,3},{3,2},{4,5},{5,4},{6,7},{7,6},{8,9},{9,8},{10,11... | collective-permute-start | bytes 1474568 | tf_op jit(solution)/shard_map/ppermute | solution.py:270
  47.8 22.4 %collective-permute-start.11 = (bf16[4,3,64,640]{3,2,1,0:T(8,128)(2,1)S(1)}, bf16[4,3,64,640]{3,2,1,0:T(8,128)(2,1)S(1)}, u32[]{:S(2)}, u32[]{:S(2)}) collective-permute-start(bf16[4,3,64,640]{3,2,1,0:T(8,128)(2,1)S(1)} %pad_maximum_fusion), channel_id=1, source_target_pairs={{9,1},{1,9},{11,3},{3,11},{13,5},{5,13},{15,7},{7,15},{16,8},{8,16... | collective-permute-start | bytes 2949128 | tf_op jit(solution)/shard_map/ppermute | solution.py:270
  48.1 22.1 %collective-permute-start.8 = (bf16[2,3,64,640]{3,2,1,0:T(8,128)(2,1)S(1)}, bf16[2,3,64,640]{3,2,1,0:T(8,128)(2,1)S(1)}, u32[]{:S(2)}, u32[]{:S(2)}) collective-permute-start(bf16[2,3,64,640]{3,2,1,0:T(8,128)(2,1)S(1)} %pad_maximum_fusion.2), channel_id=1, source_target_pairs={{9,1},{1,9},{11,3},{3,11},{13,5},{5,13},{15,7},{7,15},{16,8},{8,16... | collective-permute-start | bytes 1474568 | tf_op jit(solution)/shard_map/ppermute | solution.py:270
  49.6 16.7 %collective-permute-start.12 = (bf16[2,3,64,640]{3,2,1,0:T(8,128)(2,1)S(1)}, bf16[2,3,64,640]{3,2,1,0:T(8,128)(2,1)S(1)}, u32[]{:S(2)}, u32[]{:S(2)}) collective-permute-start(bf16[2,3,64,640]{3,2,1,0:T(8,128)(2,1)S(1)} %pad_maximum_fusion.3), channel_id=1, source_target_pairs={{0,1},{1,0},{2,3},{3,2},{4,5},{5,4},{6,7},{7,6},{8,9},{9,8},{10,11... | collective-permute-start | bytes 1474568 | tf_op jit(solution)/shard_map/ppermute | solution.py:270
  58.6 14.3 %collective-permute-start.6 = (bf16[2,3,64,640]{3,2,1,0:T(8,128)(2,1)S(1)}, bf16[2,3,64,640]{3,2,1,0:T(8,128)(2,1)S(1)}, u32[]{:S(2)}, u32[]{:S(2)}) collective-permute-start(bf16[2,3,64,640]{3,2,1,0:T(8,128)(2,1)S(1)} %pad_maximum_fusion.1), channel_id=1, source_target_pairs={{9,1},{1,9},{11,3},{3,11},{13,5},{5,13},{15,7},{7,15},{16,8},{8,16... | collective-permute-start | bytes 1474568 | tf_op jit(solution)/shard_map/ppermute | solution.py:270
  74.7 6.1 %collective-permute-start.16 = (bf16[2,64,640]{2,1,0:T(8,128)(2,1)S(1)}, bf16[2,64,640]{2,1,0:T(8,128)(2,1)S(1)}, u32[]{:S(2)}, u32[]{:S(2)}) collective-permute-start(bf16[2,64,640]{2,1,0:T(8,128)(2,1)S(1)} %get-tuple-element.31), channel_id=1, source_target_pairs={{0,1},{1,0},{2,3},{3,2},{4,5},{5,4},{6,7},{7,6},{8,9},{9,8},{10,11... | collective-permute-start | bytes 491528 | tf_op jit(solution)/shard_map/ppermute | solution.py:270
  79.7 1.4 %collective-permute-start.17 = (bf16[2,64,640]{2,1,0:T(8,128)(2,1)S(1)}, bf16[2,64,640]{2,1,0:T(8,128)(2,1)S(1)}, u32[]{:S(2)}, u32[]{:S(2)}) collective-permute-start(bf16[2,64,640]{2,1,0:T(8,128)(2,1)S(1)} %get-tuple-element.32), channel_id=1, source_target_pairs={{0,1},{1,0},{2,3},{3,2},{4,5},{5,4},{6,7},{7,6},{8,9},{9,8},{10,11... | collective-permute-start | bytes 491528 | tf_op jit(solution)/shard_map/ppermute | solution.py:270

commit v4 on v3

--- a/solution.py
+++ b/solution.py
@@ -253,9 +253,11 @@
         for x in range(chips):
             here, there = b * chans + 2 * x + b % 2, (b - 1) * chans + 2 * x + b % 2
             across += [(here, there), (there, here)]
+    across_last = list(across)
     for x in range(chips):
         here, there = 2 * x, (bands - 1) * chans + 2 * x + bands % 2
         across += [(here, there), (there, here)]
+        across_last += [(here, 2 * (x ^ 1)), (there, there - 2 * x + 2 * (x ^ 1))]
 
     def on_device(new_frames, cached_frames, conv_weight, out_bias):
         index = lax.axis_index("chan")
@@ -272,8 +274,8 @@
         def other_core(*pieces):
             return send(jnp.stack([piece[1] for piece in pieces]), swap)
 
-        def next_band(*pieces):
-            return send(jnp.stack([piece[0] for piece in pieces]), across, ("band", "chan"))
+        def next_band(pairs, *pieces):
+            return send(jnp.stack([piece[0] for piece in pieces]), pairs, ("band", "chan"))
 
         scalars = jnp.stack([flip, edge.astype(flip.dtype)] + [(chip + o) % chips for o in (0, chips - 1, 1, 2)])
         scalars, upper, even = lax.optimization_barrier((scalars.astype(jnp.int32), upper, even))
@@ -290,14 +292,14 @@
         r_lo = send(lo, left)
         weights = (conv_weight, other_weight)
 
-        z_own = next_band(lo, hi)
+        z_own = next_band(across, lo, hi)
         acc = main_call(scalars, OWN, (lo, hi), other_core(lo, hi), weights, None, None)
         f_lo = send(l_lo, right)
         f_hi = send(r_hi, left)
         acc = main_call(scalars, LEFT_RIGHT, (l_lo, r_hi), other_core(l_lo, r_hi), weights, acc, None)
-        z_sides = next_band(l_lo, r_hi, r_lo, l_hi)
+        z_sides = next_band(across, l_lo, r_hi, r_lo, l_hi)
         acc = main_call(scalars, RIGHT_LEFT, (r_lo, l_hi), other_core(r_lo, l_hi), weights, acc, None)
-        z_far = next_band(f_lo, f_hi)
+        z_far = next_band(across_last, f_lo, f_hi)
         acc, inner, inner_theirs = main_call(scalars, FAR, (f_lo, f_hi), other_core(f_lo, f_hi), weights, acc, biases)
         inner_given = send(inner_theirs, swap)
         sources = ((OWN, 0, 0), (LEFT_RIGHT, 1, 0), (RIGHT_LEFT, 1, 2))

time: 83 us -> 79.6 us (0.959)
  starting transfers between devices: 28.9 us -> 25.5 us
    ppermute x18, starting transfers between devices: 28.9 us -> 25.5 us  [send(): return lax.ppermute(a, axes, pairs)]
  transfers between devices with their start and end apart: 18 -> 18, of which waited for: 8 -> 8; matrix products, arithmetic and copies ran while one was open for 1% -> 1% of each run, Pallas kernels for 21% -> 22%
where the time goes in v4:
time: 79.6 us; the launch traced here: 79.5 us
  waiting for transfers between devices  27.7 us (35%)
  starting transfers between devices  25.5 us (32%)
  Pallas kernels  22.6 us (28%)
  local copies, waits for them, and re-layouts  2.58 us (3%)
    ppermute x18, waiting for transfers between devices, send(): return lax.ppermute(a, axes, pairs)  27.7 us
    ppermute x18, starting transfers between devices, send(): return lax.ppermute(a, axes, pairs)  25.5 us
    pallas_call x6, Pallas kernels, kernel_call(): pl.pallas_call(body, in_specs=[pl.BlockSpec(memory_space=pltpu.SMEM)] + [...  19.4 us
    unnamed x8, local copies, waits for them, and re-layouts  2.14 us
    pallas_call x1, Pallas kernels, pack(): pl.pallas_call(pack_kernel, in_specs=[pl.BlockSpec(memory_space=pltpu.SME...  1.62 us
  transfers between devices with their start and end apart: 18, of which 8 were waited for; matrix products, arithmetic and copies ran while one was open for 1% of the time, Pallas kernels for 22%

profile of v4, /device:TPU:1, one launch (start us, length us, event | category | flops | bytes accessed | tf_op | source)
XLA Modules:
  0.0 79.5 jit_solution(16164800608497154698)
XLA Ops:
  0.0 0.1 stack.61.flip_ref.refs_0_.scalars
  0.1 0.0 copy-start.1
  0.1 1.1 %copy-done.1 = bf16[4,4,64,320]{3,2,1,0:T(8,128)(2,1)S(1)} copy-done((bf16[4,4,64,320]{3,2,1,0:T(8,128)(2,1)S(1)}, bf16[4,4,64,320]{3,2,1,0:T(8,128)(2,1)}, u32[]{:S(2)}) %copy-start.1) | copy-done | bytes 655384
  1.2 0.0 copy-start.2
  1.2 1.0 %copy-done.2 = bf16[2,4,64,320]{3,2,1,0:T(8,128)(2,1)S(1)} copy-done((bf16[2,4,64,320]{3,2,1,0:T(8,128)(2,1)S(1)}, bf16[2,4,64,320]{3,2,1,0:T(8,128)(2,1)}, u32[]{:S(2)}) %copy-start.2) | copy-done | bytes 327704
  2.2 1.6 %pack.1 = (bf16[2,3,64,640]{3,2,1,0:T(8,128)(2,1)S(1)}, bf16[2,3,64,640]{3,2,1,0:T(8,128)(2,1)S(1)}) custom-call(s32[6]{0:T(128)S(1)} %stack.61.flip_ref.refs_0_.scalars, bf16[2,4,64,320]{3,2,1,0:T(8,128)(2,1)S(1)} %copy-done.2, bf16[4,4,64,320]{3,2,1,0:T(8,128)(2,1)S(1)} %copy-done.1), custom_call_target="tpu_custom_call" | custom-call | flops 100000000 | bytes 4194304 | tf_op jit(solution)/shard_map/pack/pallas_call | solution.py:45
  3.8 3.3 %collective-permute-start = (bf16[2,3,64,640]{3,2,1,0:T(8,128)(2,1)S(1)}, bf16[2,3,64,640]{3,2,1,0:T(8,128)(2,1)S(1)}, u32[]{:S(2)}, u32[]{:S(2)}) collective-permute-start(bf16[2,3,64,640]{3,2,1,0:T(8,128)(2,1)S(1)} %get-tuple-element.20), channel_id=1, source_target_pairs={{0,1},{1,0},{2,3},{3,2},{4,5},{5,4},{6,7},{7,6},{8,9},{9,8},{10,11... | collective-permute-start | bytes 1474568 | tf_op jit(solution)/shard_map/ppermute | solution.py:272
  7.1 1.5 %collective-permute-done = bf16[2,3,64,640]{3,2,1,0:T(8,128)(2,1)S(1)} collective-permute-done((bf16[2,3,64,640]{3,2,1,0:T(8,128)(2,1)S(1)}, bf16[2,3,64,640]{3,2,1,0:T(8,128)(2,1)S(1)}, u32[]{:S(2)}, u32[]{:S(2)}) %collective-permute-start) | collective-permute-done | bytes 491552 | tf_op jit(solution)/shard_map/ppermute | solution.py:272
  8.6 0.0 copy-start.3
  8.6 0.1 broadcast_select_fusion.1
  8.7 0.1 collective-permute-start.2
  8.8 0.0 copy-start
  8.8 0.1 fusion
  8.9 2.7 %collective-permute-start.4 = (bf16[2,3,64,640]{3,2,1,0:T(8,128)(2,1)S(1)}, bf16[2,3,64,640]{3,2,1,0:T(8,128)(2,1)S(1)}, u32[]{:S(2)}, u32[]{:S(2)}) collective-permute-start(bf16[2,3,64,640]{3,2,1,0:T(8,128)(2,1)S(1)} %get-tuple-element.34.refs_2_), channel_id=1, source_target_pairs={{2,0},{3,1},{4,2},{5,3},{6,4},{7,5},{0,6},{1,7},{10,8},{11,9},{12,... | collective-permute-start | bytes 1474568 | tf_op jit(solution)/shard_map/ppermute | solution.py:272
  11.7 0.1 collective-permute-start.9
  11.7 1.4 %collective-permute-start.10 = (bf16[2,3,64,640]{3,2,1,0:T(8,128)(2,1)S(1)}, bf16[2,3,64,640]{3,2,1,0:T(8,128)(2,1)S(1)}, u32[]{:S(2)}, u32[]{:S(2)}) collective-permute-start(bf16[2,3,64,640]{3,2,1,0:T(8,128)(2,1)S(1)} %get-tuple-element.34.refs_2_), channel_id=1, source_target_pairs={{0,2},{1,3},{2,4},{3,5},{4,6},{5,7},{6,0},{7,1},{8,10},{9,11},{10,... | collective-permute-start | bytes 1474568 | tf_op jit(solution)/shard_map/ppermute | solution.py:272
  13.1 0.0 copy-done.3
  13.1 1.5 %collective-permute-start.1 = (f32[64]{0:T(128)S(1)}, f32[64]{0:T(128)S(1)}, u32[]{:S(2)}, u32[]{:S(2)}) collective-permute-start(f32[64]{0:T(128)S(1)} %copy-done.3), channel_id=1, source_target_pairs={{0,1},{1,0},{2,3},{3,2},{4,5},{5,4},{6,7},{7,6},{8,9},{9,8},{10,11... | collective-permute-start | bytes 776 | tf_op jit(solution)/shard_map/ppermute | solution.py:272
  14.6 0.1 pad_maximum_fusion.6
  14.7 0.1 pad_maximum_fusion.2
  14.7 0.7 collective-permute-done.1
  15.4 0.3 collective-permute-start.15
  15.8 6.6 %collective-permute-done.2.refs_1_ = bf16[2,3,64,640]{3,2,1,0:T(8,128)(2,1)S(1)} collective-permute-done((bf16[2,3,64,640]{3,2,1,0:T(8,128)(2,1)S(1)}, bf16[2,3,64,640]{3,2,1,0:T(8,128)(2,1)S(1)}, u32[]{:S(2)}, u32[]{:S(2)}) %collective-permute-start.2) | collective-permute-done | bytes 491552 | tf_op jit(solution)/shard_map/ppermute | solution.py:272
  22.4 0.0 copy-done
  22.4 2.1 %collective-permute-start.7 = (bf16[3,3,3,64,512]{4,3,2,1,0:T(8,128)(2,1)S(1)}, bf16[3,3,3,64,512]{4,3,2,1,0:T(8,128)(2,1)S(1)}, u32[]{:S(2)}, u32[]{:S(2)}) collective-permute-start(bf16[3,3,3,64,512]{4,3,2,1,0:T(8,128)(2,1)S(1)} %copy-done), channel_id=1, source_target_pairs={{0,1},{1,0},{2,3},{3,2},{4,5},{5,4},{6,7},{7,6},{8,9},{9,8},{10,11... | collective-permute-start | bytes 5308424 | tf_op jit(solution)/shard_map/ppermute | solution.py:272
  24.5 0.0 collective-permute-done.4.refs_2_
  24.6 0.1 pad_maximum_fusion.5
  24.7 0.1 collective-permute-start.14
  24.8 7.4 %collective-permute-done.9.refs_1_ = bf16[2,3,64,640]{3,2,1,0:T(8,128)(2,1)S(1)} collective-permute-done((bf16[2,3,64,640]{3,2,1,0:T(8,128)(2,1)S(1)}, bf16[2,3,64,640]{3,2,1,0:T(8,128)(2,1)S(1)}, u32[]{:S(2)}, u32[]{:S(2)}) %collective-permute-start.9) | collective-permute-done | bytes 491552 | tf_op jit(solution)/shard_map/ppermute | solution.py:272
  32.1 0.2 collective-permute-start.3
  32.4 0.5 collective-permute-done.10.refs_2_
  33.0 2.7 %collective-permute-start.5 = (bf16[2,3,64,640]{3,2,1,0:T(8,128)(2,1)S(1)}, bf16[2,3,64,640]{3,2,1,0:T(8,128)(2,1)S(1)}, u32[]{:S(2)}, u32[]{:S(2)}) collective-permute-start(bf16[2,3,64,640]{3,2,1,0:T(8,128)(2,1)S(1)} %collective-permute-done.4.refs_2_), channel_id=1, source_target_pairs={{2,0},{3,1},{4,2},{5,3},{6,4},{7,5},{0,6},{1,7},{10,8},{11,9},{12,... | collective-permute-start | bytes 1474568 | tf_op jit(solution)/shard_map/ppermute | solution.py:272
  35.7 0.1 pad_maximum_fusion.4
  35.8 0.1 pad_maximum_fusion
  35.9 9.7 %collective-permute-done.3.refs_1_ = bf16[2,3,64,640]{3,2,1,0:T(8,128)(2,1)S(1)} collective-permute-done((bf16[2,3,64,640]{3,2,1,0:T(8,128)(2,1)S(1)}, bf16[2,3,64,640]{3,2,1,0:T(8,128)(2,1)S(1)}, u32[]{:S(2)}, u32[]{:S(2)}) %collective-permute-start.3) | collective-permute-done | bytes 491552 | tf_op jit(solution)/shard_map/ppermute | solution.py:272
  45.6 2.1 %collective-permute-start.13 = (bf16[2,3,64,640]{3,2,1,0:T(8,128)(2,1)S(1)}, bf16[2,3,64,640]{3,2,1,0:T(8,128)(2,1)S(1)}, u32[]{:S(2)}, u32[]{:S(2)}) collective-permute-start(bf16[2,3,64,640]{3,2,1,0:T(8,128)(2,1)S(1)} %pad_maximum_fusion.4), channel_id=1, source_target_pairs={{0,1},{1,0},{2,3},{3,2},{4,5},{5,4},{6,7},{7,6},{8,9},{9,8},{10,11... | collective-permute-start | bytes 1474568 | tf_op jit(solution)/shard_map/ppermute | solution.py:272
  47.7 0.0 collective-permute-done.5.refs_2_
  47.8 0.1 collective-permute-start.11
  47.9 0.1 pad_maximum_fusion.3
  48.0 0.1 pad_maximum_fusion.1
  48.0 0.0 collective-permute-done.15.refs_3_
  48.1 1.5 %collective-permute-start.8 = (bf16[2,3,64,640]{3,2,1,0:T(8,128)(2,1)S(1)}, bf16[2,3,64,640]{3,2,1,0:T(8,128)(2,1)S(1)}, u32[]{:S(2)}, u32[]{:S(2)}) collective-permute-start(bf16[2,3,64,640]{3,2,1,0:T(8,128)(2,1)S(1)} %pad_maximum_fusion.2), channel_id=1, source_target_pairs={{9,1},{1,9},{11,3},{3,11},{13,5},{5,13},{15,7},{7,15},{16,8},{8,16... | collective-permute-start | bytes 1474568 | tf_op jit(solution)/shard_map/ppermute | solution.py:272
  49.6 0.0 collective-permute-done.7.refs_5_.refs_4_.refs_3_
  49.6 5.4 %collective-permute-start.12 = (bf16[2,3,64,640]{3,2,1,0:T(8,128)(2,1)S(1)}, bf16[2,3,64,640]{3,2,1,0:T(8,128)(2,1)S(1)}, u32[]{:S(2)}, u32[]{:S(2)}) collective-permute-start(bf16[2,3,64,640]{3,2,1,0:T(8,128)(2,1)S(1)} %pad_maximum_fusion.3), channel_id=1, source_target_pairs={{0,1},{1,0},{2,3},{3,2},{4,5},{5,4},{6,7},{7,6},{8,9},{9,8},{10,11... | collective-permute-start | bytes 1474568 | tf_op jit(solution)/shard_map/ppermute | solution.py:272
  55.0 3.5 %shard_map.46.refs_6_ = f32[2,2,384,640]{3,2,1,0:T(8,128)S(1)} custom-call(s32[6]{0:T(128)S(1)} %stack.61.flip_ref.refs_0_.scalars, bf16[2,3,64,640]{3,2,1,0:T(8,128)(2,1)S(1)} %get-tuple-element.33.refs_1_, bf16[2,3,64,640]{3,2,1,0:T(8,128)(2,1)S(1)} %get-tuple-element.34.refs_2_, bf16[2,3,64,640]{3,2,1,0:T(8,128)(2,1)S(1)} %collective-permute-done.15.refs_3_, ...), custom_call_target="tpu_custom_call" | custom-call | flops 1887436800 | bytes 8388608 | tf_op jit(solution)/shard_map/pallas_call | solution.py:195
  58.6 0.0 collective-permute-done.14.refs_3_
  58.6 0.1 collective-permute-start.6
  58.7 3.8 %shard_map.47.refs_6_ = f32[2,2,384,640]{3,2,1,0:T(8,128)S(1)} custom-call(s32[6]{0:T(128)S(1)} %stack.61.flip_ref.refs_0_.scalars, bf16[2,3,64,640]{3,2,1,0:T(8,128)(2,1)S(1)} %collective-permute-done.2.refs_1_, bf16[2,3,64,640]{3,2,1,0:T(8,128)(2,1)S(1)} %collective-permute-done.4.refs_2_, ...), custom_call_target="tpu_custom_call", output_to_operand_aliasing={{}: (6, {})} | custom-call | flops 1887436800 | bytes 8388608 | tf_op jit(solution)/shard_map/pallas_call | solution.py:195
  62.5 0.0 collective-permute-done.13.refs_3_
  62.5 3.8 %shard_map.48.refs_6_ = f32[2,2,384,640]{3,2,1,0:T(8,128)S(1)} custom-call(s32[6]{0:T(128)S(1)} %stack.61.flip_ref.refs_0_.scalars, bf16[2,3,64,640]{3,2,1,0:T(8,128)(2,1)S(1)} %collective-permute-done.9.refs_1_, bf16[2,3,64,640]{3,2,1,0:T(8,128)(2,1)S(1)} %collective-permute-done.10.refs_2_, ...), custom_call_target="tpu_custom_call", output_to_operand_aliasing={{}: (6, {})} | custom-call | flops 1887436800 | bytes 8388608 | tf_op jit(solution)/shard_map/pallas_call | solution.py:195
  66.3 0.0 collective-permute-done.12.refs_3_
  66.3 3.8 %shard_map.49 = (f32[2,384,640]{2,1,0:T(8,128)S(1)}, bf16[2,64,640]{2,1,0:T(8,128)(2,1)S(1)}, bf16[2,64,640]{2,1,0:T(8,128)(2,1)S(1)}) custom-call(s32[6]{0:T(128)S(1)} %stack.61.flip_ref.refs_0_.scalars, bf16[2,3,64,640]{3,2,1,0:T(8,128)(2,1)S(1)} %collective-permute-done.3.refs_1_, bf16[2,3,64,640]{3,2,1,0:T(8,128)(2,1)S(1)} %collective-permute-done.5.refs_2_, ...), custom_call_target="tpu_custom_call" | custom-call | flops 1887436800 | bytes 8388608 | tf_op jit(solution)/shard_map/pallas_call | solution.py:195
  70.1 0.0 collective-permute-done.8.refs_1_
  70.1 0.0 collective-permute-done.11.refs_2_
  70.1 2.7 %shard_map.50.refs_4_ = f32[2,384,640]{2,1,0:T(8,128)S(1)} custom-call(s32[6]{0:T(128)S(1)} %stack.61.flip_ref.refs_0_.scalars, bf16[2,3,64,640]{3,2,1,0:T(8,128)(2,1)S(1)} %collective-permute-done.8.refs_1_, bf16[4,3,64,640]{3,2,1,0:T(8,128)(2,1)S(1)} %collective-permute-done.11.refs_2_, ...), custom_call_target="tpu_custom_call", output_to_operand_aliasing={{}: (5, {})} | custom-call | flops 1132462080 | bytes 8388608 | tf_op jit(solution)/shard_map/pallas_call | solution.py:195
  72.9 0.0 collective-permute-done.6.refs_1_
  72.9 1.8 %shard_map.51 = (bf16[2,64,640]{2,1,0:T(8,128)(2,1)S(1)}, bf16[2,64,640]{2,1,0:T(8,128)(2,1)S(1)}) custom-call(s32[6]{0:T(128)S(1)} %stack.61.flip_ref.refs_0_.scalars, bf16[2,3,64,640]{3,2,1,0:T(8,128)(2,1)S(1)} %collective-permute-done.6.refs_1_, bf16[3,3,3,64,512]{4,3,2,1,0:T(8,128)(2,1)S(1)} %copy-done, ...), custom_call_target="tpu_custom_call" | custom-call | flops 377487360 | bytes 8388608 | tf_op jit(solution)/shard_map/pallas_call | solution.py:195
  74.7 1.7 %collective-permute-start.16 = (bf16[2,64,640]{2,1,0:T(8,128)(2,1)S(1)}, bf16[2,64,640]{2,1,0:T(8,128)(2,1)S(1)}, u32[]{:S(2)}, u32[]{:S(2)}) collective-permute-start(bf16[2,64,640]{2,1,0:T(8,128)(2,1)S(1)} %get-tuple-element.31), channel_id=1, source_target_pairs={{0,1},{1,0},{2,3},{3,2},{4,5},{5,4},{6,7},{7,6},{8,9},{9,8},{10,11... | collective-permute-start | bytes 491528 | tf_op jit(solution)/shard_map/ppermute | solution.py:272
  76.3 0.1 collective-permute-start.17
  76.4 0.9 %collective-permute-done.16.refs_2_ = bf16[2,64,640]{2,1,0:T(8,128)(2,1)S(1)} collective-permute-done((bf16[2,64,640]{2,1,0:T(8,128)(2,1)S(1)}, bf16[2,64,640]{2,1,0:T(8,128)(2,1)S(1)}, u32[]{:S(2)}, u32[]{:S(2)}) %collective-permute-start.16) | collective-permute-done | bytes 163872 | tf_op jit(solution)/shard_map/ppermute | solution.py:272
  77.4 0.4 collective-permute-done.17.refs_3_
  77.7 1.6 %unpack.1 = bf16[4,4,64,320]{3,2,1,0:T(8,128)(2,1)} custom-call(s32[6]{0:T(128)S(1)} %stack.61.flip_ref.refs_0_.scalars, bf16[2,64,640]{2,1,0:T(8,128)(2,1)S(1)} %get-tuple-element.29.refs_0_, bf16[2,64,640]{2,1,0:T(8,128)(2,1)S(1)} %get-tuple-element.30.refs_1_, bf16[2,64,640]{2,1,0:T(8,128)(2,1)S(1)} %collective-permute-done.16.refs_2_, ...), custom_call_target="tpu_custom_call" | custom-call | flops 10000000 | bytes 4194304 | tf_op jit(solution)/shard_map/unpack/pallas_call | solution.py:77
  (7 shorter events, 0.3 us)
Async XLA Ops:
  0.1 1.1 %copy-start.1 = (bf16[4,4,64,320]{3,2,1,0:T(8,128)(2,1)S(1)}, bf16[4,4,64,320]{3,2,1,0:T(8,128)(2,1)}, u32[]{:S(2)}) copy-start(bf16[4,4,64,320]{3,2,1,0:T(8,128)(2,1)} %new_ref.1) | copy-start | bytes 1966084
  1.2 1.0 %copy-start.2 = (bf16[2,4,64,320]{3,2,1,0:T(8,128)(2,1)S(1)}, bf16[2,4,64,320]{3,2,1,0:T(8,128)(2,1)}, u32[]{:S(2)}) copy-start(bf16[2,4,64,320]{3,2,1,0:T(8,128)(2,1)} %cached_ref.1) | copy-start | bytes 983044
  3.8 4.8 %collective-permute-start = (bf16[2,3,64,640]{3,2,1,0:T(8,128)(2,1)S(1)}, bf16[2,3,64,640]{3,2,1,0:T(8,128)(2,1)S(1)}, u32[]{:S(2)}, u32[]{:S(2)}) collective-permute-start(bf16[2,3,64,640]{3,2,1,0:T(8,128)(2,1)S(1)} %get-tuple-element.20), channel_id=1, source_target_pairs={{0,1},{1,0},{2,3},{3,2},{4,5},{5,4},{6,7},{7,6},{8,9},{9,8},{10,11... | collective-permute-start | bytes 1474568 | tf_op jit(solution)/shard_map/ppermute | solution.py:272
  8.6 4.5 %copy-start.3 = (f32[64]{0:T(128)S(1)}, f32[64]{0:T(128)}, u32[]{:S(2)}) copy-start(f32[64]{0:T(128)} %param.7) | copy-start | bytes 772
  8.7 13.7 %collective-permute-start.2 = (bf16[2,3,64,640]{3,2,1,0:T(8,128)(2,1)S(1)}, bf16[2,3,64,640]{3,2,1,0:T(8,128)(2,1)S(1)}, u32[]{:S(2)}, u32[]{:S(2)}) collective-permute-start(bf16[2,3,64,640]{3,2,1,0:T(8,128)(2,1)S(1)} %get-tuple-element.33.refs_1_), channel_id=1, source_target_pairs={{0,2},{1,3},{2,4},{3,5},{4,6},{5,7},{6,0},{7,1},{8,10},{9,11},{10,... | collective-permute-start | bytes 1474568 | tf_op jit(solution)/shard_map/ppermute | solution.py:272
  8.8 13.6 %copy-start = (bf16[3,3,3,64,512]{4,3,2,1,0:T(8,128)(2,1)S(1)}, bf16[3,3,3,64,512]{4,3,2,1,0:T(8,128)(2,1)}, u32[]{:S(2)}) copy-start(bf16[3,3,3,64,512]{4,3,2,1,0:T(8,128)(2,1)} %refs_2_) | copy-start | bytes 5308420
  8.9 15.6 %collective-permute-start.4 = (bf16[2,3,64,640]{3,2,1,0:T(8,128)(2,1)S(1)}, bf16[2,3,64,640]{3,2,1,0:T(8,128)(2,1)S(1)}, u32[]{:S(2)}, u32[]{:S(2)}) collective-permute-start(bf16[2,3,64,640]{3,2,1,0:T(8,128)(2,1)S(1)} %get-tuple-element.34.refs_2_), channel_id=1, source_target_pairs={{2,0},{3,1},{4,2},{5,3},{6,4},{7,5},{0,6},{1,7},{10,8},{11,9},{12,... | collective-permute-start | bytes 1474568 | tf_op jit(solution)/shard_map/ppermute | solution.py:272
  11.7 20.5 %collective-permute-start.9 = (bf16[2,3,64,640]{3,2,1,0:T(8,128)(2,1)S(1)}, bf16[2,3,64,640]{3,2,1,0:T(8,128)(2,1)S(1)}, u32[]{:S(2)}, u32[]{:S(2)}) collective-permute-start(bf16[2,3,64,640]{3,2,1,0:T(8,128)(2,1)S(1)} %get-tuple-element.33.refs_1_), channel_id=1, source_target_pairs={{2,0},{3,1},{4,2},{5,3},{6,4},{7,5},{0,6},{1,7},{10,8},{11,9},{12,... | collective-permute-start | bytes 1474568 | tf_op jit(solution)/shard_map/ppermute | solution.py:272
  11.7 21.2 %collective-permute-start.10 = (bf16[2,3,64,640]{3,2,1,0:T(8,128)(2,1)S(1)}, bf16[2,3,64,640]{3,2,1,0:T(8,128)(2,1)S(1)}, u32[]{:S(2)}, u32[]{:S(2)}) collective-permute-start(bf16[2,3,64,640]{3,2,1,0:T(8,128)(2,1)S(1)} %get-tuple-element.34.refs_2_), channel_id=1, source_target_pairs={{0,2},{1,3},{2,4},{3,5},{4,6},{5,7},{6,0},{7,1},{8,10},{9,11},{10,... | collective-permute-start | bytes 1474568 | tf_op jit(solution)/shard_map/ppermute | solution.py:272
  13.1 2.3 %collective-permute-start.1 = (f32[64]{0:T(128)S(1)}, f32[64]{0:T(128)S(1)}, u32[]{:S(2)}, u32[]{:S(2)}) collective-permute-start(f32[64]{0:T(128)S(1)} %copy-done.3), channel_id=1, source_target_pairs={{0,1},{1,0},{2,3},{3,2},{4,5},{5,4},{6,7},{7,6},{8,9},{9,8},{10,11... | collective-permute-start | bytes 776 | tf_op jit(solution)/shard_map/ppermute | solution.py:272
  15.4 32.6 %collective-permute-start.15 = (bf16[2,3,64,640]{3,2,1,0:T(8,128)(2,1)S(1)}, bf16[2,3,64,640]{3,2,1,0:T(8,128)(2,1)S(1)}, u32[]{:S(2)}, u32[]{:S(2)}) collective-permute-start(bf16[2,3,64,640]{3,2,1,0:T(8,128)(2,1)S(1)} %pad_maximum_fusion.6), channel_id=1, source_target_pairs={{0,1},{1,0},{2,3},{3,2},{4,5},{5,4},{6,7},{7,6},{8,9},{9,8},{10,11... | collective-permute-start | bytes 1474568 | tf_op jit(solution)/shard_map/ppermute | solution.py:272
  22.4 27.2 %collective-permute-start.7 = (bf16[3,3,3,64,512]{4,3,2,1,0:T(8,128)(2,1)S(1)}, bf16[3,3,3,64,512]{4,3,2,1,0:T(8,128)(2,1)S(1)}, u32[]{:S(2)}, u32[]{:S(2)}) collective-permute-start(bf16[3,3,3,64,512]{4,3,2,1,0:T(8,128)(2,1)S(1)} %copy-done), channel_id=1, source_target_pairs={{0,1},{1,0},{2,3},{3,2},{4,5},{5,4},{6,7},{7,6},{8,9},{9,8},{10,11... | collective-permute-start | bytes 5308424 | tf_op jit(solution)/shard_map/ppermute | solution.py:272
  24.7 33.9 %collective-permute-start.14 = (bf16[2,3,64,640]{3,2,1,0:T(8,128)(2,1)S(1)}, bf16[2,3,64,640]{3,2,1,0:T(8,128)(2,1)S(1)}, u32[]{:S(2)}, u32[]{:S(2)}) collective-permute-start(bf16[2,3,64,640]{3,2,1,0:T(8,128)(2,1)S(1)} %pad_maximum_fusion.5), channel_id=1, source_target_pairs={{0,1},{1,0},{2,3},{3,2},{4,5},{5,4},{6,7},{7,6},{8,9},{9,8},{10,11... | collective-permute-start | bytes 1474568 | tf_op jit(solution)/shard_map/ppermute | solution.py:272
  32.1 13.5 %collective-permute-start.3 = (bf16[2,3,64,640]{3,2,1,0:T(8,128)(2,1)S(1)}, bf16[2,3,64,640]{3,2,1,0:T(8,128)(2,1)S(1)}, u32[]{:S(2)}, u32[]{:S(2)}) collective-permute-start(bf16[2,3,64,640]{3,2,1,0:T(8,128)(2,1)S(1)} %collective-permute-done.2.refs_1_), channel_id=1, source_target_pairs={{0,2},{1,3},{2,4},{3,5},{4,6},{5,7},{6,0},{7,1},{8,10},{9,11},{10,... | collective-permute-start | bytes 1474568 | tf_op jit(solution)/shard_map/ppermute | solution.py:272
  33.0 14.8 %collective-permute-start.5 = (bf16[2,3,64,640]{3,2,1,0:T(8,128)(2,1)S(1)}, bf16[2,3,64,640]{3,2,1,0:T(8,128)(2,1)S(1)}, u32[]{:S(2)}, u32[]{:S(2)}) collective-permute-start(bf16[2,3,64,640]{3,2,1,0:T(8,128)(2,1)S(1)} %collective-permute-done.4.refs_2_), channel_id=1, source_target_pairs={{2,0},{3,1},{4,2},{5,3},{6,4},{7,5},{0,6},{1,7},{10,8},{11,9},{12,... | collective-permute-start | bytes 1474568 | tf_op jit(solution)/shard_map/ppermute | solution.py:272
  45.6 16.9 %collective-permute-start.13 = (bf16[2,3,64,640]{3,2,1,0:T(8,128)(2,1)S(1)}, bf16[2,3,64,640]{3,2,1,0:T(8,128)(2,1)S(1)}, u32[]{:S(2)}, u32[]{:S(2)}) collective-permute-start(bf16[2,3,64,640]{3,2,1,0:T(8,128)(2,1)S(1)} %pad_maximum_fusion.4), channel_id=1, source_target_pairs={{0,1},{1,0},{2,3},{3,2},{4,5},{5,4},{6,7},{7,6},{8,9},{9,8},{10,11... | collective-permute-start | bytes 1474568 | tf_op jit(solution)/shard_map/ppermute | solution.py:272
  47.8 22.4 %collective-permute-start.11 = (bf16[4,3,64,640]{3,2,1,0:T(8,128)(2,1)S(1)}, bf16[4,3,64,640]{3,2,1,0:T(8,128)(2,1)S(1)}, u32[]{:S(2)}, u32[]{:S(2)}) collective-permute-start(bf16[4,3,64,640]{3,2,1,0:T(8,128)(2,1)S(1)} %pad_maximum_fusion), channel_id=1, source_target_pairs={{9,1},{1,9},{11,3},{3,11},{13,5},{5,13},{15,7},{7,15},{16,8},{8,16... | collective-permute-start | bytes 2949128 | tf_op jit(solution)/shard_map/ppermute | solution.py:272
  48.1 22.1 %collective-permute-start.8 = (bf16[2,3,64,640]{3,2,1,0:T(8,128)(2,1)S(1)}, bf16[2,3,64,640]{3,2,1,0:T(8,128)(2,1)S(1)}, u32[]{:S(2)}, u32[]{:S(2)}) collective-permute-start(bf16[2,3,64,640]{3,2,1,0:T(8,128)(2,1)S(1)} %pad_maximum_fusion.2), channel_id=1, source_target_pairs={{9,1},{1,9},{11,3},{3,11},{13,5},{5,13},{15,7},{7,15},{16,8},{8,16... | collective-permute-start | bytes 1474568 | tf_op jit(solution)/shard_map/ppermute | solution.py:272
  49.6 16.7 %collective-permute-start.12 = (bf16[2,3,64,640]{3,2,1,0:T(8,128)(2,1)S(1)}, bf16[2,3,64,640]{3,2,1,0:T(8,128)(2,1)S(1)}, u32[]{:S(2)}, u32[]{:S(2)}) collective-permute-start(bf16[2,3,64,640]{3,2,1,0:T(8,128)(2,1)S(1)} %pad_maximum_fusion.3), channel_id=1, source_target_pairs={{0,1},{1,0},{2,3},{3,2},{4,5},{5,4},{6,7},{7,6},{8,9},{9,8},{10,11... | collective-permute-start | bytes 1474568 | tf_op jit(solution)/shard_map/ppermute | solution.py:272
  58.6 14.3 %collective-permute-start.6 = (bf16[2,3,64,640]{3,2,1,0:T(8,128)(2,1)S(1)}, bf16[2,3,64,640]{3,2,1,0:T(8,128)(2,1)S(1)}, u32[]{:S(2)}, u32[]{:S(2)}) collective-permute-start(bf16[2,3,64,640]{3,2,1,0:T(8,128)(2,1)S(1)} %pad_maximum_fusion.1), channel_id=1, source_target_pairs={{9,1},{1,9},{11,3},{3,11},{13,5},{5,13},{15,7},{7,15},{16,8},{8,16... | collective-permute-start | bytes 1474568 | tf_op jit(solution)/shard_map/ppermute | solution.py:272
  74.7 2.7 %collective-permute-start.16 = (bf16[2,64,640]{2,1,0:T(8,128)(2,1)S(1)}, bf16[2,64,640]{2,1,0:T(8,128)(2,1)S(1)}, u32[]{:S(2)}, u32[]{:S(2)}) collective-permute-start(bf16[2,64,640]{2,1,0:T(8,128)(2,1)S(1)} %get-tuple-element.31), channel_id=1, source_target_pairs={{0,1},{1,0},{2,3},{3,2},{4,5},{5,4},{6,7},{7,6},{8,9},{9,8},{10,11... | collective-permute-start | bytes 491528 | tf_op jit(solution)/shard_map/ppermute | solution.py:272
  76.3 1.4 %collective-permute-start.17 = (bf16[2,64,640]{2,1,0:T(8,128)(2,1)S(1)}, bf16[2,64,640]{2,1,0:T(8,128)(2,1)S(1)}, u32[]{:S(2)}, u32[]{:S(2)}) collective-permute-start(bf16[2,64,640]{2,1,0:T(8,128)(2,1)S(1)} %get-tuple-element.32), channel_id=1, source_target_pairs={{0,1},{1,0},{2,3},{3,2},{4,5},{5,4},{6,7},{7,6},{8,9},{9,8},{10,11... | collective-permute-start | bytes 491528 | tf_op jit(solution)/shard_map/ppermute | solution.py:272

commit v5 on v4

--- a/solution.py
+++ b/solution.py
@@ -127,10 +127,11 @@
     scalars, lo, hi, csides, own, other, *refs = refs
     before = None if first else refs.pop(0)
     bias = refs.pop(0) if last else None
-    xs = refs.pop()
-    cols = xs.shape[-1] // 2
-
-    def one_pair(p, carry):
+    buffers = refs.pop()
+    cols = buffers.shape[-1] // 2
+
+    def one_pair(p):
+        xs = buffers.at[p]
         for piece, body in enumerate((lo, hi)):
             at = pl.ds(piece * HALF, HALF)
             for row in range(3):
@@ -152,9 +153,9 @@
                 refs[0][p] = acc
             else:
                 refs[1][p], refs[2][p] = column_sum(acc, bias, cols)
-        return carry
-
-    lax.fori_loop(0, 2, one_pair, 0)
+
+    for p in range(2):
+        one_pair(p)
 
 
 def z_kernel(sources, last, *refs):
@@ -163,11 +164,12 @@
     own, other, before = refs[:3]
     refs = refs[3:]
     bias = refs.pop(0) if last else None
-    xs = refs.pop()
-    width = xs.shape[-1]
+    buffers = refs.pop()
+    width = buffers.shape[-1]
     edge = scalars[1] == 1
 
-    def one_pair(p, carry):
+    def one_pair(p):
+        xs = buffers.at[p]
         lhs, window = [], []
         for slot, (blocks, which, start) in enumerate(sources):
             for piece in range(2):
@@ -185,9 +187,9 @@
             refs[0][p], refs[1][p] = column_sum(acc, bias, width // 2)
         else:
             refs[0][p] = acc
-        return carry
-
-    lax.fori_loop(0, 2, one_pair, 0)
+
+    for p in range(2):
+        one_pair(p)
 
 
 def kernel_call(body, scalars, operands, out_shape, aliases, scratch, flops):
@@ -219,7 +221,7 @@
             aliases = {len(operands): 0}
     result = kernel_call(
         functools.partial(main_kernel, blocks, first, last), scalars, operands, out_shape, aliases,
-        (3, 3, LANES, width), 2 * 6 * outs * 30 * LANES * width,
+        (2, 3, 3, LANES, width), 2 * 6 * outs * 30 * LANES * width,
     )
     return result if last else result[0]
 
@@ -237,7 +239,7 @@
         aliases = {len(operands): 0}
     result = kernel_call(
         functools.partial(z_kernel, sources, last), scalars, operands, out_shape, aliases,
-        (3, len(sources), LANES, width), 2 * 6 * outs * 6 * len(sources) * LANES * width,
+        (2, 3, len(sources), LANES, width), 2 * 6 * outs * 6 * len(sources) * LANES * width,
     )
     return result if last else result[0]
 

time: 79.6 us -> 79.4 us (level)
  no operation moved by 1% of the time
where the time goes in v5:
time: 79.4 us; the launch traced here: 79.2 us
  waiting for transfers between devices  27.7 us (35%)
  starting transfers between devices  26 us (33%)
  Pallas kernels  21.9 us (28%)
  local copies, waits for them, and re-layouts  2.58 us (3%)
    ppermute x18, waiting for transfers between devices, send(): return lax.ppermute(a, axes, pairs)  27.7 us
    ppermute x18, starting transfers between devices, send(): return lax.ppermute(a, axes, pairs)  26 us
    pallas_call x6, Pallas kernels, kernel_call(): pl.pallas_call(body, in_specs=[pl.BlockSpec(memory_space=pltpu.SMEM)] + [...  18.7 us
    unnamed x8, local copies, waits for them, and re-layouts  2.14 us
    pallas_call x1, Pallas kernels, pack(): pl.pallas_call(pack_kernel, in_specs=[pl.BlockSpec(memory_space=pltpu.SME...  1.62 us
  transfers between devices with their start and end apart: 18, of which 8 were waited for; matrix products, arithmetic and copies ran while one was open for 1% of the time, Pallas kernels for 22%

profile of v5, /device:TPU:1, one launch (start us, length us, event | category | flops | bytes accessed | tf_op | source)
XLA Modules:
  0.0 79.2 jit_solution(14114817720186077766)
XLA Ops:
  0.0 0.1 stack.61.flip_ref.refs_0_.scalars
  0.1 0.0 copy-start.1
  0.1 1.1 %copy-done.1 = bf16[4,4,64,320]{3,2,1,0:T(8,128)(2,1)S(1)} copy-done((bf16[4,4,64,320]{3,2,1,0:T(8,128)(2,1)S(1)}, bf16[4,4,64,320]{3,2,1,0:T(8,128)(2,1)}, u32[]{:S(2)}) %copy-start.1) | copy-done | bytes 655384
  1.2 0.0 copy-start.2
  1.2 1.0 %copy-done.2 = bf16[2,4,64,320]{3,2,1,0:T(8,128)(2,1)S(1)} copy-done((bf16[2,4,64,320]{3,2,1,0:T(8,128)(2,1)S(1)}, bf16[2,4,64,320]{3,2,1,0:T(8,128)(2,1)}, u32[]{:S(2)}) %copy-start.2) | copy-done | bytes 327704
  2.2 1.6 %pack.1 = (bf16[2,3,64,640]{3,2,1,0:T(8,128)(2,1)S(1)}, bf16[2,3,64,640]{3,2,1,0:T(8,128)(2,1)S(1)}) custom-call(s32[6]{0:T(128)S(1)} %stack.61.flip_ref.refs_0_.scalars, bf16[2,4,64,320]{3,2,1,0:T(8,128)(2,1)S(1)} %copy-done.2, bf16[4,4,64,320]{3,2,1,0:T(8,128)(2,1)S(1)} %copy-done.1), custom_call_target="tpu_custom_call" | custom-call | flops 100000000 | bytes 4194304 | tf_op jit(solution)/shard_map/pack/pallas_call | solution.py:45
  3.8 3.3 %collective-permute-start = (bf16[2,3,64,640]{3,2,1,0:T(8,128)(2,1)S(1)}, bf16[2,3,64,640]{3,2,1,0:T(8,128)(2,1)S(1)}, u32[]{:S(2)}, u32[]{:S(2)}) collective-permute-start(bf16[2,3,64,640]{3,2,1,0:T(8,128)(2,1)S(1)} %get-tuple-element.20), channel_id=1, source_target_pairs={{0,1},{1,0},{2,3},{3,2},{4,5},{5,4},{6,7},{7,6},{8,9},{9,8},{10,11... | collective-permute-start | bytes 1474568 | tf_op jit(solution)/shard_map/ppermute | solution.py:274
  7.1 1.5 %collective-permute-done = bf16[2,3,64,640]{3,2,1,0:T(8,128)(2,1)S(1)} collective-permute-done((bf16[2,3,64,640]{3,2,1,0:T(8,128)(2,1)S(1)}, bf16[2,3,64,640]{3,2,1,0:T(8,128)(2,1)S(1)}, u32[]{:S(2)}, u32[]{:S(2)}) %collective-permute-start) | collective-permute-done | bytes 491552 | tf_op jit(solution)/shard_map/ppermute | solution.py:274
  8.6 0.0 copy-start.3
  8.6 0.1 broadcast_select_fusion.1
  8.7 0.1 collective-permute-start.2
  8.8 0.0 copy-start
  8.8 0.1 fusion
  8.9 2.7 %collective-permute-start.4 = (bf16[2,3,64,640]{3,2,1,0:T(8,128)(2,1)S(1)}, bf16[2,3,64,640]{3,2,1,0:T(8,128)(2,1)S(1)}, u32[]{:S(2)}, u32[]{:S(2)}) collective-permute-start(bf16[2,3,64,640]{3,2,1,0:T(8,128)(2,1)S(1)} %get-tuple-element.34.refs_2_), channel_id=1, source_target_pairs={{2,0},{3,1},{4,2},{5,3},{6,4},{7,5},{0,6},{1,7},{10,8},{11,9},{12,... | collective-permute-start | bytes 1474568 | tf_op jit(solution)/shard_map/ppermute | solution.py:274
  11.7 0.1 collective-permute-start.9
  11.7 1.4 %collective-permute-start.10 = (bf16[2,3,64,640]{3,2,1,0:T(8,128)(2,1)S(1)}, bf16[2,3,64,640]{3,2,1,0:T(8,128)(2,1)S(1)}, u32[]{:S(2)}, u32[]{:S(2)}) collective-permute-start(bf16[2,3,64,640]{3,2,1,0:T(8,128)(2,1)S(1)} %get-tuple-element.34.refs_2_), channel_id=1, source_target_pairs={{0,2},{1,3},{2,4},{3,5},{4,6},{5,7},{6,0},{7,1},{8,10},{9,11},{10,... | collective-permute-start | bytes 1474568 | tf_op jit(solution)/shard_map/ppermute | solution.py:274
  13.1 0.0 copy-done.3
  13.1 1.5 %collective-permute-start.1 = (f32[64]{0:T(128)S(1)}, f32[64]{0:T(128)S(1)}, u32[]{:S(2)}, u32[]{:S(2)}) collective-permute-start(f32[64]{0:T(128)S(1)} %copy-done.3), channel_id=1, source_target_pairs={{0,1},{1,0},{2,3},{3,2},{4,5},{5,4},{6,7},{7,6},{8,9},{9,8},{10,11... | collective-permute-start | bytes 776 | tf_op jit(solution)/shard_map/ppermute | solution.py:274
  14.6 0.1 pad_maximum_fusion.6
  14.7 0.1 pad_maximum_fusion.2
  14.7 0.7 collective-permute-done.1
  15.4 0.3 collective-permute-start.15
  15.8 6.6 %collective-permute-done.2.refs_1_ = bf16[2,3,64,640]{3,2,1,0:T(8,128)(2,1)S(1)} collective-permute-done((bf16[2,3,64,640]{3,2,1,0:T(8,128)(2,1)S(1)}, bf16[2,3,64,640]{3,2,1,0:T(8,128)(2,1)S(1)}, u32[]{:S(2)}, u32[]{:S(2)}) %collective-permute-start.2) | collective-permute-done | bytes 491552 | tf_op jit(solution)/shard_map/ppermute | solution.py:274
  22.4 0.0 copy-done
  22.4 2.1 %collective-permute-start.7 = (bf16[3,3,3,64,512]{4,3,2,1,0:T(8,128)(2,1)S(1)}, bf16[3,3,3,64,512]{4,3,2,1,0:T(8,128)(2,1)S(1)}, u32[]{:S(2)}, u32[]{:S(2)}) collective-permute-start(bf16[3,3,3,64,512]{4,3,2,1,0:T(8,128)(2,1)S(1)} %copy-done), channel_id=1, source_target_pairs={{0,1},{1,0},{2,3},{3,2},{4,5},{5,4},{6,7},{7,6},{8,9},{9,8},{10,11... | collective-permute-start | bytes 5308424 | tf_op jit(solution)/shard_map/ppermute | solution.py:274
  24.5 0.0 collective-permute-done.4.refs_2_
  24.6 0.1 pad_maximum_fusion.5
  24.7 0.1 collective-permute-start.14
  24.8 7.4 %collective-permute-done.9.refs_1_ = bf16[2,3,64,640]{3,2,1,0:T(8,128)(2,1)S(1)} collective-permute-done((bf16[2,3,64,640]{3,2,1,0:T(8,128)(2,1)S(1)}, bf16[2,3,64,640]{3,2,1,0:T(8,128)(2,1)S(1)}, u32[]{:S(2)}, u32[]{:S(2)}) %collective-permute-start.9) | collective-permute-done | bytes 491552 | tf_op jit(solution)/shard_map/ppermute | solution.py:274
  32.1 0.2 collective-permute-start.3
  32.4 0.5 collective-permute-done.10.refs_2_
  33.0 2.7 %collective-permute-start.5 = (bf16[2,3,64,640]{3,2,1,0:T(8,128)(2,1)S(1)}, bf16[2,3,64,640]{3,2,1,0:T(8,128)(2,1)S(1)}, u32[]{:S(2)}, u32[]{:S(2)}) collective-permute-start(bf16[2,3,64,640]{3,2,1,0:T(8,128)(2,1)S(1)} %collective-permute-done.4.refs_2_), channel_id=1, source_target_pairs={{2,0},{3,1},{4,2},{5,3},{6,4},{7,5},{0,6},{1,7},{10,8},{11,9},{12,... | collective-permute-start | bytes 1474568 | tf_op jit(solution)/shard_map/ppermute | solution.py:274
  35.7 0.1 pad_maximum_fusion.4
  35.8 0.1 pad_maximum_fusion
  35.9 9.7 %collective-permute-done.3.refs_1_ = bf16[2,3,64,640]{3,2,1,0:T(8,128)(2,1)S(1)} collective-permute-done((bf16[2,3,64,640]{3,2,1,0:T(8,128)(2,1)S(1)}, bf16[2,3,64,640]{3,2,1,0:T(8,128)(2,1)S(1)}, u32[]{:S(2)}, u32[]{:S(2)}) %collective-permute-start.3) | collective-permute-done | bytes 491552 | tf_op jit(solution)/shard_map/ppermute | solution.py:274
  45.6 2.1 %collective-permute-start.13 = (bf16[2,3,64,640]{3,2,1,0:T(8,128)(2,1)S(1)}, bf16[2,3,64,640]{3,2,1,0:T(8,128)(2,1)S(1)}, u32[]{:S(2)}, u32[]{:S(2)}) collective-permute-start(bf16[2,3,64,640]{3,2,1,0:T(8,128)(2,1)S(1)} %pad_maximum_fusion.4), channel_id=1, source_target_pairs={{0,1},{1,0},{2,3},{3,2},{4,5},{5,4},{6,7},{7,6},{8,9},{9,8},{10,11... | collective-permute-start | bytes 1474568 | tf_op jit(solution)/shard_map/ppermute | solution.py:274
  47.7 0.0 collective-permute-done.5.refs_2_
  47.8 0.1 collective-permute-start.11
  47.9 0.1 pad_maximum_fusion.3
  48.0 0.1 pad_maximum_fusion.1
  48.0 0.0 collective-permute-done.15.refs_3_
  48.1 1.5 %collective-permute-start.8 = (bf16[2,3,64,640]{3,2,1,0:T(8,128)(2,1)S(1)}, bf16[2,3,64,640]{3,2,1,0:T(8,128)(2,1)S(1)}, u32[]{:S(2)}, u32[]{:S(2)}) collective-permute-start(bf16[2,3,64,640]{3,2,1,0:T(8,128)(2,1)S(1)} %pad_maximum_fusion.2), channel_id=1, source_target_pairs={{9,1},{1,9},{11,3},{3,11},{13,5},{5,13},{15,7},{7,15},{16,8},{8,16... | collective-permute-start | bytes 1474568 | tf_op jit(solution)/shard_map/ppermute | solution.py:274
  49.6 0.0 collective-permute-done.7.refs_5_.refs_4_.refs_3_
  49.6 5.4 %collective-permute-start.12 = (bf16[2,3,64,640]{3,2,1,0:T(8,128)(2,1)S(1)}, bf16[2,3,64,640]{3,2,1,0:T(8,128)(2,1)S(1)}, u32[]{:S(2)}, u32[]{:S(2)}) collective-permute-start(bf16[2,3,64,640]{3,2,1,0:T(8,128)(2,1)S(1)} %pad_maximum_fusion.3), channel_id=1, source_target_pairs={{0,1},{1,0},{2,3},{3,2},{4,5},{5,4},{6,7},{7,6},{8,9},{9,8},{10,11... | collective-permute-start | bytes 1474568 | tf_op jit(solution)/shard_map/ppermute | solution.py:274
  55.0 3.2 %shard_map.46.refs_6_ = f32[2,2,384,640]{3,2,1,0:T(8,128)S(1)} custom-call(s32[6]{0:T(128)S(1)} %stack.61.flip_ref.refs_0_.scalars, bf16[2,3,64,640]{3,2,1,0:T(8,128)(2,1)S(1)} %get-tuple-element.33.refs_1_, bf16[2,3,64,640]{3,2,1,0:T(8,128)(2,1)S(1)} %get-tuple-element.34.refs_2_, bf16[2,3,64,640]{3,2,1,0:T(8,128)(2,1)S(1)} %collective-permute-done.15.refs_3_, ...), custom_call_target="tpu_custom_call" | custom-call | flops 1887436800 | bytes 8388608 | tf_op jit(solution)/shard_map/pallas_call | solution.py:197
  58.2 0.0 collective-permute-done.14.refs_3_
  58.3 0.1 collective-permute-start.6
  58.4 3.8 %shard_map.47.refs_6_ = f32[2,2,384,640]{3,2,1,0:T(8,128)S(1)} custom-call(s32[6]{0:T(128)S(1)} %stack.61.flip_ref.refs_0_.scalars, bf16[2,3,64,640]{3,2,1,0:T(8,128)(2,1)S(1)} %collective-permute-done.2.refs_1_, bf16[2,3,64,640]{3,2,1,0:T(8,128)(2,1)S(1)} %collective-permute-done.4.refs_2_, ...), custom_call_target="tpu_custom_call", output_to_operand_aliasing={{}: (6, {})} | custom-call | flops 1887436800 | bytes 8388608 | tf_op jit(solution)/shard_map/pallas_call | solution.py:197
  62.2 0.0 collective-permute-done.13.refs_3_
  62.2 3.9 %shard_map.48.refs_6_ = f32[2,2,384,640]{3,2,1,0:T(8,128)S(1)} custom-call(s32[6]{0:T(128)S(1)} %stack.61.flip_ref.refs_0_.scalars, bf16[2,3,64,640]{3,2,1,0:T(8,128)(2,1)S(1)} %collective-permute-done.9.refs_1_, bf16[2,3,64,640]{3,2,1,0:T(8,128)(2,1)S(1)} %collective-permute-done.10.refs_2_, ...), custom_call_target="tpu_custom_call", output_to_operand_aliasing={{}: (6, {})} | custom-call | flops 1887436800 | bytes 8388608 | tf_op jit(solution)/shard_map/pallas_call | solution.py:197
  66.1 0.0 collective-permute-done.12.refs_3_
  66.1 3.6 %shard_map.49 = (f32[2,384,640]{2,1,0:T(8,128)S(1)}, bf16[2,64,640]{2,1,0:T(8,128)(2,1)S(1)}, bf16[2,64,640]{2,1,0:T(8,128)(2,1)S(1)}) custom-call(s32[6]{0:T(128)S(1)} %stack.61.flip_ref.refs_0_.scalars, bf16[2,3,64,640]{3,2,1,0:T(8,128)(2,1)S(1)} %collective-permute-done.3.refs_1_, bf16[2,3,64,640]{3,2,1,0:T(8,128)(2,1)S(1)} %collective-permute-done.5.refs_2_, ...), custom_call_target="tpu_custom_call" | custom-call | flops 1887436800 | bytes 8388608 | tf_op jit(solution)/shard_map/pallas_call | solution.py:197
  69.7 0.0 collective-permute-done.8.refs_1_
  69.7 0.0 collective-permute-done.11.refs_2_
  69.7 2.7 %shard_map.50.refs_4_ = f32[2,384,640]{2,1,0:T(8,128)S(1)} custom-call(s32[6]{0:T(128)S(1)} %stack.61.flip_ref.refs_0_.scalars, bf16[2,3,64,640]{3,2,1,0:T(8,128)(2,1)S(1)} %collective-permute-done.8.refs_1_, bf16[4,3,64,640]{3,2,1,0:T(8,128)(2,1)S(1)} %collective-permute-done.11.refs_2_, ...), custom_call_target="tpu_custom_call", output_to_operand_aliasing={{}: (5, {})} | custom-call | flops 1132462080 | bytes 8388608 | tf_op jit(solution)/shard_map/pallas_call | solution.py:197
  72.4 0.0 collective-permute-done.6.refs_1_
  72.4 1.5 %shard_map.51 = (bf16[2,64,640]{2,1,0:T(8,128)(2,1)S(1)}, bf16[2,64,640]{2,1,0:T(8,128)(2,1)S(1)}) custom-call(s32[6]{0:T(128)S(1)} %stack.61.flip_ref.refs_0_.scalars, bf16[2,3,64,640]{3,2,1,0:T(8,128)(2,1)S(1)} %collective-permute-done.6.refs_1_, bf16[3,3,3,64,512]{4,3,2,1,0:T(8,128)(2,1)S(1)} %copy-done, ...), custom_call_target="tpu_custom_call" | custom-call | flops 377487360 | bytes 8388608 | tf_op jit(solution)/shard_map/pallas_call | solution.py:197
  74.0 2.2 %collective-permute-start.16 = (bf16[2,64,640]{2,1,0:T(8,128)(2,1)S(1)}, bf16[2,64,640]{2,1,0:T(8,128)(2,1)S(1)}, u32[]{:S(2)}, u32[]{:S(2)}) collective-permute-start(bf16[2,64,640]{2,1,0:T(8,128)(2,1)S(1)} %get-tuple-element.31), channel_id=1, source_target_pairs={{0,1},{1,0},{2,3},{3,2},{4,5},{5,4},{6,7},{7,6},{8,9},{9,8},{10,11... | collective-permute-start | bytes 491528 | tf_op jit(solution)/shard_map/ppermute | solution.py:274
  76.1 0.1 collective-permute-start.17
  76.2 0.9 %collective-permute-done.16.refs_2_ = bf16[2,64,640]{2,1,0:T(8,128)(2,1)S(1)} collective-permute-done((bf16[2,64,640]{2,1,0:T(8,128)(2,1)S(1)}, bf16[2,64,640]{2,1,0:T(8,128)(2,1)S(1)}, u32[]{:S(2)}, u32[]{:S(2)}) %collective-permute-start.16) | collective-permute-done | bytes 163872 | tf_op jit(solution)/shard_map/ppermute | solution.py:274
  77.2 0.4 collective-permute-done.17.refs_3_
  77.5 1.6 %unpack.1 = bf16[4,4,64,320]{3,2,1,0:T(8,128)(2,1)} custom-call(s32[6]{0:T(128)S(1)} %stack.61.flip_ref.refs_0_.scalars, bf16[2,64,640]{2,1,0:T(8,128)(2,1)S(1)} %get-tuple-element.29.refs_0_, bf16[2,64,640]{2,1,0:T(8,128)(2,1)S(1)} %get-tuple-element.30.refs_1_, bf16[2,64,640]{2,1,0:T(8,128)(2,1)S(1)} %collective-permute-done.16.refs_2_, ...), custom_call_target="tpu_custom_call" | custom-call | flops 10000000 | bytes 4194304 | tf_op jit(solution)/shard_map/unpack/pallas_call | solution.py:77
  (7 shorter events, 0.3 us)
Async XLA Ops:
  0.1 1.1 %copy-start.1 = (bf16[4,4,64,320]{3,2,1,0:T(8,128)(2,1)S(1)}, bf16[4,4,64,320]{3,2,1,0:T(8,128)(2,1)}, u32[]{:S(2)}) copy-start(bf16[4,4,64,320]{3,2,1,0:T(8,128)(2,1)} %new_ref.1) | copy-start | bytes 1966084
  1.2 1.0 %copy-start.2 = (bf16[2,4,64,320]{3,2,1,0:T(8,128)(2,1)S(1)}, bf16[2,4,64,320]{3,2,1,0:T(8,128)(2,1)}, u32[]{:S(2)}) copy-start(bf16[2,4,64,320]{3,2,1,0:T(8,128)(2,1)} %cached_ref.1) | copy-start | bytes 983044
  3.8 4.8 %collective-permute-start = (bf16[2,3,64,640]{3,2,1,0:T(8,128)(2,1)S(1)}, bf16[2,3,64,640]{3,2,1,0:T(8,128)(2,1)S(1)}, u32[]{:S(2)}, u32[]{:S(2)}) collective-permute-start(bf16[2,3,64,640]{3,2,1,0:T(8,128)(2,1)S(1)} %get-tuple-element.20), channel_id=1, source_target_pairs={{0,1},{1,0},{2,3},{3,2},{4,5},{5,4},{6,7},{7,6},{8,9},{9,8},{10,11... | collective-permute-start | bytes 1474568 | tf_op jit(solution)/shard_map/ppermute | solution.py:274
  8.6 4.5 %copy-start.3 = (f32[64]{0:T(128)S(1)}, f32[64]{0:T(128)}, u32[]{:S(2)}) copy-start(f32[64]{0:T(128)} %param.7) | copy-start | bytes 772
  8.7 13.7 %collective-permute-start.2 = (bf16[2,3,64,640]{3,2,1,0:T(8,128)(2,1)S(1)}, bf16[2,3,64,640]{3,2,1,0:T(8,128)(2,1)S(1)}, u32[]{:S(2)}, u32[]{:S(2)}) collective-permute-start(bf16[2,3,64,640]{3,2,1,0:T(8,128)(2,1)S(1)} %get-tuple-element.33.refs_1_), channel_id=1, source_target_pairs={{0,2},{1,3},{2,4},{3,5},{4,6},{5,7},{6,0},{7,1},{8,10},{9,11},{10,... | collective-permute-start | bytes 1474568 | tf_op jit(solution)/shard_map/ppermute | solution.py:274
  8.8 13.6 %copy-start = (bf16[3,3,3,64,512]{4,3,2,1,0:T(8,128)(2,1)S(1)}, bf16[3,3,3,64,512]{4,3,2,1,0:T(8,128)(2,1)}, u32[]{:S(2)}) copy-start(bf16[3,3,3,64,512]{4,3,2,1,0:T(8,128)(2,1)} %refs_2_) | copy-start | bytes 5308420
  8.9 15.6 %collective-permute-start.4 = (bf16[2,3,64,640]{3,2,1,0:T(8,128)(2,1)S(1)}, bf16[2,3,64,640]{3,2,1,0:T(8,128)(2,1)S(1)}, u32[]{:S(2)}, u32[]{:S(2)}) collective-permute-start(bf16[2,3,64,640]{3,2,1,0:T(8,128)(2,1)S(1)} %get-tuple-element.34.refs_2_), channel_id=1, source_target_pairs={{2,0},{3,1},{4,2},{5,3},{6,4},{7,5},{0,6},{1,7},{10,8},{11,9},{12,... | collective-permute-start | bytes 1474568 | tf_op jit(solution)/shard_map/ppermute | solution.py:274
  11.7 20.5 %collective-permute-start.9 = (bf16[2,3,64,640]{3,2,1,0:T(8,128)(2,1)S(1)}, bf16[2,3,64,640]{3,2,1,0:T(8,128)(2,1)S(1)}, u32[]{:S(2)}, u32[]{:S(2)}) collective-permute-start(bf16[2,3,64,640]{3,2,1,0:T(8,128)(2,1)S(1)} %get-tuple-element.33.refs_1_), channel_id=1, source_target_pairs={{2,0},{3,1},{4,2},{5,3},{6,4},{7,5},{0,6},{1,7},{10,8},{11,9},{12,... | collective-permute-start | bytes 1474568 | tf_op jit(solution)/shard_map/ppermute | solution.py:274
  11.7 21.2 %collective-permute-start.10 = (bf16[2,3,64,640]{3,2,1,0:T(8,128)(2,1)S(1)}, bf16[2,3,64,640]{3,2,1,0:T(8,128)(2,1)S(1)}, u32[]{:S(2)}, u32[]{:S(2)}) collective-permute-start(bf16[2,3,64,640]{3,2,1,0:T(8,128)(2,1)S(1)} %get-tuple-element.34.refs_2_), channel_id=1, source_target_pairs={{0,2},{1,3},{2,4},{3,5},{4,6},{5,7},{6,0},{7,1},{8,10},{9,11},{10,... | collective-permute-start | bytes 1474568 | tf_op jit(solution)/shard_map/ppermute | solution.py:274
  13.1 2.3 %collective-permute-start.1 = (f32[64]{0:T(128)S(1)}, f32[64]{0:T(128)S(1)}, u32[]{:S(2)}, u32[]{:S(2)}) collective-permute-start(f32[64]{0:T(128)S(1)} %copy-done.3), channel_id=1, source_target_pairs={{0,1},{1,0},{2,3},{3,2},{4,5},{5,4},{6,7},{7,6},{8,9},{9,8},{10,11... | collective-permute-start | bytes 776 | tf_op jit(solution)/shard_map/ppermute | solution.py:274
  15.4 32.6 %collective-permute-start.15 = (bf16[2,3,64,640]{3,2,1,0:T(8,128)(2,1)S(1)}, bf16[2,3,64,640]{3,2,1,0:T(8,128)(2,1)S(1)}, u32[]{:S(2)}, u32[]{:S(2)}) collective-permute-start(bf16[2,3,64,640]{3,2,1,0:T(8,128)(2,1)S(1)} %pad_maximum_fusion.6), channel_id=1, source_target_pairs={{0,1},{1,0},{2,3},{3,2},{4,5},{5,4},{6,7},{7,6},{8,9},{9,8},{10,11... | collective-permute-start | bytes 1474568 | tf_op jit(solution)/shard_map/ppermute | solution.py:274
  22.4 27.2 %collective-permute-start.7 = (bf16[3,3,3,64,512]{4,3,2,1,0:T(8,128)(2,1)S(1)}, bf16[3,3,3,64,512]{4,3,2,1,0:T(8,128)(2,1)S(1)}, u32[]{:S(2)}, u32[]{:S(2)}) collective-permute-start(bf16[3,3,3,64,512]{4,3,2,1,0:T(8,128)(2,1)S(1)} %copy-done), channel_id=1, source_target_pairs={{0,1},{1,0},{2,3},{3,2},{4,5},{5,4},{6,7},{7,6},{8,9},{9,8},{10,11... | collective-permute-start | bytes 5308424 | tf_op jit(solution)/shard_map/ppermute | solution.py:274
  24.7 33.6 %collective-permute-start.14 = (bf16[2,3,64,640]{3,2,1,0:T(8,128)(2,1)S(1)}, bf16[2,3,64,640]{3,2,1,0:T(8,128)(2,1)S(1)}, u32[]{:S(2)}, u32[]{:S(2)}) collective-permute-start(bf16[2,3,64,640]{3,2,1,0:T(8,128)(2,1)S(1)} %pad_maximum_fusion.5), channel_id=1, source_target_pairs={{0,1},{1,0},{2,3},{3,2},{4,5},{5,4},{6,7},{7,6},{8,9},{9,8},{10,11... | collective-permute-start | bytes 1474568 | tf_op jit(solution)/shard_map/ppermute | solution.py:274
  32.1 13.5 %collective-permute-start.3 = (bf16[2,3,64,640]{3,2,1,0:T(8,128)(2,1)S(1)}, bf16[2,3,64,640]{3,2,1,0:T(8,128)(2,1)S(1)}, u32[]{:S(2)}, u32[]{:S(2)}) collective-permute-start(bf16[2,3,64,640]{3,2,1,0:T(8,128)(2,1)S(1)} %collective-permute-done.2.refs_1_), channel_id=1, source_target_pairs={{0,2},{1,3},{2,4},{3,5},{4,6},{5,7},{6,0},{7,1},{8,10},{9,11},{10,... | collective-permute-start | bytes 1474568 | tf_op jit(solution)/shard_map/ppermute | solution.py:274
  33.0 14.8 %collective-permute-start.5 = (bf16[2,3,64,640]{3,2,1,0:T(8,128)(2,1)S(1)}, bf16[2,3,64,640]{3,2,1,0:T(8,128)(2,1)S(1)}, u32[]{:S(2)}, u32[]{:S(2)}) collective-permute-start(bf16[2,3,64,640]{3,2,1,0:T(8,128)(2,1)S(1)} %collective-permute-done.4.refs_2_), channel_id=1, source_target_pairs={{2,0},{3,1},{4,2},{5,3},{6,4},{7,5},{0,6},{1,7},{10,8},{11,9},{12,... | collective-permute-start | bytes 1474568 | tf_op jit(solution)/shard_map/ppermute | solution.py:274
  45.6 16.6 %collective-permute-start.13 = (bf16[2,3,64,640]{3,2,1,0:T(8,128)(2,1)S(1)}, bf16[2,3,64,640]{3,2,1,0:T(8,128)(2,1)S(1)}, u32[]{:S(2)}, u32[]{:S(2)}) collective-permute-start(bf16[2,3,64,640]{3,2,1,0:T(8,128)(2,1)S(1)} %pad_maximum_fusion.4), channel_id=1, source_target_pairs={{0,1},{1,0},{2,3},{3,2},{4,5},{5,4},{6,7},{7,6},{8,9},{9,8},{10,11... | collective-permute-start | bytes 1474568 | tf_op jit(solution)/shard_map/ppermute | solution.py:274
  47.8 21.9 %collective-permute-start.11 = (bf16[4,3,64,640]{3,2,1,0:T(8,128)(2,1)S(1)}, bf16[4,3,64,640]{3,2,1,0:T(8,128)(2,1)S(1)}, u32[]{:S(2)}, u32[]{:S(2)}) collective-permute-start(bf16[4,3,64,640]{3,2,1,0:T(8,128)(2,1)S(1)} %pad_maximum_fusion), channel_id=1, source_target_pairs={{9,1},{1,9},{11,3},{3,11},{13,5},{5,13},{15,7},{7,15},{16,8},{8,16... | collective-permute-start | bytes 2949128 | tf_op jit(solution)/shard_map/ppermute | solution.py:274
  48.1 21.6 %collective-permute-start.8 = (bf16[2,3,64,640]{3,2,1,0:T(8,128)(2,1)S(1)}, bf16[2,3,64,640]{3,2,1,0:T(8,128)(2,1)S(1)}, u32[]{:S(2)}, u32[]{:S(2)}) collective-permute-start(bf16[2,3,64,640]{3,2,1,0:T(8,128)(2,1)S(1)} %pad_maximum_fusion.2), channel_id=1, source_target_pairs={{9,1},{1,9},{11,3},{3,11},{13,5},{5,13},{15,7},{7,15},{16,8},{8,16... | collective-permute-start | bytes 1474568 | tf_op jit(solution)/shard_map/ppermute | solution.py:274
  49.6 16.5 %collective-permute-start.12 = (bf16[2,3,64,640]{3,2,1,0:T(8,128)(2,1)S(1)}, bf16[2,3,64,640]{3,2,1,0:T(8,128)(2,1)S(1)}, u32[]{:S(2)}, u32[]{:S(2)}) collective-permute-start(bf16[2,3,64,640]{3,2,1,0:T(8,128)(2,1)S(1)} %pad_maximum_fusion.3), channel_id=1, source_target_pairs={{0,1},{1,0},{2,3},{3,2},{4,5},{5,4},{6,7},{7,6},{8,9},{9,8},{10,11... | collective-permute-start | bytes 1474568 | tf_op jit(solution)/shard_map/ppermute | solution.py:274
  58.3 14.2 %collective-permute-start.6 = (bf16[2,3,64,640]{3,2,1,0:T(8,128)(2,1)S(1)}, bf16[2,3,64,640]{3,2,1,0:T(8,128)(2,1)S(1)}, u32[]{:S(2)}, u32[]{:S(2)}) collective-permute-start(bf16[2,3,64,640]{3,2,1,0:T(8,128)(2,1)S(1)} %pad_maximum_fusion.1), channel_id=1, source_target_pairs={{9,1},{1,9},{11,3},{3,11},{13,5},{5,13},{15,7},{7,15},{16,8},{8,16... | collective-permute-start | bytes 1474568 | tf_op jit(solution)/shard_map/ppermute | solution.py:274
  74.0 3.2 %collective-permute-start.16 = (bf16[2,64,640]{2,1,0:T(8,128)(2,1)S(1)}, bf16[2,64,640]{2,1,0:T(8,128)(2,1)S(1)}, u32[]{:S(2)}, u32[]{:S(2)}) collective-permute-start(bf16[2,64,640]{2,1,0:T(8,128)(2,1)S(1)} %get-tuple-element.31), channel_id=1, source_target_pairs={{0,1},{1,0},{2,3},{3,2},{4,5},{5,4},{6,7},{7,6},{8,9},{9,8},{10,11... | collective-permute-start | bytes 491528 | tf_op jit(solution)/shard_map/ppermute | solution.py:274
  76.1 1.4 %collective-permute-start.17 = (bf16[2,64,640]{2,1,0:T(8,128)(2,1)S(1)}, bf16[2,64,640]{2,1,0:T(8,128)(2,1)S(1)}, u32[]{:S(2)}, u32[]{:S(2)}) collective-permute-start(bf16[2,64,640]{2,1,0:T(8,128)(2,1)S(1)} %get-tuple-element.32), channel_id=1, source_target_pairs={{0,1},{1,0},{2,3},{3,2},{4,5},{5,4},{6,7},{7,6},{8,9},{9,8},{10,11... | collective-permute-start | bytes 491528 | tf_op jit(solution)/shard_map/ppermute | solution.py:274
